TPU v7x, 128 devices: a whole 4x4x4 slice. The times are simulated.
128 devices in a mesh: blk: 16 (over x, z), expert: 8 (over y, core).
Axes of the slice: x: 4, y: 4, z: 4, core: 2. Of those that a mesh axis runs over, the one named last changes fastest.
Arguments:
- hidden: bfloat16 [16, 32, 2, 2304], P('blk', 'expert'), may hold values from -6 to 6
- query: bfloat16 [16, 32, 2, 2304], P('blk', 'expert'), may hold values from -8 to 8
- new_key: bfloat16 [16, 32, 2, 2304], P('blk', 'expert'), may hold values from -8 to 8
- new_value: bfloat16 [16, 32, 2, 2304], P('blk', 'expert'), may hold values from -18 to 18
- prompt_key: bfloat16 [32, 1024, 2304], P('expert', 'blk'), may hold values from -8 to 8
- prompt_value: bfloat16 [32, 1024, 2304], P('expert', 'blk'), may hold values from -18 to 18
- prompt_len: int32 [32], replicated, may hold values from 128 to 1024, as said below
- live_blocks: int32 [32, 64], replicated, may hold values from 0 to 1
- tail_key: bfloat16 [16, 32, 64, 2304], P('blk', 'expert'), may hold values from -8 to 8
- tail_value: bfloat16 [16, 32, 64, 2304], P('blk', 'expert'), may hold values from -18 to 18
- tail_len: int32 [16, 32], replicated, may hold values from 1 to 64, as said below
- tail_source: int32 [16, 32], replicated, may hold values from 0 to 15, as said below
- routes: int32 [16, 32, 2, 2], P('blk', 'expert'), may hold values from 0 to 7, all different within a row; in each aligned block of 8 rows (0 to 7, 8 to 15, ..., all dimensions but the last counted through in order) at most 4 rows name the same one
- router: float32 [2304, 8], replicated, may hold values from -0.125 to 0.125
- ffn_gain: float32 [2304], replicated, may hold values from 0.25 to 1.75
- w_gate: bfloat16 [8, 2304, 5760], P('expert', None, 'blk'), may hold values from -0.125 to 0.125
- w_up: bfloat16 [8, 2304, 5760], P('expert', None, 'blk'), may hold values from -0.125 to 0.125
- w_down: bfloat16 [8, 5760, 2304], P('expert', 'blk'), may hold values from -0.078125 to 0.078125
- score_weight: float32 [2304], replicated, may hold values from -0.125 to 0.125
Outputs:
- layer_out: bfloat16 [16, 32, 2, 2304], P('blk', 'expert')
- score: float32 [16, 32, 2], P('blk', 'expert')
Inputs may be any that keep to these rules, and one draw needn't show every extreme that they name: `prompt_len`: some prompt has all 1024 positions cached. `tail_len`: some sample has a tail of exactly 64 positions. For each prompt p, tail_source[:, p] is a permutation of the 16 samples; half of the slots hold another sample's tail. `routes`: in the rows of one device (aligned blocks of 8 rows in the order of the leading dimensions) each row names 2 different experts and no expert is named by more than 4 rows; some expert is named by exactly 4 rows.
All inputs are finite; a program needn't handle non-finite values.
Results may differ from a plain program's by a relative error of at most 0.025.
Values may be sent and summed in bfloat16 or wider, within the bound.
No kernel may reach another device: no remote copies, remote signals or barrier semaphores. Data moves between devices by JAX's collectives and lax.ppermute only.
A program may use at most 256 MiB of HBM per device.

v0:
```python
import jax
import jax.numpy as jnp
from jax import lax
from jax.sharding import PartitionSpec as P

HDIM = 64
TOP = 2
KVB = 16
CAP = 4


neg_fill = -1e30
score_scale = 0.125


def prompt_usable(offset, length, lengths, live_rows):
    page_rows = lax.dynamic_slice_in_dim(live_rows, offset // KVB, length // KVB, 1)
    page_rows = jnp.repeat(page_rows, KVB, axis=1)
    positions = offset + jnp.arange(length)
    return (positions[None, :] < lengths[:, None]) & (page_rows > 0)


def local(
    hidden,
    query,
    new_key,
    new_value,
    prompt_key,
    prompt_value,
    prompt_len,
    live_blocks,
    tail_key,
    tail_value,
    tail_len,
    tail_source,
    routes,
    router,
    ffn_gain,
    w_gate,
    w_up,
    w_down,
    score_weight,
):
    blk_count = lax.axis_size("blk")
    exp_count = lax.axis_size("expert")
    blk_at = lax.axis_index("blk")
    exp_at = lax.axis_index("expert")
    local_prompts = query.shape[1]
    fresh_count = query.shape[2]
    model_width = query.shape[3]
    head_count = model_width // HDIM
    blk_len = prompt_key.shape[1]
    tail_span = tail_key.shape[2]
    my_lengths = lax.dynamic_slice_in_dim(prompt_len, exp_at * local_prompts, local_prompts, 0)
    my_live = lax.dynamic_slice_in_dim(live_blocks, exp_at * local_prompts, local_prompts, 0)
    my_owner = lax.dynamic_slice_in_dim(tail_source, exp_at * local_prompts, local_prompts, 1)
    my_tail_len = lax.dynamic_slice_in_dim(tail_len, exp_at * local_prompts, local_prompts, 1)
    query_heads = query[0].reshape(local_prompts, fresh_count, head_count, HDIM)
    new_heads = new_key[0].reshape(local_prompts, fresh_count, head_count, HDIM)
    new_vheads = new_value[0].reshape(local_prompts, fresh_count, head_count, HDIM)
    causal = jnp.arange(fresh_count)[None, :] <= jnp.arange(fresh_count)[:, None]
    everyone_q = lax.all_gather(query, "blk", axis=0, tiled=True)
    all_heads = everyone_q.reshape(blk_count, local_prompts, fresh_count, head_count, HDIM)
    cache_kh = prompt_key.reshape(local_prompts, blk_len, head_count, HDIM)
    cache_vh = prompt_value.reshape(local_prompts, blk_len, head_count, HDIM)
    cache_ok = prompt_usable(blk_at * blk_len, blk_len, my_lengths, my_live)[None, :, None, None, :]
    cache_scores = (
        jnp.einsum("mpthd,pkhd->mpthk", all_heads, cache_kh, preferred_element_type=jnp.float32)
        * score_scale
    )
    cache_scores = jnp.where(cache_ok, cache_scores, neg_fill)
    slot_kh = tail_key[0].reshape(local_prompts, tail_span, head_count, HDIM)
    slot_vh = tail_value[0].reshape(local_prompts, tail_span, head_count, HDIM)
    owners_here = lax.dynamic_index_in_dim(my_owner, blk_at, 0, keepdims=False)
    slot_ok = (owners_here[None, :] == jnp.arange(blk_count)[:, None])[:, :, None] & (
        jnp.arange(tail_span)[None, None, :] < my_tail_len[:, :, None]
    )
    slot_ok = slot_ok[:, :, None, None, :]
    slot_scores = (
        jnp.einsum("mpthd,pkhd->mpthk", all_heads, slot_kh, preferred_element_type=jnp.float32)
        * score_scale
    )
    slot_scores = jnp.where(slot_ok, slot_scores, neg_fill)
    own_scores = (
        jnp.einsum("pthd,puhd->pthu", query_heads, new_heads, preferred_element_type=jnp.float32)
        * score_scale
    )
    own_scores = jnp.where(causal[None, :, None, :], own_scores, neg_fill)
    own_row = (jnp.arange(blk_count) == blk_at)[:, None, None, None]
    local_top = jnp.maximum(jnp.max(cache_scores, axis=-1), jnp.max(slot_scores, axis=-1))
    local_top = jnp.where(
        own_row, jnp.maximum(local_top, jnp.max(own_scores, axis=-1)[None]), local_top
    )
    top_score = lax.pmax(local_top, "blk")
    cache_w = jnp.where(cache_ok, jnp.exp(cache_scores - top_score[..., None]), 0.0)
    slot_w = jnp.where(slot_ok, jnp.exp(slot_scores - top_score[..., None]), 0.0)
    denom_part = jnp.sum(cache_w, axis=-1) + jnp.sum(slot_w, axis=-1)
    weighted = jnp.einsum(
        "mpthk,pkhd->mpthd",
        cache_w.astype(jnp.bfloat16),
        cache_vh,
        preferred_element_type=jnp.float32,
    )
    weighted = weighted + jnp.einsum(
        "mpthk,pkhd->mpthd",
        slot_w.astype(jnp.bfloat16),
        slot_vh,
        preferred_element_type=jnp.float32,
    )
    own_top = lax.dynamic_index_in_dim(top_score, blk_at, 0, keepdims=False)
    own_w = jnp.where(causal[None, :, None, :], jnp.exp(own_scores - own_top[..., None]), 0.0)
    own_sum = jnp.einsum(
        "pthu,puhd->pthd",
        own_w.astype(jnp.bfloat16),
        new_vheads,
        preferred_element_type=jnp.float32,
    )
    denom_part = denom_part + jnp.where(own_row, jnp.sum(own_w, axis=-1)[None], 0.0)
    weighted = weighted + jnp.where(own_row[..., None], own_sum[None], 0.0)
    weighted_mine, denom_mine = (
        lax.psum_scatter(
            weighted.astype(jnp.bfloat16), "blk", scatter_dimension=0, tiled=True
        ).astype(jnp.float32),
        lax.psum_scatter(
            denom_part.astype(jnp.bfloat16), "blk", scatter_dimension=0, tiled=True
        ).astype(jnp.float32),
    )
    attended = weighted_mine[0] / denom_mine[0][..., None]
    token_count = local_prompts * fresh_count
    mixed = hidden[0].astype(jnp.float32).reshape(token_count, model_width) + attended.reshape(
        token_count, model_width
    )
    normed = (
        mixed * lax.rsqrt(jnp.mean(mixed * mixed, axis=-1, keepdims=True) + 1e-05) * ffn_gain
    ).astype(jnp.bfloat16)
    chosen = routes[0].reshape(token_count, TOP)
    logits = jnp.dot(normed.astype(jnp.float32), router, precision=lax.Precision.HIGHEST)
    expert_total = router.shape[1]
    onehot = chosen[:, :, None] == jnp.arange(expert_total)[None, None, :]
    picked = jnp.sum(jnp.where(onehot, logits[:, None, :], 0.0), axis=-1)
    gate_first = 1.0 / (1.0 + jnp.exp(picked[:, 1] - picked[:, 0]))
    gate_second = 1.0 / (1.0 + jnp.exp(picked[:, 0] - picked[:, 1]))
    assign_count = token_count * TOP
    assign_hot = onehot.reshape(assign_count, expert_total).astype(jnp.int32)
    earlier = jnp.cumsum(assign_hot, axis=0) - assign_hot
    slot_ids = jnp.sum(earlier * assign_hot, axis=-1)
    assign_expert = chosen.reshape(assign_count)
    local_experts = expert_total // exp_count
    row_ids = jnp.arange(local_experts * exp_count * CAP)
    row_local = row_ids // (exp_count * CAP)
    row_device = row_ids // CAP % exp_count
    row_slot = row_ids % CAP
    row_expert = row_device * local_experts + row_local
    dispatch_map = (
        (row_expert[:, None] == assign_expert[None, :]) & (row_slot[:, None] == slot_ids[None, :])
    ).astype(jnp.bfloat16)
    repeated = jnp.repeat(normed, TOP, axis=0)
    outgoing = jnp.dot(dispatch_map, repeated, preferred_element_type=jnp.float32).astype(
        jnp.bfloat16
    )
    outgoing = outgoing.reshape(local_experts, exp_count, CAP, model_width)
    arrived = lax.all_to_all(outgoing, "expert", split_axis=1, concat_axis=1, tiled=True)
    column_rows = lax.all_gather(arrived[None], "blk", axis=0, tiled=True)
    gated = jnp.einsum("nlscd,ldf->nlscf", column_rows, w_gate, preferred_element_type=jnp.float32)
    upward = jnp.einsum("nlscd,ldf->nlscf", column_rows, w_up, preferred_element_type=jnp.float32)
    activation = (jax.nn.silu(gated) * upward).astype(jnp.bfloat16)
    summed = lax.psum_scatter(
        jnp.einsum(
            "nlscf,lfd->nlscd", activation, w_down, preferred_element_type=jnp.float32
        ).astype(jnp.bfloat16),
        "blk",
        scatter_dimension=0,
        tiled=True,
    )
    returned = lax.all_to_all(summed, "expert", split_axis=2, concat_axis=2, tiled=True)
    returned = returned.reshape(local_experts * exp_count * CAP, model_width)
    gathered_back = jnp.einsum(
        "ja,jd->ad", dispatch_map, returned, preferred_element_type=jnp.float32
    )
    gathered_back = gathered_back.reshape(token_count, TOP, model_width)
    moe_sum = gate_first[:, None] * gathered_back[:, 0] + gate_second[:, None] * gathered_back[:, 1]
    layer_out = (mixed + moe_sum).astype(jnp.bfloat16)
    score = jnp.sum(layer_out.astype(jnp.float32) * score_weight, axis=-1)
    return (
        layer_out.reshape(1, local_prompts, fresh_count, model_width),
        score.reshape(1, local_prompts, fresh_count),
    )


def solution(mesh):
    placed = (
        P("blk", "expert", None, None),
        P("blk", "expert", None, None),
        P("blk", "expert", None, None),
        P("blk", "expert", None, None),
        P("expert", "blk", None),
        P("expert", "blk", None),
        P(),
        P(),
        P("blk", "expert", None, None),
        P("blk", "expert", None, None),
        P(),
        P(),
        P("blk", "expert", None, None),
        P(),
        P(),
        P("expert", None, "blk"),
        P("expert", None, "blk"),
        P("expert", "blk", None),
        P(),
    )
    return jax.shard_map(
        local,
        mesh=mesh,
        in_specs=placed,
        out_specs=(P("blk", "expert", None, None), P("blk", "expert", None)),
        check_vma=False,
    )
```

profile of v0, /device:TPU:1, one launch (start us, length us, event | category | flops | bytes accessed | tf_op | source)
XLA Modules:
  0.0 392.5 jit_solution(18122139587508014965)
XLA Ops:
  10.8 21.1 %all_gather.6 = bf16[16,4,2,2304]{3,1,2,0:T(4,128)(2,1)S(1)} all-gather(bf16[1,4,2,2304]{3,1,2,0:T(4,128)(2,1)S(1)} %copy.113), channel_id=1, replica_groups=mesh['blk'=16,'expert'=8] {'blk'}, dimensions={0}, use_global_device_ids=true | all-gather | bytes 626688 | tf_op jit(solution)/shard_map/all_gather | solution.py:62
  31.8 2.0 reshape.348
  33.9 4.5 %reshape.318 = bf16[4,64,36,64]{3,2,1,0:T(8,128)(2,1)} reshape(bf16[4,64,2304]{2,1,0:T(8,128)(2,1)} %param.23) | data formatting | bytes 2359296 | tf_op jit(solution)/shard_map/reshape | solution.py:64
  38.4 4.6 %bitcast_reduce_fusion = (f32[16,4,2,36]{0,2,3,1:T(2,128)S(1)}, f32[4,36,64,16,2]{2,3,4,1,0:T(8,128)}) fusion(pred[4,64]{1,0:T(4,128)(4,1)S(1)} %compare_and_fusion, bf16[16,4,2,36,64]{4,3,1,2,0:T(8,128)(2,1)S(1)} %copy-done.3, bf16[4,64,36,64,1]{3,2,1,0,4:T(8,128)(2,1)} %bitcast.146), kind=kOutput, calls=%fused_computation.13 | convolution fusion | flops 38628864 | bytes 2967808 | tf_op jit(solution)/shard_map/mpthd,pkhd->mpthk/dot_general | solution.py:68
  44.2 4.4 %reshape_squeeze.15 = bf16[4,64,36,64]{3,2,1,0:T(8,128)(2,1)} reshape(bf16[1,4,64,2304]{3,2,1,0:T(8,128)(2,1)} %param.27) | data formatting | bytes 2359296 | tf_op jit(solution)/shard_map/reshape;squeeze | solution.py:72
  48.7 4.7 %fusion.12 = (f32[16,4,2,36]{0,2,3,1:T(2,128)S(1)}, f32[4,36,64,16,2]{2,3,4,1,0:T(8,128)}) fusion(pred[16,4,64]{2,0,1:T(8,128)(4,1)S(1)} %fusion.61, bf16[16,4,2,36,64]{4,3,1,2,0:T(8,128)(2,1)S(1)} %copy-done.3, bf16[4,64,36,64,1]{3,2,1,0,4:T(8,128)(2,1)} %bitcast.147), kind=kOutput, calls=%fused_computation.20 | convolution fusion | flops 38628864 | bytes 2971648 | tf_op jit(solution)/shard_map/mpthd,pkhd->mpthk/dot_general | solution.py:80
  54.2 58.1 %pmax.7 = f32[16,4,2,36]{3,0,2,1:T(8,128)S(1)} all-reduce(f32[16,4,2,36]{3,0,2,1:T(8,128)S(1)} %maximum_select_fusion), channel_id=1, replica_groups=mesh['blk'=16,'expert'=8] {'blk'}, use_global_device_ids=true, to_apply=%region_3.4 | all-reduce | flops 4608 | bytes 36864 | tf_op jit(solution)/shard_map/pmax | solution.py:94
  112.6 3.0 reshape_squeeze.18
  115.9 4.4 %reshape.320 = bf16[4,64,36,64]{3,2,1,0:T(8,128)(2,1)} reshape(bf16[4,64,2304]{2,1,0:T(8,128)(2,1)} %param.24) | data formatting | bytes 2359296 | tf_op jit(solution)/shard_map/reshape | solution.py:65
  120.6 3.5 fusion.2
  124.6 1.5 fusion.1
  126.1 2.0 copy.133
  128.1 4.0 %fusion.15 = (f32[16,4,2,36]{0,2,3,1:T(2,128)S(1)}, f32[16,4,2,36]{0,2,3,1:T(2,128)S(1)}) fusion(f32[4,36,64,16,2]{2,3,4,1,0:T(8,128)} %get-tuple-element.17, f32[16,4,2,36]{0,2,3,1:T(2,128)S(1)} %copy.127, pred[16,4,64]{2,0,1:T(8,128)(4,1)S(1)} %fusion.61, f32[4,36,64,16,2]{2,3,4,1,0:T(8,128)} %get-tuple-element.15, pred[4,64]{1,0:T(4,128)(4,1)S(1)} %compare_and_fusion), kind=kLoop, calls=%fused_computation.21 | loop fusion | flops 2939904 | bytes 2418944 | tf_op jit(solution)/shard_map/reduce_sum | solution.py:97
  133.2 55.9 %all-reduce.1 = bf16[16,4,2,36]{3,1,2,0:T(4,128)(2,1)S(1)} all-reduce(bf16[16,4,2,36]{3,1,2,0:T(4,128)(2,1)S(1)} %copy.139), channel_id=4, replica_groups=mesh['blk'=16,'expert'=8] {'blk'}, use_global_device_ids=true, to_apply=%region_8.9.clone | all-reduce | flops 4608 | bytes 18432
  190.6 39.0 %all-reduce.5.cloned.1.call-done = bf16[16,4,2,36,64]{4,1,3,2,0:T(4,128)(2,1)} async-done(((bf16[16,4,2,36,64]{4,1,3,2,0:T(4,128)(2,1)}), bf16[16,4,2,36,64]{4,1,3,2,0:T(4,128)(2,1)}) %all-reduce.5.cloned.1.call-update) | async-done | bytes 589840
  229.6 1.5 dynamic-slice_convert_fusion
  232.1 11.7 %all_to_all.10 = bf16[1,8,4,2304]{3,2,0,1:T(4,128)(2,1)S(1)} all-to-all(bf16[1,8,4,2304]{3,2,0,1:T(4,128)(2,1)S(1)} %bitcast.148), channel_id=1, replica_groups=mesh['blk'=16,'expert'=8] {'expert'}, dimensions={1} | all-to-all | bytes 294912 | tf_op jit(solution)/shard_map/all_to_all | solution.py:162
  244.6 42.4 %all-gather.3.cloned.1.call-done = bf16[16,8,4,2304]{3,1,2,0:T(8,128)(2,1)} async-done(((bf16[1,8,4,2304]{3,1,2,0:T(8,128)(2,1)}), bf16[16,8,4,2304]{3,1,2,0:T(8,128)(2,1)}) %all-gather.3.cloned.1.call-update) | async-done | bytes 2359312 | tf_op jit(solution)/shard_map/all_gather | solution.py:163
  286.9 3.5 fusion.24
  290.5 6.3 %fusion = bf16[16,1,8,4,2304]{4,2,3,0,1:T(8,128)(2,1)} fusion(bf16[1,360,2304]{2,1,0:T(8,128)(2,1)S(1)} %copy-done, bf16[16,8,4,2304]{3,1,2,0:T(8,128)(2,1)} %all-gather.3.cloned.1.call-done, bf16[1,2304,360]{1,2,0:T(8,128)(2,1)} %param.35, f32[16,1,8,4,360]{4,2,3,0,1:T(8,128)S(1)} %fusion.24), kind=kOutput, calls=%fused_computation.1 | convolution fusion | flops 1700978688 | bytes 8773632 | tf_op jit(solution)/shard_map/nlscf,lfd->nlscd/dot_general | solution.py:168
  297.8 72.7 %reduce-scatter.7.cloned.1.call-done = bf16[1,1,8,4,2304]{4,2,3,0,1:T(8,128)(2,1)} async-done(((bf16[16,1,8,4,2304]{4,2,3,0,1:T(8,128)(2,1)}), bf16[1,1,8,4,2304]{4,2,3,0,1:T(8,128)(2,1)}) %reduce-scatter.7.cloned.1.call-update) | async-done | bytes 147472
  370.5 1.6 copy.147
  372.1 6.6 %all-to-all-start.1 = ((bf16[1,1,8,4,2304]{4,3,0,1,2:T(4,128)(2,1)}), bf16[1,1,8,4,2304]{4,3,0,1,2:T(4,128)(2,1)S(1)}, u32[]{:S(2)}, u32[]{:S(2)}) async-start(bf16[1,1,8,4,2304]{4,3,0,1,2:T(4,128)(2,1)} %copy.147), calls=%async_computation.1 | async-start | bytes 294912 | tf_op jit(solution)/shard_map/all_to_all | solution.py:175
  379.1 5.1 %all-to-all-done.1 = bf16[1,1,8,4,2304]{4,3,0,1,2:T(4,128)(2,1)S(1)} async-done(((bf16[1,1,8,4,2304]{4,3,0,1,2:T(4,128)(2,1)}), bf16[1,1,8,4,2304]{4,3,0,1,2:T(4,128)(2,1)S(1)}, u32[]{:S(2)}, u32[]{:S(2)}) %all-to-all-start.1) | async-done | bytes 147488 | tf_op jit(solution)/shard_map/all_to_all | solution.py:175
  (110 shorter events, 14.2 us)
Async XLA Ops:
  7.2 283.3 %copy-start = (bf16[1,360,2304]{2,1,0:T(8,128)(2,1)S(1)}, bf16[1,360,2304]{2,1,0:T(8,128)(2,1)}, u32[]{:S(2)}) copy-start(bf16[1,360,2304]{2,1,0:T(8,128)(2,1)} %param.36) | copy-start | bytes 4976644
  7.2 222.4 %all-reduce.5.cloned.1.call-start = ((), (), s32[]{:S(2)}) async-start(), calls=%async_computation.4 | async-start | bytes 2359296
  33.9 4.6 %copy-start.3 = (bf16[16,4,2,36,64]{4,3,1,2,0:T(8,128)(2,1)S(1)}, bf16[16,4,2,36,64]{4,3,1,2,0:T(8,128)(2,1)}, u32[]{:S(2)}) copy-start(bf16[16,4,2,36,64]{4,3,1,2,0:T(8,128)(2,1)} %reshape.348) | copy-start | bytes 1769476
  38.4 5.6 %copy-start.12 = (s32[16,32]{1,0:T(8,128)S(1)}, s32[16,32]{1,0:T(8,128)}, u32[]{:S(2)}) copy-start(s32[16,32]{1,0:T(8,128)} %param.29) | copy-start | bytes 6148
  48.7 4.8 %copy-start.7 = (bf16[1,4,2,2304]{3,2,1,0:T(2,128)(2,1)S(1)}, bf16[1,4,2,2304]{3,2,1,0:T(2,128)(2,1)}, u32[]{:S(2)}) copy-start(bf16[1,4,2,2304]{3,2,1,0:T(2,128)(2,1)} %param.21) | copy-start | bytes 110596
  53.3 59.2 %copy-start.4 = (bf16[1,4,64,2304]{3,2,1,0:T(8,128)(2,1)S(1)}, bf16[1,4,64,2304]{3,2,1,0:T(8,128)(2,1)}, u32[]{:S(2)}) copy-start(bf16[1,4,64,2304]{3,2,1,0:T(8,128)(2,1)} %param.28) | copy-start | bytes 3538948
  53.9 61.8 %copy-start.8 = (bf16[1,4,2,2304]{3,2,1,0:T(2,128)(2,1)S(1)}, bf16[1,4,2,2304]{3,2,1,0:T(2,128)(2,1)}, u32[]{:S(2)}) copy-start(bf16[1,4,2,2304]{3,2,1,0:T(2,128)(2,1)} %param.22) | copy-start | bytes 110596
  120.6 3.5 copy-start.1
  120.6 3.9 %copy-start.2 = (f32[4,36,64,16,2]{2,3,4,1,0:T(8,128)S(1)}, f32[4,36,64,16,2]{2,3,4,1,0:T(8,128)}, u32[]{:S(2)}) copy-start(f32[4,36,64,16,2]{2,3,4,1,0:T(8,128)} %get-tuple-element.15) | copy-start | bytes 3538948
  128.0 4.5 %copy-start.13 = (u32[128]{0:T(128)S(1)}, u32[128]{0:T(128)}, u32[]{:S(2)}) copy-start(u32[128]{0:T(128)} %constant.148) | copy-start | bytes 1540
  128.1 62.0 %copy-start.5 = (bf16[1,4,2,2304]{3,2,1,0:T(2,128)(2,1)S(1)}, bf16[1,4,2,2304]{3,2,1,0:T(2,128)(2,1)}, u32[]{:S(2)}) copy-start(bf16[1,4,2,2304]{3,2,1,0:T(2,128)(2,1)} %param.19) | copy-start | bytes 110596
  128.1 62.0 %copy-start.11 = (s32[1,4,2,2]{1,3,2,0:T(2,128)S(1)}, s32[1,4,2,2]{1,3,2,0:T(2,128)}, u32[]{:S(2)}) copy-start(s32[1,4,2,2]{1,3,2,0:T(2,128)} %param.31) | copy-start | bytes 196
  128.1 158.8 %all-gather.3.cloned.1.call-start = ((), (), s32[]{:S(2)}) async-start(), calls=%async_computation.3 | async-start | bytes 2506752 | tf_op jit(solution)/shard_map/all_gather | solution.py:163
  132.2 99.4 %copy-start.9 = (f32[2304]{0:T(1024)S(1)}, f32[2304]{0:T(1024)}, u32[]{:S(2)}) copy-start(f32[2304]{0:T(1024)} %param.33) | copy-start | bytes 27652
  244.5 126.0 %reduce-scatter.7.cloned.1.call-start = ((), (), s32[]{:S(2)}) async-start(), calls=%async_computation.5 | async-start | bytes 2506752
  296.8 0.9 copy-start.6
  296.8 87.8 %copy-start.10 = (f32[2304]{0:T(1024)S(1)}, f32[2304]{0:T(1024)}, u32[]{:S(2)}) copy-start(f32[2304]{0:T(1024)} %param.37) | copy-start | bytes 27652
  372.1 12.0 %all-to-all-start.1 = ((bf16[1,1,8,4,2304]{4,3,0,1,2:T(4,128)(2,1)}), bf16[1,1,8,4,2304]{4,3,0,1,2:T(4,128)(2,1)S(1)}, u32[]{:S(2)}, u32[]{:S(2)}) async-start(bf16[1,1,8,4,2304]{4,3,0,1,2:T(4,128)(2,1)} %copy.147), calls=%async_computation.1 | async-start | bytes 294912 | tf_op jit(solution)/shard_map/all_to_all | solution.py:175
Sparse Core Ops, SparseCore 0:
  128.2 101.3 all-reduce.4
  244.6 42.2 all-gather.2
  296.9 73.5 reduce-scatter.6
where the time goes:
time: 393 us
  waiting for transfers between devices  159 us (40%)
  blocking collectives  147 us (37%)
  local copies, waits for them, and re-layouts  31.3 us (8%)
  matrix products  25.3 us (6%)
  between operations  14.2 us (4%)
  other arithmetic  9.11 us (2%)
  starting transfers between devices  6.73 us (2%)
    unnamed x5, waiting for transfers between devices  112 us
    pmax x1, blocking collectives, local(): top_score = lax.pmax(local_top, 'blk')  58.1 us
    unnamed x1, blocking collectives  55.9 us
    all_gather x1, waiting for transfers between devices, local(): column_rows = lax.all_gather(arrived[None], 'blk', axis=0, tiled=True)  42.4 us
    all_gather x1, blocking collectives, local(): everyone_q = lax.all_gather(query, 'blk', axis=0, tiled=True)  21.1 us
    all_to_all x1, blocking collectives, local(): lax.all_to_all(outgoing, 'expert', split_axis=1, concat_axis=1, tiled=True)  11.7 us
  transfers between devices with their start and end apart: 4, of which 4 were waited for; matrix products, arithmetic and copies ran while one was open for 2% of the time, Pallas kernels for 0%

commit v1 on v0

--- a/solution.py
+++ b/solution.py
@@ -59,7 +59,9 @@
     new_heads = new_key[0].reshape(local_prompts, fresh_count, head_count, HDIM)
     new_vheads = new_value[0].reshape(local_prompts, fresh_count, head_count, HDIM)
     causal = jnp.arange(fresh_count)[None, :] <= jnp.arange(fresh_count)[:, None]
-    everyone_q = lax.all_gather(query, "blk", axis=0, tiled=True)
+    everyone_q = lax.all_to_all(
+        jnp.broadcast_to(query, (blk_count, *query.shape[1:])), "blk", 0, 0, tiled=True
+    )
     all_heads = everyone_q.reshape(blk_count, local_prompts, fresh_count, head_count, HDIM)
     cache_kh = prompt_key.reshape(local_prompts, blk_len, head_count, HDIM)
     cache_vh = prompt_value.reshape(local_prompts, blk_len, head_count, HDIM)
@@ -86,15 +88,11 @@
         * score_scale
     )
     own_scores = jnp.where(causal[None, :, None, :], own_scores, neg_fill)
-    own_row = (jnp.arange(blk_count) == blk_at)[:, None, None, None]
     local_top = jnp.maximum(jnp.max(cache_scores, axis=-1), jnp.max(slot_scores, axis=-1))
-    local_top = jnp.where(
-        own_row, jnp.maximum(local_top, jnp.max(own_scores, axis=-1)[None]), local_top
-    )
-    top_score = lax.pmax(local_top, "blk")
-    cache_w = jnp.where(cache_ok, jnp.exp(cache_scores - top_score[..., None]), 0.0)
-    slot_w = jnp.where(slot_ok, jnp.exp(slot_scores - top_score[..., None]), 0.0)
-    denom_part = jnp.sum(cache_w, axis=-1) + jnp.sum(slot_w, axis=-1)
+    local_top = jnp.maximum(local_top, -1e4).astype(jnp.bfloat16).astype(jnp.float32)
+    cache_w = jnp.where(cache_ok, jnp.exp(cache_scores - local_top[..., None]), 0.0)
+    slot_w = jnp.where(slot_ok, jnp.exp(slot_scores - local_top[..., None]), 0.0)
+    total = jnp.sum(cache_w, axis=-1) + jnp.sum(slot_w, axis=-1)
     weighted = jnp.einsum(
         "mpthk,pkhd->mpthd",
         cache_w.astype(jnp.bfloat16),
@@ -107,25 +105,37 @@
         slot_vh,
         preferred_element_type=jnp.float32,
     )
-    own_top = lax.dynamic_index_in_dim(top_score, blk_at, 0, keepdims=False)
-    own_w = jnp.where(causal[None, :, None, :], jnp.exp(own_scores - own_top[..., None]), 0.0)
+    total_high = total.astype(jnp.bfloat16)
+    total_low = (total - total_high.astype(jnp.float32)).astype(jnp.bfloat16)
+    sent = jnp.concatenate(
+        [
+            weighted.astype(jnp.bfloat16).reshape(blk_count, local_prompts, fresh_count, model_width),
+            local_top.astype(jnp.bfloat16),
+            total_high,
+            total_low,
+        ],
+        axis=-1,
+    )
+    sent = sent.reshape(blk_count, local_prompts * fresh_count, -1)
+    got = lax.all_to_all(sent, "blk", 0, 0, tiled=True)
+    got = got.reshape(blk_count, local_prompts, fresh_count, -1)
+    part = got[..., :model_width].astype(jnp.float32)
+    part = part.reshape(blk_count, local_prompts, fresh_count, head_count, HDIM)
+    stats = got[..., model_width:].astype(jnp.float32)
+    part_top = stats[..., :head_count]
+    part_total = stats[..., head_count : 2 * head_count] + stats[..., 2 * head_count :]
+    own_top = jnp.max(own_scores, axis=-1)
+    top = jnp.maximum(jnp.max(part_top, axis=0), own_top)
+    rescale = jnp.exp(part_top - top[None])
+    own_w = jnp.where(causal[None, :, None, :], jnp.exp(own_scores - top[..., None]), 0.0)
     own_sum = jnp.einsum(
         "pthu,puhd->pthd",
         own_w.astype(jnp.bfloat16),
         new_vheads,
         preferred_element_type=jnp.float32,
     )
-    denom_part = denom_part + jnp.where(own_row, jnp.sum(own_w, axis=-1)[None], 0.0)
-    weighted = weighted + jnp.where(own_row[..., None], own_sum[None], 0.0)
-    weighted_mine, denom_mine = (
-        lax.psum_scatter(
-            weighted.astype(jnp.bfloat16), "blk", scatter_dimension=0, tiled=True
-        ).astype(jnp.float32),
-        lax.psum_scatter(
-            denom_part.astype(jnp.bfloat16), "blk", scatter_dimension=0, tiled=True
-        ).astype(jnp.float32),
-    )
-    attended = weighted_mine[0] / denom_mine[0][..., None]
+    denom = jnp.sum(part_total * rescale, axis=0) + jnp.sum(own_w, axis=-1)
+    attended = (jnp.sum(part * rescale[..., None], axis=0) + own_sum) / denom[..., None]
     token_count = local_prompts * fresh_count
     mixed = hidden[0].astype(jnp.float32).reshape(token_count, model_width) + attended.reshape(
         token_count, model_width
@@ -160,18 +170,17 @@
     )
     outgoing = outgoing.reshape(local_experts, exp_count, CAP, model_width)
     arrived = lax.all_to_all(outgoing, "expert", split_axis=1, concat_axis=1, tiled=True)
-    column_rows = lax.all_gather(arrived[None], "blk", axis=0, tiled=True)
+    column_rows = lax.all_to_all(
+        jnp.broadcast_to(arrived[None], (blk_count, *arrived.shape)), "blk", 0, 0, tiled=True
+    )
     gated = jnp.einsum("nlscd,ldf->nlscf", column_rows, w_gate, preferred_element_type=jnp.float32)
     upward = jnp.einsum("nlscd,ldf->nlscf", column_rows, w_up, preferred_element_type=jnp.float32)
     activation = (jax.nn.silu(gated) * upward).astype(jnp.bfloat16)
-    summed = lax.psum_scatter(
-        jnp.einsum(
-            "nlscf,lfd->nlscd", activation, w_down, preferred_element_type=jnp.float32
-        ).astype(jnp.bfloat16),
-        "blk",
-        scatter_dimension=0,
-        tiled=True,
-    )
+    partial_out = jnp.einsum(
+        "nlscf,lfd->nlscd", activation, w_down, preferred_element_type=jnp.float32
+    ).astype(jnp.bfloat16)
+    partial_out = lax.all_to_all(partial_out, "blk", 0, 0, tiled=True)
+    summed = jnp.sum(partial_out.astype(jnp.float32), axis=0, keepdims=True).astype(jnp.bfloat16)
     returned = lax.all_to_all(summed, "expert", split_axis=2, concat_axis=2, tiled=True)
     returned = returned.reshape(local_experts * exp_count * CAP, model_width)
     gathered_back = jnp.einsum(

time: 393 us -> 196 us (0.50)
  waiting for transfers between devices: 159 us -> 42.6 us
  blocking collectives: 147 us -> 45 us
  starting transfers between devices: 6.73 us -> 28.5 us
  between operations: 14.2 us -> 1.05 us
  local copies, waits for them, and re-layouts: 31.3 us -> 40.8 us
    unnamed x5 -> x0, waiting for transfers between devices: 112 us -> none
    pmax x1 -> x0, blocking collectives: 58.1 us -> none  [local(): top_score = lax.pmax(local_top, 'blk')]
    unnamed x1 -> x0, blocking collectives: 55.9 us -> none
    all_gather x1 -> x0, waiting for transfers between devices: 42.4 us -> none  [local(): column_rows = lax.all_gather(arrived[None], 'blk', axis=0, tiled=True)]
    all_to_all x0 -> x3, waiting for transfers between devices: none -> 37.8 us  [the longest x1 27.5 us: local(): partial_out = lax.all_to_all(partial_out, 'blk', 0, 0, tiled=True)]
    all_to_all x0 -> x1, blocking collectives: none -> 32.5 us  [local(): lax.all_to_all(jnp.broadcast_to(arrived[None], (blk_count, *arrived.shape...]
    all_gather x1 -> x0, blocking collectives: 21.1 us -> none  [local(): everyone_q = lax.all_gather(query, 'blk', axis=0, tiled=True)]
    all_to_all x0 -> x3, starting transfers between devices: none -> 19.7 us  [the longest x1 8.43 us: local(): lax.all_to_all(jnp.broadcast_to(query, (blk_count, *query.shape[1:])), 'b...]
  transfers between devices with their start and end apart: 4 -> 4, of which waited for: 4 -> 3; matrix products, arithmetic and copies ran while one was open for 2% -> 13% of each run, Pallas kernels for 0% -> 0%
where the time goes in v1:
time: 196 us; the launch traced here: 195 us
  blocking collectives  45 us (23%)
  waiting for transfers between devices  42.6 us (22%)
  local copies, waits for them, and re-layouts  40.8 us (21%)
  starting transfers between devices  28.5 us (15%)
  matrix products  24.3 us (12%)
  other arithmetic  12.9 us (7%)
    all_to_all x1, blocking collectives, local(): lax.all_to_all(jnp.broadcast_to(arrived[None], (blk_count, *arrived.shape...  32.5 us
    all_to_all x1, waiting for transfers between devices, local(): partial_out = lax.all_to_all(partial_out, 'blk', 0, 0, tiled=True)  27.5 us
    all_to_all x1, blocking collectives, local(): lax.all_to_all(outgoing, 'expert', split_axis=1, concat_axis=1, tiled=True)  12.5 us
    all_to_all x1, waiting for transfers between devices, local(): got = lax.all_to_all(sent, 'blk', 0, 0, tiled=True)  10.3 us
    all_to_all x1, starting transfers between devices, local(): lax.all_to_all(summed, 'expert', split_axis=2, concat_axis=2, tiled=True)  8.89 us
    all_to_all x1, starting transfers between devices, local(): lax.all_to_all(jnp.broadcast_to(query, (blk_count, *query.shape[1:])), 'b...  8.43 us
    all_to_all x1, starting transfers between devices, local(): got = lax.all_to_all(sent, 'blk', 0, 0, tiled=True)  6.65 us
    dot_general x1, matrix products, local(): jnp.einsum('nlscf,lfd->nlscd', activation, w_down, preferred_element_type...  6.32 us
  transfers between devices with their start and end apart: 4, of which 3 were waited for; matrix products, arithmetic and copies ran while one was open for 13% of the time, Pallas kernels for 0%

profile of v1, /device:TPU:1, one launch (start us, length us, event | category | flops | bytes accessed | tf_op | source)
XLA Modules:
  0.0 195.2 jit_solution(6186664996181829147)
XLA Ops:
  0.7 2.1 %broadcast_in_dim.123 = bf16[16,4,2,2304]{3,2,1,0:T(2,128)(2,1)} broadcast(bf16[4,2,2304]{2,1,0:T(2,128)(2,1)} %bitcast.170), dimensions={1,2,3} | broadcast | bytes 626688 | tf_op jit(solution)/shard_map/broadcast_in_dim | solution.py:63
  2.7 8.4 %all-to-all-start = ((bf16[16,4,2,2304]{3,2,1,0:T(2,128)(2,1)}), bf16[16,4,2,2304]{3,2,1,0:T(2,128)(2,1)S(1)}, u32[]{:S(2)}, u32[]{:S(2)}) async-start(bf16[16,4,2,2304]{3,2,1,0:T(2,128)(2,1)} %broadcast_in_dim.123), calls=%async_computation | async-start | bytes 1179648 | tf_op jit(solution)/shard_map/all_to_all | solution.py:62
  16.7 3.0 %reshape.348 = bf16[4,64,36,64]{3,2,1,0:T(8,128)(2,1)} reshape(bf16[4,64,2304]{2,1,0:T(8,128)(2,1)S(1)} %copy-done.6) | data formatting | bytes 2359296 | tf_op jit(solution)/shard_map/reshape | solution.py:66
  20.8 4.4 %reshape_squeeze.15 = bf16[4,64,36,64]{3,2,1,0:T(8,128)(2,1)} reshape(bf16[1,4,64,2304]{3,2,1,0:T(8,128)(2,1)} %param.27) | data formatting | bytes 2359296 | tf_op jit(solution)/shard_map/reshape;squeeze | solution.py:74
  25.2 3.0 %reshape_squeeze.16 = bf16[4,64,36,64]{3,2,1,0:T(8,128)(2,1)} reshape(bf16[1,4,64,2304]{3,2,1,0:T(8,128)(2,1)S(1)} %copy-done.7) | data formatting | bytes 2359296 | tf_op jit(solution)/shard_map/reshape;squeeze | solution.py:75
  28.2 4.4 %reshape.350 = bf16[4,64,36,64]{3,2,1,0:T(8,128)(2,1)} reshape(bf16[4,64,2304]{2,1,0:T(8,128)(2,1)} %param.24) | data formatting | bytes 2359296 | tf_op jit(solution)/shard_map/reshape | solution.py:67
  34.3 2.2 %reshape.374 = bf16[16,4,2,36,64]{4,3,2,1,0:T(8,128)(2,1)} reshape(bf16[16,4,2,2304]{3,2,1,0:T(2,128)(2,1)S(1)} %all-to-all-done) | data formatting | bytes 1179648 | tf_op jit(solution)/shard_map/reshape | solution.py:65
  36.5 5.0 %bitcast_reduce_fusion.1 = (bf16[16,4,2,36]{0,2,3,1:T(2,128)(2,1)S(1)}, f32[4,36,64,16,2]{2,3,4,1,0:T(8,128)}) fusion(pred[4,64]{1,0:T(4,128)(4,1)S(1)} %compare_and_fusion, bf16[16,4,2,36,64]{4,3,2,1,0:T(8,128)(2,1)} %reshape.374, bf16[4,64,36,64,1]{3,2,1,0,4:T(8,128)(2,1)} %bitcast.162), kind=kOutput, calls=%fused_computation.16 | convolution fusion | flops 38628864 | bytes 2958592 | tf_op jit(solution)/shard_map/mpthd,pkhd->mpthk/dot_general | solution.py:70
  41.7 4.6 %fusion.15 = (bf16[16,4,2,36]{0,2,3,1:T(2,128)(2,1)S(1)}, f32[4,36,64,16,2]{2,3,4,1,0:T(8,128)}) fusion(pred[16,4,64]{2,0,1:T(8,128)(4,1)S(1)} %fusion.84, bf16[16,4,2,36,64]{4,3,2,1,0:T(8,128)(2,1)S(1)} %copy-done.5, bf16[4,64,36,64,1]{3,2,1,0,4:T(8,128)(2,1)} %bitcast.163), kind=kOutput, calls=%fused_computation.24 | convolution fusion | flops 38628864 | bytes 2962432 | tf_op jit(solution)/shard_map/mpthd,pkhd->mpthk/dot_general | solution.py:82
  46.6 4.0 %fusion.18 = (f32[16,4,2,36]{0,2,3,1:T(2,128)S(1)}, f32[16,4,2,36]{0,2,3,1:T(2,128)S(1)}) fusion(f32[4,36,64,16,2]{2,3,4,1,0:T(8,128)} %get-tuple-element.17, f32[16,4,2,36]{0,2,3,1:T(2,128)S(1)} %copy.274, pred[16,4,64]{2,0,1:T(8,128)(4,1)S(1)} %fusion.84, f32[4,36,64,16,2]{2,3,4,1,0:T(8,128)} %get-tuple-element.15, pred[4,64]{1,0:T(4,128)(4,1)S(1)} %compare_and_fusion), kind=kLoop, calls=%fused_computation.25 | loop fusion | flops 2939904 | bytes 2418944 | tf_op jit(solution)/shard_map/reduce_sum | solution.py:95
  51.0 3.5 %fusion.5 = f32[4,36,16,2,64]{4,2,3,1,0:T(8,128)S(1)} fusion(bf16[4,64,36,64,1]{3,2,1,0,4:T(8,128)(2,1)} %bitcast.161, f32[4,36,64,16,2]{2,3,4,1,0:T(8,128)} %get-tuple-element.17, f32[16,4,2,36]{0,2,3,1:T(2,128)S(1)} %copy.274, pred[16,4,64]{2,0,1:T(8,128)(4,1)S(1)} %fusion.84), kind=kOutput, calls=%fused_computation.8 | convolution fusion | flops 39223296 | bytes 3561472 | tf_op jit(solution)/shard_map/mpthk,pkhd->mpthd/dot_general | solution.py:102
  58.3 1.9 concatenate.7
  60.2 6.7 %all-to-all-start.1 = ((bf16[16,8,2412]{2,1,0:T(8,128)(2,1)}), bf16[16,8,2412]{2,1,0:T(8,128)(2,1)S(1)}, u32[]{:S(2)}, u32[]{:S(2)}) async-start(bf16[16,8,2412]{2,1,0:T(8,128)(2,1)} %concatenate.7), calls=%async_computation.1 | async-start | bytes 1245184 | tf_op jit(solution)/shard_map/all_to_all | solution.py:120
  67.3 10.3 %all-to-all-done.1 = bf16[16,8,2412]{2,1,0:T(8,128)(2,1)S(1)} async-done(((bf16[16,8,2412]{2,1,0:T(8,128)(2,1)}), bf16[16,8,2412]{2,1,0:T(8,128)(2,1)S(1)}, u32[]{:S(2)}, u32[]{:S(2)}) %all-to-all-start.1) | async-done | bytes 617504 | tf_op jit(solution)/shard_map/all_to_all | solution.py:120
  78.6 1.9 mul.135
  80.6 2.0 %mul.136 = f32[16,4,2,2304]{3,0,2,1:T(8,128)S(1)} reshape(f32[16,4,2,36,64]{4,3,0,2,1:T(8,128)} %mul.135) | data formatting | bytes 2359296 | tf_op jit(solution)/shard_map/mul | solution.py:138
  88.9 12.5 %all_to_all.30 = bf16[1,8,4,2304]{3,2,0,1:T(4,128)(2,1)S(1)} all-to-all(bf16[1,8,4,2304]{3,2,0,1:T(4,128)(2,1)S(1)} %bitcast.165), channel_id=1, replica_groups=mesh['blk'=16,'expert'=8] {'expert'}, dimensions={1} | all-to-all | bytes 294912 | tf_op jit(solution)/shard_map/all_to_all | solution.py:172
  101.7 32.5 %all_to_all.31 = bf16[16,1,8,4,2304]{4,2,3,1,0:T(8,128)(2,1)S(1)} all-to-all(bf16[16,1,8,4,2304]{4,2,3,1,0:T(8,128)(2,1)S(1)} %broadcast_in_dim.135), channel_id=1, replica_groups=mesh['blk'=16,'expert'=8] {'blk'}, dimensions={0} | all-to-all | bytes 4718592 | tf_op jit(solution)/shard_map/all_to_all | solution.py:173
  136.9 6.3 %fusion = bf16[16,1,8,4,2304]{4,2,3,1,0:T(8,128)(2,1)} fusion(bf16[1,360,2304]{2,1,0:T(8,128)(2,1)S(1)} %copy-done, bf16[1,2304,360]{1,2,0:T(8,128)(2,1)} %param.35, bf16[16,1,8,4,2304]{4,2,3,1,0:T(8,128)(2,1)} %copy-done.3, f32[16,1,8,4,360]{4,2,3,0,1:T(8,128)S(1)} %fusion.28), kind=kOutput, calls=%fused_computation.1 | convolution fusion | flops 1700978688 | bytes 8773632 | tf_op jit(solution)/shard_map/nlscf,lfd->nlscd/dot_general | solution.py:179
  143.3 4.6 %all-to-all-start.4 = ((bf16[16,1,8,4,2304]{4,2,3,1,0:T(8,128)(2,1)}), bf16[16,1,8,4,2304]{4,2,3,1,0:T(8,128)(2,1)}, u32[]{:S(2)}, u32[]{:S(2)}) async-start(bf16[16,1,8,4,2304]{4,2,3,1,0:T(8,128)(2,1)} %fusion), calls=%async_computation.4 | async-start | bytes 4718592 | tf_op jit(solution)/shard_map/all_to_all | solution.py:182
  148.4 27.5 %all-to-all-done.4 = bf16[16,1,8,4,2304]{4,2,3,1,0:T(8,128)(2,1)} async-done(((bf16[16,1,8,4,2304]{4,2,3,1,0:T(8,128)(2,1)}), bf16[16,1,8,4,2304]{4,2,3,1,0:T(8,128)(2,1)}, u32[]{:S(2)}, u32[]{:S(2)}) %all-to-all-start.4) | async-done | bytes 2359328 | tf_op jit(solution)/shard_map/all_to_all | solution.py:182
  176.0 2.0 %bitcast_reduce_fusion = bf16[8,4,2304]{2,0,1:T(8,128)(2,1)S(1)} fusion(bf16[16,1,8,4,2304]{4,2,3,1,0:T(8,128)(2,1)} %all-to-all-done.4), kind=kLoop, calls=%fused_computation.3 | loop fusion | flops 1105920 | bytes 2506752 | tf_op jit(solution)/shard_map/reduce_sum | solution.py:183
  178.6 8.9 %all-to-all-start.5 = ((bf16[1,1,8,4,2304]{4,3,1,0,2:T(4,128)(2,1)}), bf16[1,1,8,4,2304]{4,3,1,0,2:T(4,128)(2,1)S(1)}, u32[]{:S(2)}, u32[]{:S(2)}) async-start(bf16[1,1,8,4,2304]{4,3,1,0,2:T(4,128)(2,1)} %copy.310), calls=%async_computation.5 | async-start | bytes 294912 | tf_op jit(solution)/shard_map/all_to_all | solution.py:184
  188.2 4.8 %all-to-all-done.5 = bf16[1,1,8,4,2304]{4,3,1,0,2:T(4,128)(2,1)S(1)} async-done(((bf16[1,1,8,4,2304]{4,3,1,0,2:T(4,128)(2,1)}), bf16[1,1,8,4,2304]{4,3,1,0,2:T(4,128)(2,1)S(1)}, u32[]{:S(2)}, u32[]{:S(2)}) %all-to-all-start.5) | async-done | bytes 147488 | tf_op jit(solution)/shard_map/all_to_all | solution.py:184
  (125 shorter events, 27.6 us)
Async XLA Ops:
  0.6 136.3 %copy-start = (bf16[1,360,2304]{2,1,0:T(8,128)(2,1)S(1)}, bf16[1,360,2304]{2,1,0:T(8,128)(2,1)}, u32[]{:S(2)}) copy-start(bf16[1,360,2304]{2,1,0:T(8,128)(2,1)} %param.36) | copy-start | bytes 4976644
  0.6 16.1 %copy-start.6 = (bf16[4,64,2304]{2,1,0:T(8,128)(2,1)S(1)}, bf16[4,64,2304]{2,1,0:T(8,128)(2,1)}, u32[]{:S(2)}) copy-start(bf16[4,64,2304]{2,1,0:T(8,128)(2,1)} %param.23) | copy-start | bytes 3538948
  2.7 31.6 %all-to-all-start = ((bf16[16,4,2,2304]{3,2,1,0:T(2,128)(2,1)}), bf16[16,4,2,2304]{3,2,1,0:T(2,128)(2,1)S(1)}, u32[]{:S(2)}, u32[]{:S(2)}) async-start(bf16[16,4,2,2304]{3,2,1,0:T(2,128)(2,1)} %broadcast_in_dim.123), calls=%async_computation | async-start | bytes 1179648 | tf_op jit(solution)/shard_map/all_to_all | solution.py:62
  11.1 9.5 %copy-start.15 = (s32[16,32]{1,0:T(8,128)S(1)}, s32[16,32]{1,0:T(8,128)}, u32[]{:S(2)}) copy-start(s32[16,32]{1,0:T(8,128)} %param.29) | copy-start | bytes 6148
  19.7 5.5 %copy-start.7 = (bf16[1,4,64,2304]{3,2,1,0:T(8,128)(2,1)S(1)}, bf16[1,4,64,2304]{3,2,1,0:T(8,128)(2,1)}, u32[]{:S(2)}) copy-start(bf16[1,4,64,2304]{3,2,1,0:T(8,128)(2,1)} %param.28) | copy-start | bytes 3538948
  28.2 4.4 %copy-start.10 = (bf16[1,4,2,2304]{3,2,1,0:T(2,128)(2,1)S(1)}, bf16[1,4,2,2304]{3,2,1,0:T(2,128)(2,1)}, u32[]{:S(2)}) copy-start(bf16[1,4,2,2304]{3,2,1,0:T(2,128)(2,1)} %param.21) | copy-start | bytes 110596
  28.2 5.0 %copy-start.11 = (bf16[1,4,2,2304]{3,2,1,0:T(2,128)(2,1)S(1)}, bf16[1,4,2,2304]{3,2,1,0:T(2,128)(2,1)}, u32[]{:S(2)}) copy-start(bf16[1,4,2,2304]{3,2,1,0:T(2,128)(2,1)} %param.22) | copy-start | bytes 110596
  28.2 5.8 %copy-start.14 = (s32[1,4,2,2]{1,3,2,0:T(2,128)S(1)}, s32[1,4,2,2]{1,3,2,0:T(2,128)}, u32[]{:S(2)}) copy-start(s32[1,4,2,2]{1,3,2,0:T(2,128)} %param.31) | copy-start | bytes 196
  36.5 5.2 %copy-start.5 = (bf16[16,4,2,36,64]{4,3,2,1,0:T(8,128)(2,1)S(1)}, bf16[16,4,2,36,64]{4,3,2,1,0:T(8,128)(2,1)}, u32[]{:S(2)}) copy-start(bf16[16,4,2,36,64]{4,3,2,1,0:T(8,128)(2,1)} %reshape.374) | copy-start | bytes 1769476
  51.0 3.5 %copy-start.1 = (bf16[4,64,36,64]{3,2,1,0:T(8,128)(2,1)S(1)}, bf16[4,64,36,64]{3,2,1,0:T(8,128)(2,1)}, u32[]{:S(2)}) copy-start(bf16[4,64,36,64]{3,2,1,0:T(8,128)(2,1)} %reshape.350) | copy-start | bytes 3538948
  51.0 3.9 %copy-start.2 = (f32[4,36,64,16,2]{2,3,4,1,0:T(8,128)S(1)}, f32[4,36,64,16,2]{2,3,4,1,0:T(8,128)}, u32[]{:S(2)}) copy-start(f32[4,36,64,16,2]{2,3,4,1,0:T(8,128)} %get-tuple-element.15) | copy-start | bytes 3538948
  60.2 17.3 %all-to-all-start.1 = ((bf16[16,8,2412]{2,1,0:T(8,128)(2,1)}), bf16[16,8,2412]{2,1,0:T(8,128)(2,1)S(1)}, u32[]{:S(2)}, u32[]{:S(2)}) async-start(bf16[16,8,2412]{2,1,0:T(8,128)(2,1)} %concatenate.7), calls=%async_computation.1 | async-start | bytes 1245184 | tf_op jit(solution)/shard_map/all_to_all | solution.py:120
  82.6 5.0 %copy-start.12 = (f32[2304]{0:T(1024)S(1)}, f32[2304]{0:T(1024)}, u32[]{:S(2)}) copy-start(f32[2304]{0:T(1024)} %param.33) | copy-start | bytes 27652
  101.7 33.9 %copy-start.16 = (bf16[1,2304,360]{1,2,0:T(8,128)(2,1)S(1)}, bf16[1,2304,360]{1,2,0:T(8,128)(2,1)}, u32[]{:S(2)}) copy-start(bf16[1,2304,360]{1,2,0:T(8,128)(2,1)} %param.34) | copy-start | bytes 4976644
  134.1 1.4 copy-start.3
  143.3 4.9 %copy-start.13 = (f32[2304]{0:T(1024)S(1)}, f32[2304]{0:T(1024)}, u32[]{:S(2)}) copy-start(f32[2304]{0:T(1024)} %param.37) | copy-start | bytes 27652
  143.3 5.0 %copy-start.9 = (f32[2304,8]{0,1:T(8,128)S(1)}, f32[2304,8]{0,1:T(8,128)}, u32[]{:S(2)}) copy-start(f32[2304,8]{0,1:T(8,128)} %param.32) | copy-start | bytes 221188
  143.3 32.7 %all-to-all-start.4 = ((bf16[16,1,8,4,2304]{4,2,3,1,0:T(8,128)(2,1)}), bf16[16,1,8,4,2304]{4,2,3,1,0:T(8,128)(2,1)}, u32[]{:S(2)}, u32[]{:S(2)}) async-start(bf16[16,1,8,4,2304]{4,2,3,1,0:T(8,128)(2,1)} %fusion), calls=%async_computation.4 | async-start | bytes 4718592 | tf_op jit(solution)/shard_map/all_to_all | solution.py:182
  148.4 45.1 %copy-start.8 = (bf16[1,4,2,2304]{3,2,1,0:T(2,128)(2,1)S(1)}, bf16[1,4,2,2304]{3,2,1,0:T(2,128)(2,1)}, u32[]{:S(2)}) copy-start(bf16[1,4,2,2304]{3,2,1,0:T(2,128)(2,1)} %param.19) | copy-start | bytes 110596
  148.4 45.9 %copy-start.4 = (f32[4,2,36,64]{3,2,1,0:T(8,128)S(1)}, f32[4,2,36,64]{3,2,1,0:T(8,128)}, u32[]{:S(2)}) copy-start(f32[4,2,36,64]{3,2,1,0:T(8,128)} %reshape.364) | copy-start | bytes 221188
  178.6 14.3 %all-to-all-start.5 = ((bf16[1,1,8,4,2304]{4,3,1,0,2:T(4,128)(2,1)}), bf16[1,1,8,4,2304]{4,3,1,0,2:T(4,128)(2,1)S(1)}, u32[]{:S(2)}, u32[]{:S(2)}) async-start(bf16[1,1,8,4,2304]{4,3,1,0,2:T(4,128)(2,1)} %copy.310), calls=%async_computation.5 | async-start | bytes 294912 | tf_op jit(solution)/shard_map/all_to_all | solution.py:184

commit v2 on v0

v2 whole, which is shorter than its diff:
```python
import jax
import jax.numpy as jnp
from jax import lax
from jax.experimental import pallas as pl
from jax.experimental.pallas import tpu as pltpu
from jax.sharding import PartitionSpec as P

HDIM = 64
TOP = 2
KVB = 16
CAP = 4
LANES = 128

BF = jnp.bfloat16
F32 = jnp.float32
HIDE = -1e30
FLOOR = -1e4
NT = (((1,), (1,)), ((), ()))


def vmem():
    return pl.BlockSpec(memory_space=pltpu.VMEM)


def smem():
    return pl.BlockSpec(memory_space=pltpu.SMEM)


def iota(shape, dim):
    return lax.broadcasted_iota(jnp.int32, shape, dim)


def dot(a, b, dims=(((1,), (0,)), ((), ()))):
    return lax.dot_general(a, b, dims, preferred_element_type=F32)


def attend_kernel(
    place, lengths, live, tail_len, source, q_ref, k_ref, v_ref, tk_ref, tv_ref, out_ref,
    bias, picks, stat_top, stat_sum,
):
    step = pl.program_id(0)
    prompts, span, width = k_ref.shape
    rows = q_ref.shape[0]
    fresh = 2
    group = prompts * fresh
    samples = rows // group
    heads = out_ref.shape[1] // HDIM - 2
    model = heads * HDIM
    pairs = width // LANES

    @pl.when(step == 0)
    def _():
        blk, exp = place[0], place[1]
        lane = iota((group, LANES), 1)
        sub = iota((group, LANES), 0) // fresh
        ok = jnp.zeros((group, LANES), jnp.int32)
        tail_ok = jnp.zeros((group, LANES), jnp.int32)
        owner = jnp.zeros((group, LANES), jnp.int32)
        for p in range(prompts):
            at = exp * prompts + p
            kept = jnp.zeros((group, LANES), jnp.int32)
            for b in range(span // KVB):
                page = live[at, blk * (span // KVB) + b]
                kept = jnp.where(lane // KVB == b, page, kept)
            left = jnp.minimum(lengths[at] - blk * span, span)
            ok_p = jnp.where(lane < left, jnp.where(kept > 0, 1, 0), 0)
            who = source[blk, at]
            held = tail_len[who, at]
            tail_p = jnp.where(lane >= span, jnp.where(lane - span < held, 1, 0), 0)
            ok = jnp.where(sub == p, ok_p, ok)
            tail_ok = jnp.where(sub == p, tail_p, tail_ok)
            owner = jnp.where(sub == p, who, owner)
        for m in range(samples):
            use = ok + jnp.where(owner == m, tail_ok, 0)
            bias[m * group : (m + 1) * group, :] = jnp.where(use > 0, 0.0, HIDE)
        row_p = (iota((rows, LANES), 0) % group) // fresh
        half = iota((rows, LANES), 1) // HDIM
        for p in range(prompts):
            mine = jnp.where(row_p == p, 1.0, 0.0)
            picks[2 * prompts + p] = mine.astype(BF)
            for h in range(2):
                picks[2 * p + h] = jnp.where(half == h, mine * 0.125, 0.0).astype(BF)
        stat_top[...] = jnp.zeros_like(stat_top)
        stat_sum[...] = jnp.zeros_like(stat_sum)

    lane = iota((rows, LANES), 1)
    hide = jnp.concatenate([bias[...], bias[...]], axis=0)
    for i in range(pairs):
        cut = slice(i * LANES, (i + 1) * LANES)
        pair = step * pairs + i
        q = q_ref[:, cut]
        q_wide = jnp.concatenate(
            [
                jnp.concatenate([q * picks[2 * p], q * picks[2 * p + 1]], axis=0)
                for p in range(prompts)
            ],
            axis=1,
        )
        k_wide = jnp.concatenate(
            [jnp.concatenate([k_ref[p, :, cut], tk_ref[p, :, cut]], axis=0) for p in range(prompts)],
            axis=1,
        )
        scores = dot(q_wide, k_wide, NT) + hide
        top = jnp.maximum(jnp.max(scores, axis=1, keepdims=True), FLOOR)
        top = top.astype(BF).astype(F32)
        weight = jnp.exp(scores - top)
        total = jnp.sum(weight, axis=1, keepdims=True)
        weight = weight.astype(BF)
        w_wide = jnp.concatenate(
            [
                weight * jnp.concatenate([picks[2 * prompts + p], picks[2 * prompts + p]], axis=0)
                for p in range(prompts)
            ],
            axis=1,
        )
        v_high = jnp.concatenate(
            [jnp.concatenate([v_ref[p, :, cut], tv_ref[p, :, cut]], axis=0) for p in range(prompts)],
            axis=0,
        )
        both = dot(w_wide, v_high)
        mixed = jnp.where(lane < HDIM, both[:rows], both[rows:])
        out_ref[:, pl.ds(pl.multiple_of(pair * LANES, LANES), LANES)] = mixed.astype(BF)
        for h in range(2):
            at = 2 * pair + h
            stat_top[...] = jnp.where(lane == at, top[h * rows : (h + 1) * rows], stat_top[...])
            stat_sum[...] = jnp.where(
                lane == heads + at, total[h * rows : (h + 1) * rows], stat_sum[...]
            )

    @pl.when(step == pl.num_programs(0) - 1)
    def _():
        sums = stat_sum[...]
        high = sums.astype(BF).astype(F32)
        low = pltpu.roll(sums - high, heads, 1)
        out_ref[:, model:] = (stat_top[...] + high + low).astype(BF)


def attend(place, lengths, live, tail_len, source, everyone, key, value, tail_key, tail_value):
    rows, model = everyone.shape
    prompts, span, _ = key.shape
    chunk = 3 * LANES
    cache = pl.BlockSpec((prompts, span, chunk), lambda i, *_: (0, 0, i))
    return pl.pallas_call(
        attend_kernel,
        out_shape=jax.ShapeDtypeStruct((rows, model + LANES), BF),
        grid_spec=pltpu.PrefetchScalarGridSpec(
            num_scalar_prefetch=5,
            grid=(model // chunk,),
            in_specs=[pl.BlockSpec((rows, chunk), lambda i, *_: (0, i)), cache, cache, cache, cache],
            out_specs=pl.BlockSpec((rows, model + LANES), lambda i, *_: (0, 0)),
            scratch_shapes=[
                pltpu.VMEM((rows, LANES), F32),
                pltpu.VMEM((3 * prompts, rows, LANES), BF),
                pltpu.VMEM((rows, LANES), F32),
                pltpu.VMEM((rows, LANES), F32),
            ],
        ),
        compiler_params=pltpu.CompilerParams(vmem_limit_bytes=24 << 20),
        name="attend",
    )(place, lengths, live, tail_len, source, everyone, key, value, tail_key, tail_value)


def combine_kernel(
    routes, got_ref, q_ref, k_ref, v_ref, h_ref, router_ref, gain_ref,
    mixed_ref, rows_ref, gate_ref, q8, k0, k1, v0, v1, spread,
):
    parts, tokens, wide = got_ref.shape
    model = wide - LANES
    heads = model // HDIM
    prompts, fresh = q_ref.shape[1], q_ref.shape[2]
    experts = router_ref.shape[0]
    for p in range(prompts):
        at = slice(fresh * p, fresh * (p + 1))
        q8[at, :] = q_ref[0, p].astype(F32)
        mixed_ref[at, :] = h_ref[0, p].astype(F32)
        key, val = k_ref[0, p].astype(F32), v_ref[0, p].astype(F32)
        k0[at, :] = jnp.broadcast_to(key[0:1], (fresh, model))
        k1[at, :] = jnp.broadcast_to(key[1:2], (fresh, model))
        v0[at, :] = jnp.broadcast_to(val[0:1], (fresh, model))
        v1[at, :] = jnp.broadcast_to(val[1:2], (fresh, model))
    spread[...] = jnp.where(
        iota((LANES, model), 1) // HDIM == iota((LANES, model), 0), 1.0, 0.0
    ).astype(BF)
    product = jnp.concatenate([q8[...] * k0[...], q8[...] * k1[...]], axis=0)
    high = product.astype(BF)
    low = (product - high.astype(F32)).astype(BF)
    own = (dot(high, spread[...], NT) + dot(low, spread[...], NT)) * 0.125
    lane = iota((tokens, LANES), 1)
    sub = iota((tokens, LANES), 0)
    s0 = own[:tokens]
    s1 = jnp.where(sub % fresh == 1, own[tokens:], HIDE)
    top = jnp.maximum(s0, s1)
    tops, sums = [], []
    for j in range(parts):
        stat = got_ref[j, :, model:].astype(F32)
        tops.append(jnp.where(lane < heads, stat, 0.0))
        total = pltpu.roll(stat, LANES - heads, 1) + pltpu.roll(stat, LANES - 2 * heads, 1)
        sums.append(jnp.where(lane < heads, total, 1.0))
        top = jnp.maximum(top, tops[-1])
    w0, w1 = jnp.exp(s0 - top), jnp.exp(s1 - top)
    scale = [jnp.exp(t - top) for t in tops]
    total = w0 + w1
    for c, l in zip(scale, sums):
        total = total + c * l
    inverse = 1.0 / total
    share = jnp.concatenate([c * inverse for c in scale] + [w0 * inverse, w1 * inverse], axis=0)
    share_high = share.astype(BF)
    share_low = (share - share_high.astype(F32)).astype(BF)
    square = jnp.zeros((tokens, LANES), F32)
    chunk = 2 * LANES
    for c in range(model // chunk):
        cut = slice(c * chunk, (c + 1) * chunk)
        each = dot(share_high, spread[:, cut]) + dot(share_low, spread[:, cut])
        here = mixed_ref[:, cut]
        for j in range(parts):
            here = here + each[j * tokens : (j + 1) * tokens] * got_ref[j, :, cut].astype(F32)
        here = here + each[parts * tokens : (parts + 1) * tokens] * v0[:, cut]
        here = here + each[(parts + 1) * tokens :] * v1[:, cut]
        mixed_ref[:, cut] = here
        for i in range(chunk // LANES):
            part = here[:, i * LANES : (i + 1) * LANES]
            square = square + part * part
    mean = jnp.sum(square, axis=1, keepdims=True) / model
    normed = (mixed_ref[...] * lax.rsqrt(mean + 1e-05) * gain_ref[...]).astype(BF).astype(F32)
    logits = [jnp.sum(normed * router_ref[e : e + 1, :], axis=1, keepdims=True) for e in range(experts)]
    token = iota((tokens, 1), 0)
    first = jnp.zeros((tokens, 1), jnp.int32)
    second = jnp.zeros((tokens, 1), jnp.int32)
    slots = experts * CAP
    row = iota((slots, tokens), 0)
    column = iota((slots, tokens), 1)
    pick = jnp.zeros((slots, tokens), F32)
    seen = jnp.zeros((slots, tokens), jnp.int32)
    for i in range(tokens):
        pair = [routes[0, i // fresh, i % fresh, r] for r in range(TOP)]
        first = jnp.where(token == i, pair[0], first)
        second = jnp.where(token == i, pair[1], second)
        for expert in pair:
            match = row // CAP == expert
            hit = jnp.where(match, jnp.where(column == i, jnp.where(row % CAP == seen, 1.0, 0.0), 0.0), 0.0)
            pick = pick + hit
            seen = seen + jnp.where(match, 1, 0)
    logit0 = jnp.zeros((tokens, 1), F32)
    logit1 = jnp.zeros((tokens, 1), F32)
    for e in range(experts):
        logit0 = jnp.where(first == e, logits[e], logit0)
        logit1 = jnp.where(second == e, logits[e], logit1)
    gate0 = 1.0 / (1.0 + jnp.exp(logit1 - logit0))
    gate1 = 1.0 / (1.0 + jnp.exp(logit0 - logit1))
    gate_ref[...] = jnp.where(lane == 0, gate0, jnp.where(lane == 1, gate1, 0.0))
    outgoing = dot(pick, normed).astype(BF)
    for e in range(experts):
        rows_ref[e] = outgoing[e * CAP : (e + 1) * CAP]


def combine(routes, got, query, new_key, new_value, hidden, router, gain):
    parts, tokens, wide = got.shape
    model = wide - LANES
    experts = router.shape[0]
    return pl.pallas_call(
        combine_kernel,
        out_shape=(
            jax.ShapeDtypeStruct((tokens, model), F32),
            jax.ShapeDtypeStruct((experts, CAP, model), BF),
            jax.ShapeDtypeStruct((tokens, LANES), F32),
        ),
        in_specs=[smem()] + [vmem()] * 7,
        out_specs=(vmem(), vmem(), vmem()),
        scratch_shapes=[pltpu.VMEM((tokens, model), F32)] * 5 + [pltpu.VMEM((LANES, model), BF)],
        compiler_params=pltpu.CompilerParams(vmem_limit_bytes=16 << 20),
        name="combine",
    )(routes, got, query, new_key, new_value, hidden, router, gain)


def ffn_kernel(x_ref, gate_ref, up_ref, down_ref, out_ref):
    x = x_ref[...]
    gated = dot(x, gate_ref[...], NT)
    upward = dot(x, up_ref[...], NT)
    activation = (gated / (1.0 + jnp.exp(-gated)) * upward).astype(BF)
    out_ref[...] = dot(activation, down_ref[...]).astype(BF)


def ffn(x, w_gate, w_up, w_down):
    rows, model = x.shape
    units = w_down.shape[0]
    step = 128
    whole = pl.BlockSpec((units, model), lambda i: (0, 0))
    moving = pl.BlockSpec((step, model), lambda i: (i, 0))
    return pl.pallas_call(
        ffn_kernel,
        out_shape=jax.ShapeDtypeStruct((rows, model), BF),
        grid=(rows // step,),
        in_specs=[moving, whole, whole, whole],
        out_specs=moving,
        compiler_params=pltpu.CompilerParams(vmem_limit_bytes=24 << 20),
        name="ffn",
    )(x, w_gate, w_up, w_down)


def finish_kernel(routes, back_ref, mixed_ref, gate_ref, weight_ref, out_ref, score_ref, whole):
    slots, model = whole.shape
    tokens = mixed_ref.shape[0]
    prompts, fresh = out_ref.shape[1], out_ref.shape[2]
    for e in range(slots // CAP):
        whole[e * CAP : (e + 1) * CAP, :] = back_ref[e].astype(F32)
    row = iota((tokens, slots), 0)
    column = iota((tokens, slots), 1)
    seen = jnp.zeros((tokens, slots), jnp.int32)
    picks = [jnp.zeros((tokens, slots), F32) for _ in range(TOP)]
    for i in range(tokens):
        for r in range(TOP):
            match = column // CAP == routes[0, i // fresh, i % fresh, r]
            hit = jnp.where(match, jnp.where(row == i, jnp.where(column % CAP == seen, 1.0, 0.0), 0.0), 0.0)
            picks[r] = picks[r] + hit
            seen = seen + jnp.where(match, 1, 0)
    every = whole[...]
    total = mixed_ref[...]
    for r in range(TOP):
        total = total + gate_ref[:, r : r + 1] * dot(picks[r], every)
    done = total.astype(BF)
    score_ref[...] = jnp.sum(done.astype(F32) * weight_ref[...], axis=1, keepdims=True)
    for p in range(prompts):
        out_ref[0, p] = done[fresh * p : fresh * (p + 1)]


def finish(routes, back, mixed, gates, weight):
    tokens, model = mixed.shape
    prompts, fresh = routes.shape[1], routes.shape[2]
    return pl.pallas_call(
        finish_kernel,
        out_shape=(
            jax.ShapeDtypeStruct((1, prompts, fresh, model), BF),
            jax.ShapeDtypeStruct((tokens, 1), F32),
        ),
        in_specs=[smem()] + [vmem()] * 4,
        out_specs=(vmem(), vmem()),
        scratch_shapes=[pltpu.VMEM((back.shape[0] * CAP, model), F32)],
        compiler_params=pltpu.CompilerParams(vmem_limit_bytes=16 << 20),
        name="finish",
    )(routes, back, mixed, gates, weight)


def exchange(x, axis):
    return lax.all_to_all(x, axis, 0, 0, tiled=True)


def local(
    hidden,
    query,
    new_key,
    new_value,
    prompt_key,
    prompt_value,
    prompt_len,
    live_blocks,
    tail_key,
    tail_value,
    tail_len,
    tail_source,
    routes,
    router,
    ffn_gain,
    w_gate,
    w_up,
    w_down,
    score_weight,
):
    blk_count = lax.axis_size("blk")
    place = jnp.stack([lax.axis_index("blk"), lax.axis_index("expert")])
    prompts, fresh, model = query.shape[1:]
    tokens = prompts * fresh
    own = query.reshape(1, tokens, model)
    everyone = exchange(jnp.broadcast_to(own, (blk_count, tokens, model)), "blk")
    sent = attend(
        place,
        prompt_len,
        live_blocks,
        tail_len,
        tail_source,
        everyone.reshape(blk_count * tokens, model),
        prompt_key,
        prompt_value,
        tail_key[0],
        tail_value[0],
    )
    got = exchange(sent.reshape(blk_count, tokens, -1), "blk")
    mixed, outgoing, gates = combine(
        routes, got, query, new_key, new_value, hidden, router.T, ffn_gain[None]
    )
    arrived = exchange(outgoing, "expert")
    arrived = arrived.reshape(1, -1, model)
    rows = exchange(jnp.broadcast_to(arrived, (blk_count, *arrived.shape[1:])), "blk")
    partial = ffn(rows.reshape(-1, model), w_gate[0].T, w_up[0].T, w_down[0])
    partial = exchange(partial.reshape(rows.shape), "blk")
    summed = jnp.sum(partial.astype(F32), axis=0).astype(BF)
    back = exchange(summed.reshape(outgoing.shape), "expert")
    layer_out, score = finish(routes, back, mixed, gates, score_weight[None])
    return layer_out, score.reshape(1, prompts, fresh)


def solution(mesh):
    token = P("blk", "expert", None, None)
    cache = P("expert", "blk", None)
    columns = P("expert", None, "blk")
    placed = (
        token, token, token, token, cache, cache, P(), P(), token, token, P(), P(), token, P(), P(),
        columns, columns, cache, P(),
    )
    return jax.shard_map(
        local,
        mesh=mesh,
        in_specs=placed,
        out_specs=(token, P("blk", "expert", None)),
        check_vma=False,
    )
```

time: 393 us -> 152 us (0.39)
  waiting for transfers between devices: 159 us -> 26.1 us
  blocking collectives: 147 us -> 77.7 us
  matrix products: 25.3 us -> 0 us
  local copies, waits for them, and re-layouts: 31.3 us -> 7.43 us
  Pallas kernels: 0 us -> 19.2 us
  between operations: 14.2 us -> 0.85 us
  starting transfers between devices: 6.73 us -> 19.2 us
  other arithmetic: 9.11 us -> 0.55 us
    unnamed x5 -> x0, waiting for transfers between devices: 112 us -> none
    all_to_all x1 -> x3, blocking collectives: 11.7 us -> 77.7 us  [exchange(): return lax.all_to_all(x, axis, 0, 0, tiled=True)]
    pmax x1 -> x0, blocking collectives: 58.1 us -> none  [local(): top_score = lax.pmax(local_top, 'blk')]
    unnamed x1 -> x0, blocking collectives: 55.9 us -> none
    all_gather x1 -> x0, waiting for transfers between devices: 42.4 us -> none  [local(): column_rows = lax.all_gather(arrived[None], 'blk', axis=0, tiled=True)]
    dot_general x11 -> x0, matrix products: 25.3 us -> none  [the longest x1 6.3 us: local(): jnp.einsum('nlscf,lfd->nlscd', activation, w_down, preferred_element_type...]
    all_gather x1 -> x0, blocking collectives: 21.1 us -> none  [local(): everyone_q = lax.all_gather(query, 'blk', axis=0, tiled=True)]
    all_to_all x1 -> x3, waiting for transfers between devices: 5.07 us -> 26.1 us  [exchange(): return lax.all_to_all(x, axis, 0, 0, tiled=True)]
  transfers between devices with their start and end apart: 4 -> 3, of which waited for: 4 -> 3; matrix products, arithmetic and copies ran while one was open for 2% -> 0% of each run, Pallas kernels for 0% -> 0%
where the time goes in v2:
time: 152 us; the launch traced here: 151 us
  blocking collectives  77.7 us (51%)
  waiting for transfers between devices  26.1 us (17%)
  starting transfers between devices  19.2 us (13%)
  Pallas kernels  19.2 us (13%)
  local copies, waits for them, and re-layouts  7.43 us (5%)
    all_to_all x3, blocking collectives, exchange(): return lax.all_to_all(x, axis, 0, 0, tiled=True)  77.7 us
    all_to_all x3, waiting for transfers between devices, exchange(): return lax.all_to_all(x, axis, 0, 0, tiled=True)  26.1 us
    all_to_all x3, starting transfers between devices, exchange(): return lax.all_to_all(x, axis, 0, 0, tiled=True)  19.2 us
    pallas_call x1, Pallas kernels, attend(): pl.pallas_call(attend_kernel, out_shape=jax.ShapeDtypeStruct((rows, model...  9.52 us
    pallas_call x1, Pallas kernels, ffn(): pl.pallas_call(ffn_kernel, out_shape=jax.ShapeDtypeStruct((rows, model),...  6.39 us
    unnamed x40, local copies, waits for them, and re-layouts  4.63 us
  transfers between devices with their start and end apart: 3, of which 3 were waited for; matrix products, arithmetic and copies ran while one was open for 0% of the time, Pallas kernels for 0%

profile of v2, /device:TPU:1, one launch (start us, length us, event | category | flops | bytes accessed | tf_op | source)
XLA Modules:
  0.0 151.0 jit_solution(1036263015069636146)
XLA Ops:
  0.7 0.9 broadcast_in_dim.20
  1.6 0.9 broadcast_in_dim.21
  2.4 8.4 %all-to-all-start = ((bf16[16,8,2304]{2,1,0:T(8,128)(2,1)}), bf16[16,8,2304]{2,1,0:T(8,128)(2,1)S(1)}, u32[]{:S(2)}, u32[]{:S(2)}) async-start(bf16[16,8,2304]{2,1,0:T(8,128)(2,1)} %broadcast_in_dim.21), calls=%async_computation | async-start | bytes 1179648 | tf_op jit(solution)/shard_map/all_to_all | solution.py:344
  10.9 10.9 %all-to-all-done = bf16[16,8,2304]{2,1,0:T(8,128)(2,1)S(1)} async-done(((bf16[16,8,2304]{2,1,0:T(8,128)(2,1)}), bf16[16,8,2304]{2,1,0:T(8,128)(2,1)S(1)}, u32[]{:S(2)}, u32[]{:S(2)}) %all-to-all-start) | async-done | bytes 589856 | tf_op jit(solution)/shard_map/all_to_all | solution.py:344
  21.9 1.3 copy-done.4
  23.2 1.3 copy-done.5
  24.4 1.3 copy-done.6
  25.8 9.5 %attend.1 = bf16[128,2432]{1,0:T(8,128)(2,1)} custom-call(s32[2]{0:T(128)S(1)} %pad_add_fusion.place, s32[32]{0:T(128)S(1)} %copy-done.15, s32[32,64]{1,0:T(8,128)S(1)} %copy-done.12, s32[16,32]{1,0:T(8,128)S(1)} %copy-done.13, s32[16,32]{1,0:T(8,128)S(1)} %copy-done.14, bf16[128,2304]{1,0:T(8,128)(2,1)S(1)} %bitcast.18, bf16[4,64,2304]{2,1,0:T(8,128)(2,1)S(1)} %copy-done.3, ...), custom_call_target="tpu_custom_call" | custom-call | tf_op jit(solution)/shard_map/attend/pallas_call | solution.py:143
  35.3 3.6 %all-to-all-start.1 = ((bf16[16,8,2432]{2,1,0:T(8,128)(2,1)}), bf16[16,8,2432]{2,1,0:T(8,128)(2,1)S(1)}, u32[]{:S(2)}, u32[]{:S(2)}) async-start(bf16[16,8,2432]{2,1,0:T(8,128)(2,1)} %bitcast.5), calls=%async_computation.1 | async-start | bytes 1245184 | tf_op jit(solution)/shard_map/all_to_all | solution.py:344
  38.9 0.1 copy.25.routes
  39.0 9.7 %all-to-all-done.1.got_ref = bf16[16,8,2432]{2,1,0:T(8,128)(2,1)S(1)} async-done(((bf16[16,8,2432]{2,1,0:T(8,128)(2,1)}), bf16[16,8,2432]{2,1,0:T(8,128)(2,1)S(1)}, u32[]{:S(2)}, u32[]{:S(2)}) %all-to-all-start.1) | async-done | bytes 622624 | tf_op jit(solution)/shard_map/all_to_all | solution.py:344
  48.7 1.9 %combine.1 = (f32[8,2304]{1,0:T(8,128)S(1)}, bf16[8,4,2304]{2,1,0:T(4,128)(2,1)S(1)}, f32[8,128]{1,0:T(8,128)S(1)}) custom-call(s32[1,4,2,2]{3,2,1,0:T(2,128)S(1)} %copy.25.routes, bf16[16,8,2432]{2,1,0:T(8,128)(2,1)S(1)} %all-to-all-done.1.got_ref, bf16[1,4,2,2304]{3,2,1,0:T(2,128)(2,1)S(1)} %copy-done.7, bf16[1,4,2,2304]{3,2,1,0:T(2,128)(2,1)S(1)} %copy-done.9, ...), custom_call_target="tpu_custom_call" | custom-call | tf_op jit(solution)/shard_map/combine/pallas_call | solution.py:260
  50.6 13.3 %all_to_all.30 = bf16[8,4,2304]{2,1,0:T(4,128)(2,1)S(1)} all-to-all(bf16[8,4,2304]{2,1,0:T(4,128)(2,1)S(1)} %get-tuple-element.7), channel_id=1, replica_groups=mesh['blk'=16,'expert'=8] {'expert'}, dimensions={0} | all-to-all | bytes 294912 | tf_op jit(solution)/shard_map/all_to_all | solution.py:344
  64.0 0.2 broadcast_in_dim.24
  64.3 32.6 %all_to_all.31 = bf16[16,32,2304]{2,1,0:T(8,128)(2,1)S(1)} all-to-all(bf16[16,32,2304]{2,1,0:T(8,128)(2,1)S(1)} %broadcast_in_dim.24), channel_id=1, replica_groups=mesh['blk'=16,'expert'=8] {'blk'}, dimensions={0} | all-to-all | bytes 4718592 | tf_op jit(solution)/shard_map/all_to_all | solution.py:344
  96.8 6.4 %ffn.1 = bf16[512,2304]{1,0:T(8,128)(2,1)S(1)} custom-call(bf16[512,2304]{1,0:T(8,128)(2,1)S(1)} %bitcast.16, bf16[360,2304]{1,0:T(8,128)(2,1)S(1)} %bitcast.19, bf16[360,2304]{1,0:T(8,128)(2,1)S(1)} %bitcast.20, bf16[360,2304]{1,0:T(8,128)(2,1)S(1)} %bitcast.21), custom_call_target="tpu_custom_call" | custom-call | tf_op jit(solution)/shard_map/ffn/pallas_call | solution.py:289
  103.2 31.8 %all_to_all.32 = bf16[16,32,2304]{2,1,0:T(8,128)(2,1)S(1)} all-to-all(bf16[16,32,2304]{2,1,0:T(8,128)(2,1)S(1)} %bitcast.17), channel_id=1, replica_groups=mesh['blk'=16,'expert'=8] {'blk'}, dimensions={0} | all-to-all | bytes 4718592 | tf_op jit(solution)/shard_map/all_to_all | solution.py:344
  135.1 0.4 reduce_sum.12
  135.4 0.7 reshape.30
  136.1 7.1 %all-to-all-start.5 = ((bf16[8,4,2304]{2,1,0:T(4,128)(2,1)}), bf16[8,4,2304]{2,1,0:T(4,128)(2,1)S(1)}, u32[]{:S(2)}, u32[]{:S(2)}) async-start(bf16[8,4,2304]{2,1,0:T(4,128)(2,1)} %reshape.30), calls=%async_computation.5 | async-start | bytes 294912 | tf_op jit(solution)/shard_map/all_to_all | solution.py:344
  143.3 5.4 %all-to-all-done.5.back_ref = bf16[8,4,2304]{2,1,0:T(4,128)(2,1)S(1)} async-done(((bf16[8,4,2304]{2,1,0:T(4,128)(2,1)}), bf16[8,4,2304]{2,1,0:T(4,128)(2,1)S(1)}, u32[]{:S(2)}, u32[]{:S(2)}) %all-to-all-start.5) | async-done | bytes 147488 | tf_op jit(solution)/shard_map/all_to_all | solution.py:344
  148.7 1.4 finish.1
  150.1 0.1 reduce.1
  150.3 0.7 copy.26
  (40 shorter events, 0.3 us)
Async XLA Ops:
  0.6 21.2 %copy-start.3 = (bf16[4,64,2304]{2,1,0:T(8,128)(2,1)S(1)}, bf16[4,64,2304]{2,1,0:T(8,128)(2,1)}, u32[]{:S(2)}) copy-start(bf16[4,64,2304]{2,1,0:T(8,128)(2,1)} %k_ref.2) | copy-start | bytes 3538948
  0.6 21.2 %copy-start.15 = (s32[32]{0:T(128)S(1)}, s32[32]{0:T(128)}, u32[]{:S(2)}) copy-start(s32[32]{0:T(128)} %lengths.1) | copy-start | bytes 388
  0.7 21.2 %copy-start.12 = (s32[32,64]{1,0:T(8,128)S(1)}, s32[32,64]{1,0:T(8,128)}, u32[]{:S(2)}) copy-start(s32[32,64]{1,0:T(8,128)} %live.1) | copy-start | bytes 24580
  0.7 21.2 %copy-start.13 = (s32[16,32]{1,0:T(8,128)S(1)}, s32[16,32]{1,0:T(8,128)}, u32[]{:S(2)}) copy-start(s32[16,32]{1,0:T(8,128)} %tail_len.1) | copy-start | bytes 6148
  0.7 21.2 %copy-start.14 = (s32[16,32]{1,0:T(8,128)S(1)}, s32[16,32]{1,0:T(8,128)}, u32[]{:S(2)}) copy-start(s32[16,32]{1,0:T(8,128)} %source.1) | copy-start | bytes 6148
  2.4 19.4 %all-to-all-start = ((bf16[16,8,2304]{2,1,0:T(8,128)(2,1)}), bf16[16,8,2304]{2,1,0:T(8,128)(2,1)S(1)}, u32[]{:S(2)}, u32[]{:S(2)}) async-start(bf16[16,8,2304]{2,1,0:T(8,128)(2,1)} %broadcast_in_dim.21), calls=%async_computation | async-start | bytes 1179648 | tf_op jit(solution)/shard_map/all_to_all | solution.py:344
  21.9 1.3 copy-start.4
  23.2 1.3 copy-start.5
  24.4 1.3 copy-start.6
  25.7 13.2 %copy-start.18 = (s32[1,4,2,2]{1,3,2,0:T(2,128)S(1)}, s32[1,4,2,2]{1,3,2,0:T(2,128)}, u32[]{:S(2)}) copy-start(s32[1,4,2,2]{1,3,2,0:T(2,128)} %param.31) | copy-start | bytes 196
  25.7 13.3 %copy-start.16 = (f32[2304]{0:T(1024)S(1)}, f32[2304]{0:T(1024)}, u32[]{:S(2)}) copy-start(f32[2304]{0:T(1024)} %param.33) | copy-start | bytes 27652
  25.7 23.0 %copy-start.7 = (bf16[1,4,2,2304]{3,2,1,0:T(2,128)(2,1)S(1)}, bf16[1,4,2,2304]{3,2,1,0:T(2,128)(2,1)}, u32[]{:S(2)}) copy-start(bf16[1,4,2,2304]{3,2,1,0:T(2,128)(2,1)} %q_ref.1) | copy-start | bytes 110596
  25.7 23.0 %copy-start.8 = (f32[2304,8]{0,1:T(8,128)S(1)}, f32[2304,8]{0,1:T(8,128)}, u32[]{:S(2)}) copy-start(f32[2304,8]{0,1:T(8,128)} %param.32) | copy-start | bytes 221188
  25.7 23.0 %copy-start.9 = (bf16[1,4,2,2304]{3,2,1,0:T(2,128)(2,1)S(1)}, bf16[1,4,2,2304]{3,2,1,0:T(2,128)(2,1)}, u32[]{:S(2)}) copy-start(bf16[1,4,2,2304]{3,2,1,0:T(2,128)(2,1)} %k_ref.3) | copy-start | bytes 110596
  25.7 23.0 %copy-start.10 = (bf16[1,4,2,2304]{3,2,1,0:T(2,128)(2,1)S(1)}, bf16[1,4,2,2304]{3,2,1,0:T(2,128)(2,1)}, u32[]{:S(2)}) copy-start(bf16[1,4,2,2304]{3,2,1,0:T(2,128)(2,1)} %v_ref.3) | copy-start | bytes 110596
  25.7 23.0 %copy-start.11 = (bf16[1,4,2,2304]{3,2,1,0:T(2,128)(2,1)S(1)}, bf16[1,4,2,2304]{3,2,1,0:T(2,128)(2,1)}, u32[]{:S(2)}) copy-start(bf16[1,4,2,2304]{3,2,1,0:T(2,128)(2,1)} %h_ref.1) | copy-start | bytes 110596
  35.3 13.4 %all-to-all-start.1 = ((bf16[16,8,2432]{2,1,0:T(8,128)(2,1)}), bf16[16,8,2432]{2,1,0:T(8,128)(2,1)S(1)}, u32[]{:S(2)}, u32[]{:S(2)}) async-start(bf16[16,8,2432]{2,1,0:T(8,128)(2,1)} %bitcast.5), calls=%async_computation.1 | async-start | bytes 1245184 | tf_op jit(solution)/shard_map/all_to_all | solution.py:344
  64.0 32.8 %copy-start.2 = (bf16[1,360,2304]{2,1,0:T(8,128)(2,1)S(1)}, bf16[1,360,2304]{2,1,0:T(8,128)(2,1)}, u32[]{:S(2)}) copy-start(bf16[1,360,2304]{2,1,0:T(8,128)(2,1)} %param.36) | copy-start | bytes 4976644
  64.2 32.6 %copy-start = (bf16[1,2304,360]{1,2,0:T(8,128)(2,1)S(1)}, bf16[1,2304,360]{1,2,0:T(8,128)(2,1)}, u32[]{:S(2)}) copy-start(bf16[1,2304,360]{1,2,0:T(8,128)(2,1)} %param.34) | copy-start | bytes 4976644
  64.2 32.6 %copy-start.1 = (bf16[1,2304,360]{1,2,0:T(8,128)(2,1)S(1)}, bf16[1,2304,360]{1,2,0:T(8,128)(2,1)}, u32[]{:S(2)}) copy-start(bf16[1,2304,360]{1,2,0:T(8,128)(2,1)} %param.35) | copy-start | bytes 4976644
  135.1 8.2 %copy-start.17 = (f32[2304]{0:T(1024)S(1)}, f32[2304]{0:T(1024)}, u32[]{:S(2)}) copy-start(f32[2304]{0:T(1024)} %param.37) | copy-start | bytes 27652
  136.1 12.6 %all-to-all-start.5 = ((bf16[8,4,2304]{2,1,0:T(4,128)(2,1)}), bf16[8,4,2304]{2,1,0:T(4,128)(2,1)S(1)}, u32[]{:S(2)}, u32[]{:S(2)}) async-start(bf16[8,4,2304]{2,1,0:T(4,128)(2,1)} %reshape.30), calls=%async_computation.5 | async-start | bytes 294912 | tf_op jit(solution)/shard_map/all_to_all | solution.py:344

commit v3 on v2

v3 whole, which is shorter than its diff:
```python
import jax
import jax.numpy as jnp
from jax import lax
from jax.experimental import pallas as pl
from jax.experimental.pallas import tpu as pltpu
from jax.sharding import PartitionSpec as P

HDIM = 64
TOP = 2
KVB = 16
CAP = 4
LANES = 128
ROOM = 61 << 20

BF = jnp.bfloat16
F32 = jnp.float32
HIDE = -1e30
FLOOR = -1e4
NT = (((1,), (1,)), ((), ()))


def vmem():
    return pl.BlockSpec(memory_space=pltpu.VMEM)


def smem():
    return pl.BlockSpec(memory_space=pltpu.SMEM)


def iota(shape, dim):
    return lax.broadcasted_iota(jnp.int32, shape, dim)


def dot(a, b, dims=(((1,), (0,)), ((), ()))):
    return lax.dot_general(a, b, dims, preferred_element_type=F32)


def share_kernel(q_ref, out_ref, flat):
    prompts, fresh = q_ref.shape[1], q_ref.shape[2]
    for p in range(prompts):
        flat[fresh * p : fresh * (p + 1), :] = q_ref[0, p].astype(F32) * 0.125
    rows = flat[...].astype(BF)
    for m in range(out_ref.shape[0]):
        out_ref[m] = rows


def share(query, samples):
    _, prompts, fresh, model = query.shape
    tokens = prompts * fresh
    return pl.pallas_call(
        share_kernel,
        out_shape=jax.ShapeDtypeStruct((samples, tokens, model), BF),
        in_specs=[vmem()],
        out_specs=vmem(),
        scratch_shapes=[pltpu.VMEM((tokens, model), F32)],
        compiler_params=pltpu.CompilerParams(vmem_limit_bytes=16 << 20),
        name="share",
    )(query)


def attend_kernel(
    lengths, live, tail_len, source, q_ref, k_ref, tk_hbm, v_hbm, tv_hbm, out_ref,
    tk_buf, v_buf, tv_buf, rows_in, rows_out, stats_in, score_buf, weight_buf, sems,
):
    prompts, span, model = k_ref.shape
    rows = q_ref.shape[0]
    fresh = 2
    group = prompts * fresh
    samples = rows // group
    each = fresh * samples
    heads = model // HDIM
    pairs = model // LANES
    blk, exp = lax.axis_index("blk"), lax.axis_index("expert")
    moves = ((tk_hbm, tk_buf), (v_hbm, v_buf), (tv_hbm, tv_buf))

    def copy(p, i):
        src, dst = moves[i]
        return pltpu.make_async_copy(src.at[p], dst.at[p], sems.at[p, i])

    for p in range(prompts):
        for i in range(len(moves)):
            copy(p, i).start()
    for i in range(pairs):
        rows_in[i] = q_ref[:, i * LANES : (i + 1) * LANES].astype(F32)
    lane = iota((each, LANES), 1)
    sample = iota((each, LANES), 0) % samples

    @pl.loop(0, prompts)
    def _(p):
        at = exp * prompts + p
        kept = jnp.zeros((each, LANES), jnp.int32)
        for b in range(span // KVB):
            kept = jnp.where(lane // KVB == b, live[at, blk * (span // KVB) + b], kept)
        left = jnp.minimum(lengths[at] - blk * span, span)
        prompt_ok = jnp.where(lane < left, jnp.where(kept > 0, 1, 0), 0)
        who = source[blk, at]
        held = tail_len[who, at]
        tail_ok = jnp.where(lane >= span, jnp.where(lane - span < held, 1, 0), 0)
        use = prompt_ok + jnp.where(sample == who, tail_ok, 0)
        hide = jnp.where(use > 0, 0.0, HIDE)
        hide = jnp.concatenate([hide, hide], axis=0)
        copy(p, 0).wait()
        tops = jnp.zeros((each, LANES), F32)
        sums = jnp.zeros((each, LANES), F32)
        for i in range(pairs):
            cut = slice(i * LANES, (i + 1) * LANES)
            q = jnp.concatenate(
                [rows_in[i, pl.ds(fresh * p + t, samples, stride=group), :] for t in range(fresh)],
                axis=0,
            )
            q = jnp.concatenate([jnp.where(lane < HDIM, q, 0.0), jnp.where(lane < HDIM, 0.0, q)], axis=0)
            score_buf[i] = dot(
                q.astype(BF), jnp.concatenate([k_ref[p, :, cut], tk_buf[p, :, cut]], axis=0), NT
            ) + hide
        for i in range(pairs):
            scores = score_buf[i]
            top = jnp.maximum(jnp.max(scores, axis=1, keepdims=True), FLOOR)
            top = top.astype(BF).astype(F32)
            weight = jnp.exp(scores - top)
            total = jnp.sum(weight, axis=1, keepdims=True)
            weight_buf[i] = weight.astype(BF)
            for h in range(2):
                part = slice(h * each, (h + 1) * each)
                tops = jnp.where(lane == 2 * i + h, top[part], tops)
                sums = jnp.where(lane == heads + 2 * i + h, total[part], sums)
        copy(p, 1).wait()
        copy(p, 2).wait()
        for i in range(pairs):
            cut = slice(i * LANES, (i + 1) * LANES)
            val = jnp.concatenate([v_buf[p, :, cut], tv_buf[p, :, cut]], axis=0)
            both = dot(weight_buf[i], val)
            mixed = jnp.where(lane < HDIM, both[:each], both[each:])
            for t in range(fresh):
                rows_out[i, pl.ds(fresh * p + t, samples, stride=group), :] = mixed[
                    t * samples : (t + 1) * samples
                ]
        high = sums.astype(BF).astype(F32)
        stats = tops + high + pltpu.roll(sums - high, heads, 1)
        for t in range(fresh):
            stats_in[pl.ds(fresh * p + t, samples, stride=group), :] = stats[
                t * samples : (t + 1) * samples
            ]

    for i in range(pairs):
        out_ref[:, i * LANES : (i + 1) * LANES] = rows_out[i].astype(BF)
    out_ref[:, model:] = stats_in[...].astype(BF)


def attend(lengths, live, tail_len, source, everyone, key, tail_key, value, tail_value):
    rows, model = everyone.shape
    prompts, span, _ = key.shape
    pairs = model // LANES
    cache = pltpu.VMEM((prompts, span, model), BF)
    where = pl.BlockSpec(memory_space=pl.ANY)
    return pl.pallas_call(
        attend_kernel,
        out_shape=jax.ShapeDtypeStruct((rows, model + LANES), BF),
        in_specs=[smem()] * 4 + [vmem()] * 2 + [where] * 3,
        out_specs=vmem(),
        scratch_shapes=[
            cache,
            cache,
            cache,
            pltpu.VMEM((pairs, rows, LANES), F32),
            pltpu.VMEM((pairs, rows, LANES), F32),
            pltpu.VMEM((rows, LANES), F32),
            pltpu.VMEM((pairs, 2 * rows // prompts, LANES), F32),
            pltpu.VMEM((pairs, 2 * rows // prompts, LANES), BF),
            pltpu.SemaphoreType.DMA((prompts, 3)),
        ],
        compiler_params=pltpu.CompilerParams(vmem_limit_bytes=ROOM),
        name="attend",
    )(lengths, live, tail_len, source, everyone, key, tail_key, value, tail_value)


def row_of(expert, core):
    away = jnp.where(expert % 2 == core, 0, CAP)
    return expert // 2 * (2 * CAP) + away


def combine_kernel(
    routes, got_ref, q_ref, k_ref, v_ref, h_ref, router_ref, gain_ref,
    mixed_ref, rows_ref, gate_ref, q8, k0, k1, v0, v1, spread,
):
    parts, tokens, wide = got_ref.shape
    model = wide - LANES
    heads = model // HDIM
    prompts, fresh = q_ref.shape[1], q_ref.shape[2]
    experts = router_ref.shape[0]
    for p in range(prompts):
        at = slice(fresh * p, fresh * (p + 1))
        q8[at, :] = q_ref[0, p].astype(F32)
        mixed_ref[at, :] = h_ref[0, p].astype(F32)
        key, val = k_ref[0, p].astype(F32), v_ref[0, p].astype(F32)
        k0[at, :] = jnp.broadcast_to(key[0:1], (fresh, model))
        k1[at, :] = jnp.broadcast_to(key[1:2], (fresh, model))
        v0[at, :] = jnp.broadcast_to(val[0:1], (fresh, model))
        v1[at, :] = jnp.broadcast_to(val[1:2], (fresh, model))
    spread[...] = jnp.where(
        iota((LANES, model), 1) // HDIM == iota((LANES, model), 0), 1.0, 0.0
    ).astype(BF)
    product = jnp.concatenate([q8[...] * k0[...], q8[...] * k1[...]], axis=0)
    high = product.astype(BF)
    low = (product - high.astype(F32)).astype(BF)
    own = (dot(high, spread[...], NT) + dot(low, spread[...], NT)) * 0.125
    lane = iota((tokens, LANES), 1)
    sub = iota((tokens, LANES), 0)
    s0 = own[:tokens]
    s1 = jnp.where(sub % fresh == 1, own[tokens:], HIDE)
    top = jnp.maximum(s0, s1)
    tops, sums = [], []
    for j in range(parts):
        stat = got_ref[j, :, model:].astype(F32)
        tops.append(jnp.where(lane < heads, stat, 0.0))
        total = pltpu.roll(stat, LANES - heads, 1) + pltpu.roll(stat, LANES - 2 * heads, 1)
        sums.append(jnp.where(lane < heads, total, 1.0))
        top = jnp.maximum(top, tops[-1])
    w0, w1 = jnp.exp(s0 - top), jnp.exp(s1 - top)
    scale = [jnp.exp(t - top) for t in tops]
    total = w0 + w1
    for c, l in zip(scale, sums):
        total = total + c * l
    inverse = 1.0 / total
    share = jnp.concatenate([c * inverse for c in scale] + [w0 * inverse, w1 * inverse], axis=0)
    share_high = share.astype(BF)
    share_low = (share - share_high.astype(F32)).astype(BF)
    square = jnp.zeros((tokens, LANES), F32)
    chunk = 2 * LANES
    for c in range(model // chunk):
        cut = slice(c * chunk, (c + 1) * chunk)
        each = dot(share_high, spread[:, cut]) + dot(share_low, spread[:, cut])
        here = mixed_ref[:, cut]
        for j in range(parts):
            here = here + each[j * tokens : (j + 1) * tokens] * got_ref[j, :, cut].astype(F32)
        here = here + each[parts * tokens : (parts + 1) * tokens] * v0[:, cut]
        here = here + each[(parts + 1) * tokens :] * v1[:, cut]
        mixed_ref[:, cut] = here
        for i in range(chunk // LANES):
            part = here[:, i * LANES : (i + 1) * LANES]
            square = square + part * part
    mean = jnp.sum(square, axis=1, keepdims=True) / model
    scale = lax.rsqrt(mean + 1e-05)
    normed = jnp.concatenate(
        [
            mixed_ref[:, i * LANES : (i + 1) * LANES] * scale * gain_ref[i : i + 1, :]
            for i in range(model // LANES)
        ],
        axis=1,
    )
    normed = normed.astype(BF).astype(F32)
    logits = [jnp.sum(normed * router_ref[e : e + 1, :], axis=1, keepdims=True) for e in range(experts)]
    token = iota((tokens, 1), 0)
    first = jnp.zeros((tokens, 1), jnp.int32)
    second = jnp.zeros((tokens, 1), jnp.int32)
    slots = experts * CAP
    core = lax.axis_index("expert") % 2
    row = iota((slots, tokens), 0)
    column = iota((slots, tokens), 1)
    pick = jnp.zeros((slots, tokens), F32)
    seen = jnp.zeros((slots, tokens), jnp.int32)
    for i in range(tokens):
        pair = [routes[i % fresh, r, i // fresh] for r in range(TOP)]
        first = jnp.where(token == i, pair[0], first)
        second = jnp.where(token == i, pair[1], second)
        for expert in pair:
            match = row // CAP * CAP == row_of(expert, core)
            hit = jnp.where(match, jnp.where(column == i, jnp.where(row % CAP == seen, 1.0, 0.0), 0.0), 0.0)
            pick = pick + hit
            seen = seen + jnp.where(match, 1, 0)
    logit0 = jnp.zeros((tokens, 1), F32)
    logit1 = jnp.zeros((tokens, 1), F32)
    for e in range(experts):
        logit0 = jnp.where(first == e, logits[e], logit0)
        logit1 = jnp.where(second == e, logits[e], logit1)
    gate0 = 1.0 / (1.0 + jnp.exp(logit1 - logit0))
    gate1 = 1.0 / (1.0 + jnp.exp(logit0 - logit1))
    gate_ref[...] = jnp.where(lane == 0, gate0, jnp.where(lane == 1, gate1, 0.0))
    rows_ref[...] = dot(pick, normed).astype(BF)


def combine(routes, got, query, new_key, new_value, hidden, router, gain):
    parts, tokens, wide = got.shape
    model = wide - LANES
    experts = router.shape[0]
    return pl.pallas_call(
        combine_kernel,
        out_shape=(
            jax.ShapeDtypeStruct((tokens, model), F32),
            jax.ShapeDtypeStruct((experts * CAP, model), BF),
            jax.ShapeDtypeStruct((tokens, LANES), F32),
        ),
        in_specs=[smem()] + [vmem()] * 7,
        out_specs=(vmem(), vmem(), vmem()),
        scratch_shapes=[pltpu.VMEM((tokens, model), F32)] * 5 + [pltpu.VMEM((LANES, model), BF)],
        compiler_params=pltpu.CompilerParams(vmem_limit_bytes=16 << 20),
        name="combine",
    )(routes, got, query, new_key, new_value, hidden, router, gain)


def ffn_kernel(x_ref, gate_ref, up_ref, down_ref, out_ref):
    x = x_ref[...]
    gated = dot(x, gate_ref[...], NT)
    upward = dot(x, up_ref[...], NT)
    activation = (gated / (1.0 + jnp.exp(-gated)) * upward).astype(BF)
    out_ref[...] = dot(activation, down_ref[...]).astype(BF)


def ffn(x, w_gate, w_up, w_down):
    return pl.pallas_call(
        ffn_kernel,
        out_shape=jax.ShapeDtypeStruct(x.shape, BF),
        in_specs=[vmem()] * 4,
        out_specs=vmem(),
        compiler_params=pltpu.CompilerParams(vmem_limit_bytes=16 << 20),
        cost_estimate=pl.CostEstimate(
            flops=6 * x.size * w_gate.shape[0],
            bytes_accessed=2 * (2 * x.size + 3 * w_gate.size),
            transcendentals=x.shape[0] * w_gate.shape[0],
        ),
        name="ffn",
    )(x, w_gate, w_up, w_down)


def finish_kernel(routes, mine_ref, back_ref, mixed_ref, gate_ref, weight_ref, out_ref, score_ref):
    slots, model = mine_ref.shape
    tokens = mixed_ref.shape[0]
    prompts, fresh = out_ref.shape[1], out_ref.shape[2]
    near = iota((slots, model), 0) % (2 * CAP) < CAP
    every = jnp.where(near, mine_ref[...].astype(F32), back_ref[...].astype(F32))
    core = lax.axis_index("expert") % 2
    row = iota((tokens, slots), 0)
    column = iota((tokens, slots), 1)
    seen = jnp.zeros((tokens, slots), jnp.int32)
    picks = [jnp.zeros((tokens, slots), F32) for _ in range(TOP)]
    for i in range(tokens):
        for r in range(TOP):
            match = column // CAP * CAP == row_of(routes[i % fresh, r, i // fresh], core)
            hit = jnp.where(match, jnp.where(row == i, jnp.where(column % CAP == seen, 1.0, 0.0), 0.0), 0.0)
            picks[r] = picks[r] + hit
            seen = seen + jnp.where(match, 1, 0)
    total = mixed_ref[...]
    for r in range(TOP):
        total = total + gate_ref[:, r : r + 1] * dot(picks[r], every)
    done = total.astype(BF)
    kept = done.astype(F32)
    partial = jnp.zeros((tokens, LANES), F32)
    for i in range(model // LANES):
        partial = partial + kept[:, i * LANES : (i + 1) * LANES] * weight_ref[i : i + 1, :]
    score = jnp.sum(partial, axis=1, keepdims=True)
    token = iota((tokens, LANES), 0)
    score = jnp.where(token // fresh == iota((tokens, LANES), 1), score, 0.0)
    for t in range(fresh):
        line = jnp.sum(jnp.where(token % fresh == t, score, 0.0), axis=0, keepdims=True)
        score_ref[t : t + 1, :] = line[:, :prompts]
    for p in range(prompts):
        out_ref[0, p] = done[fresh * p : fresh * (p + 1)]


def finish(routes, mine, back, mixed, gates, weight):
    tokens, model = mixed.shape
    fresh, _, prompts = routes.shape
    return pl.pallas_call(
        finish_kernel,
        out_shape=(
            jax.ShapeDtypeStruct((1, prompts, fresh, model), BF),
            jax.ShapeDtypeStruct((fresh, prompts), F32),
        ),
        in_specs=[smem()] + [vmem()] * 5,
        out_specs=(vmem(), vmem()),
        compiler_params=pltpu.CompilerParams(vmem_limit_bytes=16 << 20),
        name="finish",
    )(routes, mine, back, mixed, gates, weight)


def exchange(x, axis):
    return lax.all_to_all(x, axis, 0, 0, tiled=True)


def local(
    hidden,
    query,
    new_key,
    new_value,
    prompt_key,
    prompt_value,
    prompt_len,
    live_blocks,
    tail_key,
    tail_value,
    tail_len,
    tail_source,
    routes,
    router,
    ffn_gain,
    w_gate,
    w_up,
    w_down,
    score_weight,
):
    blk_count = lax.axis_size("blk")
    prompts, fresh, model = query.shape[1:]
    tokens = prompts * fresh
    everyone = exchange(share(query, blk_count), "blk")
    chosen = routes[0].transpose(1, 2, 0)
    sent = attend(
        prompt_len,
        live_blocks,
        tail_len,
        tail_source,
        everyone.reshape(blk_count * tokens, model),
        prompt_key,
        tail_key[0],
        prompt_value,
        tail_value[0],
    )
    got = exchange(sent.reshape(blk_count, tokens, -1), "blk")
    mixed, outgoing, gates = combine(
        chosen, got, query, new_key, new_value, hidden, router.T, ffn_gain.reshape(-1, LANES)
    )
    exp_count = lax.axis_size("expert")
    both = ("blk", "expert")
    side = 4
    planes = exp_count // 2
    device = lambda x, z, y, c: (x * side + z) * exp_count + y * 2 + c
    swap = [(i, i ^ 1) for i in range(exp_count)]
    lines = [
        [device(o, k, y, 0) if c == 0 else device(k, o, y, 1) for k in range(side) for y in range(planes)]
        for c in range(2)
        for o in range(side)
    ]

    def shift(step):
        moves = []
        for x in range(side):
            for z in range(side):
                for y in range(planes):
                    moves.append((device(x, z, y, 0), device((x + step) % side, z, y, 0)))
                    moves.append((device(x, z, y, 1), device(x, (z + step) % side, y, 1)))
        return moves

    wide = (planes, 2 * CAP, model)
    near = jnp.arange(2 * CAP)[None, :, None] < CAP
    rows = jnp.where(
        near, outgoing.reshape(wide), lax.ppermute(outgoing, "expert", swap).reshape(wide)
    )
    rows = jnp.broadcast_to(rows[None], (side, *wide)).reshape(-1, 2 * CAP, model)
    rows = lax.all_to_all(rows, both, 0, 0, tiled=True, axis_index_groups=lines)
    rows = rows.reshape(-1, model)
    weights = (w_gate[0].T, w_up[0].T, w_down[0])
    order = (2, 1, 3)
    arrivals = [lax.ppermute(rows, both, shift(s)) for s in order]
    total = ffn(rows, *weights)
    parts = [total]
    for s, arrived in zip(order, arrivals):
        arrived, parts[0] = lax.optimization_barrier((arrived, parts[0]))
        parts.append(lax.ppermute(ffn(arrived, *weights), both, shift(-s)))
    total = sum(part.astype(F32) for part in parts).astype(BF)
    total = lax.all_to_all(
        total.reshape(-1, 2 * CAP, model), both, 0, 0, tiled=True, axis_index_groups=lines
    )
    total = total.reshape(side, -1, model)
    mine = jnp.sum(total.astype(F32), axis=0).astype(BF)
    back = lax.ppermute(mine, "expert", swap)
    layer_out, score = finish(chosen, mine, back, mixed, gates, score_weight.reshape(-1, LANES))
    return layer_out, score.T[None]


def solution(mesh):
    token = P("blk", "expert", None, None)
    cache = P("expert", "blk", None)
    columns = P("expert", None, "blk")
    placed = (
        token, token, token, token, cache, cache, P(), P(), token, token, P(), P(), token, P(), P(),
        columns, columns, cache, P(),
    )
    return jax.shard_map(
        local,
        mesh=mesh,
        in_specs=placed,
        out_specs=(token, P("blk", "expert", None)),
        check_vma=False,
    )
```

time: 152 us -> 117 us (0.77)
  blocking collectives: 77.7 us -> 59.8 us
  local copies, waits for them, and re-layouts: 7.43 us -> 0.87 us
  waiting for transfers between devices: 26.1 us -> 20.2 us
  starting transfers between devices: 19.2 us -> 16.8 us
  Pallas kernels: 19.2 us -> 17.4 us
    all_to_all x3 -> x2, blocking collectives: 77.7 us -> 32.9 us  [exchange(): return lax.all_to_all(x, axis, 0, 0, tiled=True)]
    all_to_all x0 -> x2, blocking collectives: none -> 26.9 us  [the longest x1 14.4 us: local(): rows = lax.all_to_all(rows, both, 0, 0, tiled=True, axis_index_groups=lines)]
    all_to_all x3 -> x0, waiting for transfers between devices: 26.1 us -> none  [exchange(): return lax.all_to_all(x, axis, 0, 0, tiled=True)]
    ppermute x0 -> x8, waiting for transfers between devices: none -> 20.2 us  [the longest x3 9.1 us: local(): parts.append(lax.ppermute(ffn(arrived, *weights), both, shift(-s)))]
    all_to_all x3 -> x0, starting transfers between devices: 19.2 us -> none  [exchange(): return lax.all_to_all(x, axis, 0, 0, tiled=True)]
    ppermute x0 -> x8, starting transfers between devices: none -> 16.8 us  [the longest x1 7.02 us: local(): back = lax.ppermute(mine, 'expert', swap)]
    unnamed x40 -> x24, local copies, waits for them, and re-layouts: 4.63 us -> 0.83 us
    broadcast_in_dim x6 -> x1, local copies, waits for them, and re-layouts: 2.01 us -> 0.04 us  [local(): jnp.broadcast_to(rows[None], (side, *wide)).reshape(-1, 2 * CAP, model)]
  transfers between devices with their start and end apart: 3 -> 8, of which waited for: 3 -> 7; matrix products, arithmetic and copies ran while one was open for 0% -> 0% of each run, Pallas kernels for 0% -> 5%
where the time goes in v3:
time: 117 us; the launch traced here: 116 us
  blocking collectives  59.8 us (51%)
  waiting for transfers between devices  20.2 us (17%)
  Pallas kernels  17.4 us (15%)
  starting transfers between devices  16.8 us (14%)
    all_to_all x2, blocking collectives, exchange(): return lax.all_to_all(x, axis, 0, 0, tiled=True)  32.9 us
    all_to_all x1, blocking collectives, local(): rows = lax.all_to_all(rows, both, 0, 0, tiled=True, axis_index_groups=lines)  14.4 us
    all_to_all x1, blocking collectives, local(): lax.all_to_all(total.reshape(-1, 2 * CAP, model), both, 0, 0, tiled=True,...  12.5 us
    ppermute x3, waiting for transfers between devices, local(): parts.append(lax.ppermute(ffn(arrived, *weights), both, shift(-s)))  9.1 us
    ppermute x3, waiting for transfers between devices, local(): arrivals = [lax.ppermute(rows, both, shift(s)) for s in order]  9.05 us
    pallas_call x1, Pallas kernels, attend(): pl.pallas_call(attend_kernel, out_shape=jax.ShapeDtypeStruct((rows, model...  7.6 us
    ppermute x1, starting transfers between devices, local(): back = lax.ppermute(mine, 'expert', swap)  7.02 us
    pallas_call x4, Pallas kernels, ffn(): pl.pallas_call(ffn_kernel, out_shape=jax.ShapeDtypeStruct(x.shape, BF), i...  6.35 us
  transfers between devices with their start and end apart: 8, of which 7 were waited for; matrix products, arithmetic and copies ran while one was open for 0% of the time, Pallas kernels for 5%

profile of v3, /device:TPU:1, one launch (start us, length us, event | category | flops | bytes accessed | tf_op | source)
XLA Modules:
  0.0 116.3 jit_solution(2854288752511689936)
XLA Ops:
  1.5 19.3 %all_to_all.20 = bf16[16,8,2304]{2,1,0:T(8,128)(2,1)} all-to-all(bf16[16,8,2304]{2,1,0:T(8,128)(2,1)S(1)} %share.1), channel_id=1, replica_groups=mesh['blk'=16,'expert'=8] {'blk'}, dimensions={0} | all-to-all | bytes 1179648 | tf_op jit(solution)/shard_map/all_to_all | solution.py:376
  20.8 7.6 %attend.1 = bf16[128,2432]{1,0:T(8,128)(2,1)} custom-call(s32[32]{0:T(128)} %lengths.1, s32[32,64]{1,0:T(8,128)} %live.1, s32[16,32]{1,0:T(8,128)} %tail_len.1, s32[16,32]{1,0:T(8,128)} %source.1, bf16[128,2304]{1,0:T(8,128)(2,1)} %bitcast.53, bf16[4,64,2304]{2,1,0:T(8,128)(2,1)} %k_ref.2, bf16[4,64,2304]{2,1,0:T(8,128)(2,1)} %bitcast.56, ...), custom_call_target="tpu_custom_call" | custom-call | tf_op jit(solution)/shard_map/attend/pallas_call | solution.py:155
  28.5 13.6 %all_to_all.21.got_ref = bf16[16,8,2432]{2,1,0:T(8,128)(2,1)S(1)} all-to-all(bf16[16,8,2432]{2,1,0:T(8,128)(2,1)} %bitcast.52), channel_id=1, replica_groups=mesh['blk'=16,'expert'=8] {'blk'}, dimensions={0} | all-to-all | bytes 1245184 | tf_op jit(solution)/shard_map/all_to_all | solution.py:376
  42.1 1.9 %combine.1 = (f32[8,2304]{1,0:T(8,128)S(1)}, bf16[32,2304]{1,0:T(8,128)(2,1)S(1)}, f32[8,128]{1,0:T(8,128)S(1)}) custom-call(s32[2,2,4]{2,1,0:T(2,128)S(1)} %bitcast.50, bf16[16,8,2432]{2,1,0:T(8,128)(2,1)S(1)} %all_to_all.21.got_ref, bf16[1,4,2,2304]{3,2,1,0:T(2,128)(2,1)S(1)} %copy-done.4, bf16[1,4,2,2304]{3,2,1,0:T(2,128)(2,1)S(1)} %copy-done.6, ...), custom_call_target="tpu_custom_call" | custom-call | tf_op jit(solution)/shard_map/combine/pallas_call | solution.py:285
  44.0 3.6 %collective-permute-start = (bf16[32,2304]{1,0:T(8,128)(2,1)S(1)}, bf16[32,2304]{1,0:T(8,128)(2,1)S(1)}, u32[]{:S(2)}, u32[]{:S(2)}) collective-permute-start(bf16[32,2304]{1,0:T(8,128)(2,1)S(1)} %get-tuple-element.13), channel_id=1, source_target_pairs={{0,1},{1,0},{2,3},{3,2},{4,5},{5,4},{6,7},{7,6},{8,9},{9,8},{10,11... | collective-permute-start | bytes 442376 | tf_op jit(solution)/shard_map/ppermute | solution.py:444
  47.6 1.0 collective-permute-done
  48.8 14.4 %all_to_all.22 = bf16[16,8,2304]{2,1,0:T(8,128)(2,1)S(1)} all-to-all(bf16[16,8,2304]{2,1,0:T(8,128)(2,1)S(1)} %bitcast.54), channel_id=1, replica_groups={{0,2,4,6,8,10,12,14,16,18,20,22,24,26,28,30},{32,34,36,38,40,42,44,46,4..., dimensions={0} | all-to-all | bytes 1179648 | tf_op jit(solution)/shard_map/all_to_all | solution.py:447
  63.2 0.9 collective-permute-start.3
  64.4 2.4 %collective-permute-start.1 = (bf16[128,2304]{1,0:T(8,128)(2,1)S(1)}, bf16[128,2304]{1,0:T(8,128)(2,1)S(1)}, u32[]{:S(2)}, u32[]{:S(2)}) collective-permute-start(bf16[128,2304]{1,0:T(8,128)(2,1)S(1)} %bitcast.45), channel_id=1, source_target_pairs={{0,96},{1,25},{2,98},{3,27},{4,100},{5,29},{6,102},{7,31},{8,104},... | collective-permute-start | bytes 1769480 | tf_op jit(solution)/shard_map/ppermute | solution.py:451
  66.8 1.6 %ffn.4 = bf16[128,2304]{1,0:T(8,128)(2,1)S(1)} custom-call(bf16[128,2304]{1,0:T(8,128)(2,1)S(1)} %bitcast.46, bf16[360,2304]{1,0:T(8,128)(2,1)S(1)} %bitcast.31, bf16[360,2304]{1,0:T(8,128)(2,1)S(1)} %bitcast.35, bf16[360,2304]{1,0:T(8,128)(2,1)S(1)} %bitcast.39), custom_call_target="tpu_custom_call" | custom-call | flops 637009920 | bytes 6156288 | tf_op jit(solution)/shard_map/ffn/pallas_call | solution.py:309
  68.4 5.4 %collective-permute-done.3.x_ref = bf16[128,2304]{1,0:T(8,128)(2,1)S(1)} collective-permute-done((bf16[128,2304]{1,0:T(8,128)(2,1)S(1)}, bf16[128,2304]{1,0:T(8,128)(2,1)S(1)}, u32[]{:S(2)}, u32[]{:S(2)}) %collective-permute-start.3) | collective-permute-done | bytes 589856 | tf_op jit(solution)/shard_map/ppermute | solution.py:451
  73.8 1.6 %ffn.5 = bf16[128,2304]{1,0:T(8,128)(2,1)S(1)} custom-call(bf16[128,2304]{1,0:T(8,128)(2,1)S(1)} %collective-permute-done.3.x_ref, bf16[360,2304]{1,0:T(8,128)(2,1)S(1)} %bitcast.32, bf16[360,2304]{1,0:T(8,128)(2,1)S(1)} %bitcast.36, bf16[360,2304]{1,0:T(8,128)(2,1)S(1)} %bitcast.40), custom_call_target="tpu_custom_call" | custom-call | flops 637009920 | bytes 6156288 | tf_op jit(solution)/shard_map/ffn/pallas_call | solution.py:309
  75.3 1.0 collective-permute-start.4
  76.4 3.7 %collective-permute-done.2.x_ref = bf16[128,2304]{1,0:T(8,128)(2,1)S(1)} collective-permute-done((bf16[128,2304]{1,0:T(8,128)(2,1)S(1)}, bf16[128,2304]{1,0:T(8,128)(2,1)S(1)}, u32[]{:S(2)}, u32[]{:S(2)}) %collective-permute-start.2) | collective-permute-done | bytes 589856 | tf_op jit(solution)/shard_map/ppermute | solution.py:451
  80.0 1.6 %ffn.6 = bf16[128,2304]{1,0:T(8,128)(2,1)S(1)} custom-call(bf16[128,2304]{1,0:T(8,128)(2,1)S(1)} %collective-permute-done.2.x_ref, bf16[360,2304]{1,0:T(8,128)(2,1)S(1)} %bitcast.33, bf16[360,2304]{1,0:T(8,128)(2,1)S(1)} %bitcast.37, bf16[360,2304]{1,0:T(8,128)(2,1)S(1)} %bitcast.41), custom_call_target="tpu_custom_call" | custom-call | flops 637009920 | bytes 6156288 | tf_op jit(solution)/shard_map/ffn/pallas_call | solution.py:309
  82.0 1.6 %ffn.7 = bf16[128,2304]{1,0:T(8,128)(2,1)S(1)} custom-call(bf16[128,2304]{1,0:T(8,128)(2,1)S(1)} %collective-permute-done.1.x_ref, bf16[360,2304]{1,0:T(8,128)(2,1)S(1)} %bitcast.34, bf16[360,2304]{1,0:T(8,128)(2,1)S(1)} %bitcast.38, bf16[360,2304]{1,0:T(8,128)(2,1)S(1)} %bitcast.42), custom_call_target="tpu_custom_call" | custom-call | flops 637009920 | bytes 6156288 | tf_op jit(solution)/shard_map/ffn/pallas_call | solution.py:309
  83.6 1.2 %collective-permute-start.6 = (bf16[128,2304]{1,0:T(8,128)(2,1)S(1)}, bf16[128,2304]{1,0:T(8,128)(2,1)S(1)}, u32[]{:S(2)}, u32[]{:S(2)}) collective-permute-start(bf16[128,2304]{1,0:T(8,128)(2,1)S(1)} %ffn.7), channel_id=1, source_target_pairs={{0,32},{1,9},{2,34},{3,11},{4,36},{5,13},{6,38},{7,15},{8,40},{9,1... | collective-permute-start | bytes 1769480 | tf_op jit(solution)/shard_map/ppermute | solution.py:456
  84.8 1.6 %collective-permute-done.4 = bf16[128,2304]{1,0:T(8,128)(2,1)S(1)} collective-permute-done((bf16[128,2304]{1,0:T(8,128)(2,1)S(1)}, bf16[128,2304]{1,0:T(8,128)(2,1)S(1)}, u32[]{:S(2)}, u32[]{:S(2)}) %collective-permute-start.4) | collective-permute-done | bytes 589856 | tf_op jit(solution)/shard_map/ppermute | solution.py:456
  86.4 4.6 %collective-permute-done.5 = bf16[128,2304]{1,0:T(8,128)(2,1)S(1)} collective-permute-done((bf16[128,2304]{1,0:T(8,128)(2,1)S(1)}, bf16[128,2304]{1,0:T(8,128)(2,1)S(1)}, u32[]{:S(2)}, u32[]{:S(2)}) %collective-permute-start.5) | collective-permute-done | bytes 589856 | tf_op jit(solution)/shard_map/ppermute | solution.py:456
  91.0 3.0 %collective-permute-done.6 = bf16[128,2304]{1,0:T(8,128)(2,1)S(1)} collective-permute-done((bf16[128,2304]{1,0:T(8,128)(2,1)S(1)}, bf16[128,2304]{1,0:T(8,128)(2,1)S(1)}, u32[]{:S(2)}, u32[]{:S(2)}) %collective-permute-start.6) | collective-permute-done | bytes 589856 | tf_op jit(solution)/shard_map/ppermute | solution.py:456
  94.2 12.5 %all_to_all.23 = bf16[16,8,2304]{2,1,0:T(8,128)(2,1)S(1)} all-to-all(bf16[16,8,2304]{2,1,0:T(8,128)(2,1)S(1)} %fusion), channel_id=1, replica_groups={{0,2,4,6,8,10,12,14,16,18,20,22,24,26,28,30},{32,34,36,38,40,42,44,46,4..., dimensions={0} | all-to-all | bytes 1179648 | tf_op jit(solution)/shard_map/all_to_all | solution.py:458
  106.8 7.0 %collective-permute-start.7 = (bf16[32,2304]{1,0:T(8,128)(2,1)S(1)}, bf16[32,2304]{1,0:T(8,128)(2,1)S(1)}, u32[]{:S(2)}, u32[]{:S(2)}) collective-permute-start(bf16[32,2304]{1,0:T(8,128)(2,1)S(1)} %bitcast_reduce_fusion.mine_ref), channel_id=1, source_target_pairs={{0,1},{1,0},{2,3},{3,2},{4,5},{5,4},{6,7},{7,6},{8,9},{9,8},{10,11... | collective-permute-start | bytes 442376 | tf_op jit(solution)/shard_map/ppermute | solution.py:463
  113.8 1.0 collective-permute-done.7.back_ref
  114.8 1.5 %finish.1 = (bf16[1,4,2,2304]{3,2,1,0:T(2,128)(2,1)}, f32[2,4]{1,0:T(2,128)}) custom-call(s32[2,2,4]{2,1,0:T(2,128)S(1)} %bitcast.51, bf16[32,2304]{1,0:T(8,128)(2,1)S(1)} %bitcast_reduce_fusion.mine_ref, bf16[32,2304]{1,0:T(8,128)(2,1)S(1)} %collective-permute-done.7.back_ref, f32[8,2304]{1,0:T(8,128)S(1)} %get-tuple-element.20.mixed_ref, ...), custom_call_target="tpu_custom_call" | custom-call | tf_op jit(solution)/shard_map/finish/pallas_call | solution.py:362
  (33 shorter events, 2.1 us)
Async XLA Ops:
  0.6 0.8 copy-start.3
  20.8 46.0 %copy-start.2 = (bf16[1,360,2304]{2,1,0:T(8,128)(2,1)S(1)}, bf16[1,360,2304]{2,1,0:T(8,128)(2,1)}, u32[]{:S(2)}) copy-start(bf16[1,360,2304]{2,1,0:T(8,128)(2,1)} %param.36) | copy-start | bytes 4976644
  28.4 13.7 %copy-start.4 = (bf16[1,4,2,2304]{3,2,1,0:T(2,128)(2,1)S(1)}, bf16[1,4,2,2304]{3,2,1,0:T(2,128)(2,1)}, u32[]{:S(2)}) copy-start(bf16[1,4,2,2304]{3,2,1,0:T(2,128)(2,1)} %q_ref.3) | copy-start | bytes 110596
  28.4 13.7 %copy-start.5 = (f32[2304,8]{0,1:T(8,128)S(1)}, f32[2304,8]{0,1:T(8,128)}, u32[]{:S(2)}) copy-start(f32[2304,8]{0,1:T(8,128)} %param.32) | copy-start | bytes 221188
  28.4 13.7 %copy-start.6 = (bf16[1,4,2,2304]{3,2,1,0:T(2,128)(2,1)S(1)}, bf16[1,4,2,2304]{3,2,1,0:T(2,128)(2,1)}, u32[]{:S(2)}) copy-start(bf16[1,4,2,2304]{3,2,1,0:T(2,128)(2,1)} %k_ref.3) | copy-start | bytes 110596
  28.4 13.6 %copy-start.7 = (bf16[1,4,2,2304]{3,2,1,0:T(2,128)(2,1)S(1)}, bf16[1,4,2,2304]{3,2,1,0:T(2,128)(2,1)}, u32[]{:S(2)}) copy-start(bf16[1,4,2,2304]{3,2,1,0:T(2,128)(2,1)} %v_ref.1) | copy-start | bytes 110596
  28.4 13.6 %copy-start.8 = (bf16[1,4,2,2304]{3,2,1,0:T(2,128)(2,1)S(1)}, bf16[1,4,2,2304]{3,2,1,0:T(2,128)(2,1)}, u32[]{:S(2)}) copy-start(bf16[1,4,2,2304]{3,2,1,0:T(2,128)(2,1)} %h_ref.1) | copy-start | bytes 110596
  28.4 13.6 %copy-start.10 = (f32[2304]{0:T(1024)S(1)}, f32[2304]{0:T(1024)}, u32[]{:S(2)}) copy-start(f32[2304]{0:T(1024)} %param.33) | copy-start | bytes 27652
  28.5 13.6 %copy-start.11 = (s32[1,4,2,2]{1,3,2,0:T(2,128)S(1)}, s32[1,4,2,2]{1,3,2,0:T(2,128)}, u32[]{:S(2)}) copy-start(s32[1,4,2,2]{1,3,2,0:T(2,128)} %param.31) | copy-start | bytes 196
  28.5 38.3 %copy-start.1 = (bf16[1,2304,360]{1,2,0:T(8,128)(2,1)S(1)}, bf16[1,2304,360]{1,2,0:T(8,128)(2,1)}, u32[]{:S(2)}) copy-start(bf16[1,2304,360]{1,2,0:T(8,128)(2,1)} %param.35) | copy-start | bytes 4976644
  44.0 4.6 %collective-permute-start = (bf16[32,2304]{1,0:T(8,128)(2,1)S(1)}, bf16[32,2304]{1,0:T(8,128)(2,1)S(1)}, u32[]{:S(2)}, u32[]{:S(2)}) collective-permute-start(bf16[32,2304]{1,0:T(8,128)(2,1)S(1)} %get-tuple-element.13), channel_id=1, source_target_pairs={{0,1},{1,0},{2,3},{3,2},{4,5},{5,4},{6,7},{7,6},{8,9},{9,8},{10,11... | collective-permute-start | bytes 442376 | tf_op jit(solution)/shard_map/ppermute | solution.py:444
  47.6 19.2 %copy-start = (bf16[1,2304,360]{1,2,0:T(8,128)(2,1)S(1)}, bf16[1,2304,360]{1,2,0:T(8,128)(2,1)}, u32[]{:S(2)}) copy-start(bf16[1,2304,360]{1,2,0:T(8,128)(2,1)} %param.34) | copy-start | bytes 4976644
  63.2 10.6 %collective-permute-start.3 = (bf16[128,2304]{1,0:T(8,128)(2,1)S(1)}, bf16[128,2304]{1,0:T(8,128)(2,1)S(1)}, u32[]{:S(2)}, u32[]{:S(2)}) collective-permute-start(bf16[128,2304]{1,0:T(8,128)(2,1)S(1)} %bitcast.43), channel_id=1, source_target_pairs={{0,64},{1,17},{2,66},{3,19},{4,68},{5,21},{6,70},{7,23},{8,72},{9,... | collective-permute-start | bytes 1769480 | tf_op jit(solution)/shard_map/ppermute | solution.py:451
  64.1 15.9 %collective-permute-start.2 = (bf16[128,2304]{1,0:T(8,128)(2,1)S(1)}, bf16[128,2304]{1,0:T(8,128)(2,1)S(1)}, u32[]{:S(2)}, u32[]{:S(2)}) collective-permute-start(bf16[128,2304]{1,0:T(8,128)(2,1)S(1)} %bitcast.44), channel_id=1, source_target_pairs={{0,32},{1,9},{2,34},{3,11},{4,36},{5,13},{6,38},{7,15},{8,40},{9,1... | collective-permute-start | bytes 1769480 | tf_op jit(solution)/shard_map/ppermute | solution.py:451
  64.4 17.6 %collective-permute-start.1 = (bf16[128,2304]{1,0:T(8,128)(2,1)S(1)}, bf16[128,2304]{1,0:T(8,128)(2,1)S(1)}, u32[]{:S(2)}, u32[]{:S(2)}) collective-permute-start(bf16[128,2304]{1,0:T(8,128)(2,1)S(1)} %bitcast.45), channel_id=1, source_target_pairs={{0,96},{1,25},{2,98},{3,27},{4,100},{5,29},{6,102},{7,31},{8,104},... | collective-permute-start | bytes 1769480 | tf_op jit(solution)/shard_map/ppermute | solution.py:451
  75.3 11.0 %collective-permute-start.4 = (bf16[128,2304]{1,0:T(8,128)(2,1)S(1)}, bf16[128,2304]{1,0:T(8,128)(2,1)S(1)}, u32[]{:S(2)}, u32[]{:S(2)}) collective-permute-start(bf16[128,2304]{1,0:T(8,128)(2,1)S(1)} %ffn.5), channel_id=1, source_target_pairs={{0,64},{1,17},{2,66},{3,19},{4,68},{5,21},{6,70},{7,23},{8,72},{9,... | collective-permute-start | bytes 1769480 | tf_op jit(solution)/shard_map/ppermute | solution.py:456
  81.6 9.3 %collective-permute-start.5 = (bf16[128,2304]{1,0:T(8,128)(2,1)S(1)}, bf16[128,2304]{1,0:T(8,128)(2,1)S(1)}, u32[]{:S(2)}, u32[]{:S(2)}) collective-permute-start(bf16[128,2304]{1,0:T(8,128)(2,1)S(1)} %ffn.6), channel_id=1, source_target_pairs={{0,96},{1,25},{2,98},{3,27},{4,100},{5,29},{6,102},{7,31},{8,104},... | collective-permute-start | bytes 1769480 | tf_op jit(solution)/shard_map/ppermute | solution.py:456
  83.6 10.3 %collective-permute-start.6 = (bf16[128,2304]{1,0:T(8,128)(2,1)S(1)}, bf16[128,2304]{1,0:T(8,128)(2,1)S(1)}, u32[]{:S(2)}, u32[]{:S(2)}) collective-permute-start(bf16[128,2304]{1,0:T(8,128)(2,1)S(1)} %ffn.7), channel_id=1, source_target_pairs={{0,32},{1,9},{2,34},{3,11},{4,36},{5,13},{6,38},{7,15},{8,40},{9,1... | collective-permute-start | bytes 1769480 | tf_op jit(solution)/shard_map/ppermute | solution.py:456
  94.2 20.6 %copy-start.9 = (f32[2304]{0:T(1024)S(1)}, f32[2304]{0:T(1024)}, u32[]{:S(2)}) copy-start(f32[2304]{0:T(1024)} %param.37) | copy-start | bytes 27652
  106.8 8.0 %collective-permute-start.7 = (bf16[32,2304]{1,0:T(8,128)(2,1)S(1)}, bf16[32,2304]{1,0:T(8,128)(2,1)S(1)}, u32[]{:S(2)}, u32[]{:S(2)}) collective-permute-start(bf16[32,2304]{1,0:T(8,128)(2,1)S(1)} %bitcast_reduce_fusion.mine_ref), channel_id=1, source_target_pairs={{0,1},{1,0},{2,3},{3,2},{4,5},{5,4},{6,7},{7,6},{8,9},{9,8},{10,11... | collective-permute-start | bytes 442376 | tf_op jit(solution)/shard_map/ppermute | solution.py:463

commit v4 on v3

--- a/solution.py
+++ b/solution.py
@@ -10,7 +10,7 @@
 KVB = 16
 CAP = 4
 LANES = 128
-ROOM = 61 << 20
+ROOM = 51 << 20
 
 BF = jnp.bfloat16
 F32 = jnp.float32
@@ -424,7 +424,7 @@
     device = lambda x, z, y, c: (x * side + z) * exp_count + y * 2 + c
     swap = [(i, i ^ 1) for i in range(exp_count)]
     lines = [
-        [device(o, k, y, 0) if c == 0 else device(k, o, y, 1) for k in range(side) for y in range(planes)]
+        [device(o, k, y, 1) if c == 0 else device(k, o, y, 0) for k in range(side) for y in range(planes)]
         for c in range(2)
         for o in range(side)
     ]
@@ -434,8 +434,8 @@
         for x in range(side):
             for z in range(side):
                 for y in range(planes):
-                    moves.append((device(x, z, y, 0), device((x + step) % side, z, y, 0)))
-                    moves.append((device(x, z, y, 1), device(x, (z + step) % side, y, 1)))
+                    moves.append((device(x, z, y, 1), device((x + step) % side, z, y, 1)))
+                    moves.append((device(x, z, y, 0), device(x, (z + step) % side, y, 0)))
         return moves
 
     wide = (planes, 2 * CAP, model)

time: 117 us -> 113 us (0.966)
  starting transfers between devices: 16.8 us -> 11.3 us
  blocking collectives: 59.8 us -> 64.6 us
  waiting for transfers between devices: 20.2 us -> 18.9 us
  Pallas kernels: 17.4 us -> 16.1 us
    ppermute x1, starting transfers between devices: 7.02 us -> 0.09 us  [local(): back = lax.ppermute(mine, 'expert', swap)]
    all_to_all x1, blocking collectives: 14.4 us -> 16.9 us  [local(): rows = lax.all_to_all(rows, both, 0, 0, tiled=True, axis_index_groups=lines)]
    all_to_all x1, blocking collectives: 12.5 us -> 14.9 us  [local(): lax.all_to_all(total.reshape(-1, 2 * CAP, model), both, 0, 0, tiled=True,...]
    ppermute x3, waiting for transfers between devices: 9.05 us -> 7.1 us  [local(): arrivals = [lax.ppermute(rows, both, shift(s)) for s in order]]
    pallas_call x1, Pallas kernels: 7.6 us -> 6.27 us  [attend(): pl.pallas_call(attend_kernel, out_shape=jax.ShapeDtypeStruct((rows, model...]
  transfers between devices with their start and end apart: 8 -> 8, of which waited for: 7 -> 7; matrix products, arithmetic and copies ran while one was open for 0% -> 0% of each run, Pallas kernels for 5% -> 6%
where the time goes in v4:
time: 113 us
  blocking collectives  64.6 us (57%)
  waiting for transfers between devices  18.9 us (17%)
  Pallas kernels  16.1 us (14%)
  starting transfers between devices  11.3 us (10%)
    all_to_all x2, blocking collectives, exchange(): return lax.all_to_all(x, axis, 0, 0, tiled=True)  32.8 us
    all_to_all x1, blocking collectives, local(): rows = lax.all_to_all(rows, both, 0, 0, tiled=True, axis_index_groups=lines)  16.9 us
    all_to_all x1, blocking collectives, local(): lax.all_to_all(total.reshape(-1, 2 * CAP, model), both, 0, 0, tiled=True,...  14.9 us
    ppermute x3, waiting for transfers between devices, local(): parts.append(lax.ppermute(ffn(arrived, *weights), both, shift(-s)))  9.4 us
    ppermute x3, waiting for transfers between devices, local(): arrivals = [lax.ppermute(rows, both, shift(s)) for s in order]  7.1 us
    pallas_call x4, Pallas kernels, ffn(): pl.pallas_call(ffn_kernel, out_shape=jax.ShapeDtypeStruct(x.shape, BF), i...  6.36 us
    pallas_call x1, Pallas kernels, attend(): pl.pallas_call(attend_kernel, out_shape=jax.ShapeDtypeStruct((rows, model...  6.27 us
    ppermute x3, starting transfers between devices, local(): arrivals = [lax.ppermute(rows, both, shift(s)) for s in order]  4.3 us
  transfers between devices with their start and end apart: 8, of which 7 were waited for; matrix products, arithmetic and copies ran while one was open for 0% of the time, Pallas kernels for 6%

profile of v4, /device:TPU:1, one launch (start us, length us, event | category | flops | bytes accessed | tf_op | source)
XLA Modules:
  0.0 113.1 jit_solution(15089188020119399206)
XLA Ops:
  0.7 0.9 copy-done.4
  1.6 19.2 %all_to_all.20 = bf16[16,8,2304]{2,1,0:T(8,128)(2,1)S(1)} all-to-all(bf16[16,8,2304]{2,1,0:T(8,128)(2,1)S(1)} %share.1), channel_id=1, replica_groups=mesh['blk'=16,'expert'=8] {'blk'}, dimensions={0} | all-to-all | bytes 1179648 | tf_op jit(solution)/shard_map/all_to_all | solution.py:376
  20.8 6.3 %attend.1 = bf16[128,2432]{1,0:T(8,128)(2,1)S(1)} custom-call(s32[32]{0:T(128)S(1)} %copy-done.16, s32[32,64]{1,0:T(8,128)S(1)} %copy-done.10, s32[16,32]{1,0:T(8,128)S(1)} %copy-done.13, s32[16,32]{1,0:T(8,128)S(1)} %copy-done.14, bf16[128,2304]{1,0:T(8,128)(2,1)S(1)} %bitcast.44, bf16[4,64,2304]{2,1,0:T(8,128)(2,1)S(1)} %copy-done.3, ...), custom_call_target="tpu_custom_call" | custom-call | tf_op jit(solution)/shard_map/attend/pallas_call | solution.py:155
  27.2 13.6 %all_to_all.21.got_ref = bf16[16,8,2432]{2,1,0:T(8,128)(2,1)S(1)} all-to-all(bf16[16,8,2432]{2,1,0:T(8,128)(2,1)S(1)} %bitcast.43), channel_id=1, replica_groups=mesh['blk'=16,'expert'=8] {'blk'}, dimensions={0} | all-to-all | bytes 1245184 | tf_op jit(solution)/shard_map/all_to_all | solution.py:376
  40.9 1.9 %combine.1 = (f32[8,2304]{1,0:T(8,128)S(1)}, bf16[32,2304]{1,0:T(8,128)(2,1)S(1)}, f32[8,128]{1,0:T(8,128)S(1)}) custom-call(s32[2,2,4]{2,1,0:T(2,128)S(1)} %bitcast.52, bf16[16,8,2432]{2,1,0:T(8,128)(2,1)S(1)} %all_to_all.21.got_ref, bf16[1,4,2,2304]{3,2,1,0:T(2,128)(2,1)S(1)} %copy-done.5, bf16[1,4,2,2304]{3,2,1,0:T(2,128)(2,1)S(1)} %copy-done.7, ...), custom_call_target="tpu_custom_call" | custom-call | tf_op jit(solution)/shard_map/combine/pallas_call | solution.py:285
  42.8 3.3 %collective-permute-start = (bf16[32,2304]{1,0:T(8,128)(2,1)S(1)}, bf16[32,2304]{1,0:T(8,128)(2,1)S(1)}, u32[]{:S(2)}, u32[]{:S(2)}) collective-permute-start(bf16[32,2304]{1,0:T(8,128)(2,1)S(1)} %get-tuple-element.13), channel_id=1, source_target_pairs={{0,1},{1,0},{2,3},{3,2},{4,5},{5,4},{6,7},{7,6},{8,9},{9,8},{10,11... | collective-permute-start | bytes 442376 | tf_op jit(solution)/shard_map/ppermute | solution.py:444
  46.1 1.0 collective-permute-done
  47.3 16.9 %all_to_all.22 = bf16[16,8,2304]{2,1,0:T(8,128)(2,1)S(1)} all-to-all(bf16[16,8,2304]{2,1,0:T(8,128)(2,1)S(1)} %bitcast.54), channel_id=1, replica_groups={{1,3,5,7,9,11,13,15,17,19,21,23,25,27,29,31},{33,35,37,39,41,43,45,47,4..., dimensions={0} | all-to-all | bytes 1179648 | tf_op jit(solution)/shard_map/all_to_all | solution.py:447
  64.1 1.6 %collective-permute-start.3 = (bf16[128,2304]{1,0:T(8,128)(2,1)S(1)}, bf16[128,2304]{1,0:T(8,128)(2,1)S(1)}, u32[]{:S(2)}, u32[]{:S(2)}) collective-permute-start(bf16[128,2304]{1,0:T(8,128)(2,1)S(1)} %bitcast.45), channel_id=1, source_target_pairs={{1,65},{0,16},{3,67},{2,18},{5,69},{4,20},{7,71},{6,22},{9,73},{8,... | collective-permute-start | bytes 1769480 | tf_op jit(solution)/shard_map/ppermute | solution.py:451
  66.2 2.2 %collective-permute-start.1 = (bf16[128,2304]{1,0:T(8,128)(2,1)S(1)}, bf16[128,2304]{1,0:T(8,128)(2,1)S(1)}, u32[]{:S(2)}, u32[]{:S(2)}) collective-permute-start(bf16[128,2304]{1,0:T(8,128)(2,1)S(1)} %bitcast.47), channel_id=1, source_target_pairs={{1,97},{0,24},{3,99},{2,26},{5,101},{4,28},{7,103},{6,30},{9,105},... | collective-permute-start | bytes 1769480 | tf_op jit(solution)/shard_map/ppermute | solution.py:451
  68.4 1.6 %ffn.4 = bf16[128,2304]{1,0:T(8,128)(2,1)S(1)} custom-call(bf16[128,2304]{1,0:T(8,128)(2,1)S(1)} %bitcast.48, bf16[360,2304]{1,0:T(8,128)(2,1)S(1)} %bitcast.31, bf16[360,2304]{1,0:T(8,128)(2,1)S(1)} %bitcast.35, bf16[360,2304]{1,0:T(8,128)(2,1)S(1)} %bitcast.39), custom_call_target="tpu_custom_call" | custom-call | flops 637009920 | bytes 6156288 | tf_op jit(solution)/shard_map/ffn/pallas_call | solution.py:309
  70.0 4.4 %collective-permute-done.3.x_ref = bf16[128,2304]{1,0:T(8,128)(2,1)S(1)} collective-permute-done((bf16[128,2304]{1,0:T(8,128)(2,1)S(1)}, bf16[128,2304]{1,0:T(8,128)(2,1)S(1)}, u32[]{:S(2)}, u32[]{:S(2)}) %collective-permute-start.3) | collective-permute-done | bytes 589856 | tf_op jit(solution)/shard_map/ppermute | solution.py:451
  74.5 1.6 %ffn.5 = bf16[128,2304]{1,0:T(8,128)(2,1)S(1)} custom-call(bf16[128,2304]{1,0:T(8,128)(2,1)S(1)} %collective-permute-done.3.x_ref, bf16[360,2304]{1,0:T(8,128)(2,1)S(1)} %bitcast.32, bf16[360,2304]{1,0:T(8,128)(2,1)S(1)} %bitcast.36, bf16[360,2304]{1,0:T(8,128)(2,1)S(1)} %bitcast.40), custom_call_target="tpu_custom_call" | custom-call | flops 637009920 | bytes 6156288 | tf_op jit(solution)/shard_map/ffn/pallas_call | solution.py:309
  76.1 1.9 %collective-permute-start.4 = (bf16[128,2304]{1,0:T(8,128)(2,1)S(1)}, bf16[128,2304]{1,0:T(8,128)(2,1)S(1)}, u32[]{:S(2)}, u32[]{:S(2)}) collective-permute-start(bf16[128,2304]{1,0:T(8,128)(2,1)S(1)} %ffn.5), channel_id=1, source_target_pairs={{1,65},{0,16},{3,67},{2,18},{5,69},{4,20},{7,71},{6,22},{9,73},{8,... | collective-permute-start | bytes 1769480 | tf_op jit(solution)/shard_map/ppermute | solution.py:456
  78.0 2.7 %collective-permute-done.2.x_ref = bf16[128,2304]{1,0:T(8,128)(2,1)S(1)} collective-permute-done((bf16[128,2304]{1,0:T(8,128)(2,1)S(1)}, bf16[128,2304]{1,0:T(8,128)(2,1)S(1)}, u32[]{:S(2)}, u32[]{:S(2)}) %collective-permute-start.2) | collective-permute-done | bytes 589856 | tf_op jit(solution)/shard_map/ppermute | solution.py:451
  80.7 1.6 %ffn.6 = bf16[128,2304]{1,0:T(8,128)(2,1)S(1)} custom-call(bf16[128,2304]{1,0:T(8,128)(2,1)S(1)} %collective-permute-done.2.x_ref, bf16[360,2304]{1,0:T(8,128)(2,1)S(1)} %bitcast.33, bf16[360,2304]{1,0:T(8,128)(2,1)S(1)} %bitcast.37, bf16[360,2304]{1,0:T(8,128)(2,1)S(1)} %bitcast.41), custom_call_target="tpu_custom_call" | custom-call | flops 637009920 | bytes 6156288 | tf_op jit(solution)/shard_map/ffn/pallas_call | solution.py:309
  83.0 1.6 %ffn.7 = bf16[128,2304]{1,0:T(8,128)(2,1)S(1)} custom-call(bf16[128,2304]{1,0:T(8,128)(2,1)S(1)} %collective-permute-done.1.x_ref, bf16[360,2304]{1,0:T(8,128)(2,1)S(1)} %bitcast.34, bf16[360,2304]{1,0:T(8,128)(2,1)S(1)} %bitcast.38, bf16[360,2304]{1,0:T(8,128)(2,1)S(1)} %bitcast.42), custom_call_target="tpu_custom_call" | custom-call | flops 637009920 | bytes 6156288 | tf_op jit(solution)/shard_map/ffn/pallas_call | solution.py:309
  84.6 0.9 collective-permute-start.6
  85.5 1.9 %collective-permute-done.4 = bf16[128,2304]{1,0:T(8,128)(2,1)S(1)} collective-permute-done((bf16[128,2304]{1,0:T(8,128)(2,1)S(1)}, bf16[128,2304]{1,0:T(8,128)(2,1)S(1)}, u32[]{:S(2)}, u32[]{:S(2)}) %collective-permute-start.4) | collective-permute-done | bytes 589856 | tf_op jit(solution)/shard_map/ppermute | solution.py:456
  87.3 5.5 %collective-permute-done.5 = bf16[128,2304]{1,0:T(8,128)(2,1)S(1)} collective-permute-done((bf16[128,2304]{1,0:T(8,128)(2,1)S(1)}, bf16[128,2304]{1,0:T(8,128)(2,1)S(1)}, u32[]{:S(2)}, u32[]{:S(2)}) %collective-permute-start.5) | collective-permute-done | bytes 589856 | tf_op jit(solution)/shard_map/ppermute | solution.py:456
  92.8 2.1 %collective-permute-done.6 = bf16[128,2304]{1,0:T(8,128)(2,1)S(1)} collective-permute-done((bf16[128,2304]{1,0:T(8,128)(2,1)S(1)}, bf16[128,2304]{1,0:T(8,128)(2,1)S(1)}, u32[]{:S(2)}, u32[]{:S(2)}) %collective-permute-start.6) | collective-permute-done | bytes 589856 | tf_op jit(solution)/shard_map/ppermute | solution.py:456
  95.2 14.9 %all_to_all.23 = bf16[16,8,2304]{2,1,0:T(8,128)(2,1)S(1)} all-to-all(bf16[16,8,2304]{2,1,0:T(8,128)(2,1)S(1)} %fusion), channel_id=1, replica_groups={{1,3,5,7,9,11,13,15,17,19,21,23,25,27,29,31},{33,35,37,39,41,43,45,47,4..., dimensions={0} | all-to-all | bytes 1179648 | tf_op jit(solution)/shard_map/all_to_all | solution.py:458
  110.2 1.4 %collective-permute-done.7.back_ref = bf16[32,2304]{1,0:T(8,128)(2,1)S(1)} collective-permute-done((bf16[32,2304]{1,0:T(8,128)(2,1)S(1)}, bf16[32,2304]{1,0:T(8,128)(2,1)S(1)}, u32[]{:S(2)}, u32[]{:S(2)}) %collective-permute-start.7) | collective-permute-done | bytes 147488 | tf_op jit(solution)/shard_map/ppermute | solution.py:463
  111.6 1.5 %finish.1 = (bf16[1,4,2,2304]{3,2,1,0:T(2,128)(2,1)}, f32[2,4]{1,0:T(2,128)}) custom-call(s32[2,2,4]{2,1,0:T(2,128)S(1)} %bitcast.53, bf16[32,2304]{1,0:T(8,128)(2,1)S(1)} %bitcast_reduce_fusion.mine_ref, bf16[32,2304]{1,0:T(8,128)(2,1)S(1)} %collective-permute-done.7.back_ref, f32[8,2304]{1,0:T(8,128)S(1)} %get-tuple-element.20.mixed_ref, ...), custom_call_target="tpu_custom_call" | custom-call | tf_op jit(solution)/shard_map/finish/pallas_call | solution.py:362
  (43 shorter events, 1.9 us)
Async XLA Ops:
  0.6 20.2 %copy-start.3 = (bf16[4,64,2304]{2,1,0:T(8,128)(2,1)S(1)}, bf16[4,64,2304]{2,1,0:T(8,128)(2,1)}, u32[]{:S(2)}) copy-start(bf16[4,64,2304]{2,1,0:T(8,128)(2,1)} %k_ref.2) | copy-start | bytes 3538948
  1.5 19.3 %copy-start.10 = (s32[32,64]{1,0:T(8,128)S(1)}, s32[32,64]{1,0:T(8,128)}, u32[]{:S(2)}) copy-start(s32[32,64]{1,0:T(8,128)} %live.1) | copy-start | bytes 24580
  1.5 19.3 %copy-start.13 = (s32[16,32]{1,0:T(8,128)S(1)}, s32[16,32]{1,0:T(8,128)}, u32[]{:S(2)}) copy-start(s32[16,32]{1,0:T(8,128)} %tail_len.1) | copy-start | bytes 6148
  1.5 19.3 %copy-start.14 = (s32[16,32]{1,0:T(8,128)S(1)}, s32[16,32]{1,0:T(8,128)}, u32[]{:S(2)}) copy-start(s32[16,32]{1,0:T(8,128)} %source.1) | copy-start | bytes 6148
  1.5 19.3 %copy-start.16 = (s32[32]{0:T(128)S(1)}, s32[32]{0:T(128)}, u32[]{:S(2)}) copy-start(s32[32]{0:T(128)} %lengths.1) | copy-start | bytes 388
  20.8 47.6 %copy-start.2 = (bf16[1,360,2304]{2,1,0:T(8,128)(2,1)S(1)}, bf16[1,360,2304]{2,1,0:T(8,128)(2,1)}, u32[]{:S(2)}) copy-start(bf16[1,360,2304]{2,1,0:T(8,128)(2,1)} %param.36) | copy-start | bytes 4976644
  27.1 13.7 %copy-start.5 = (bf16[1,4,2,2304]{3,2,1,0:T(2,128)(2,1)S(1)}, bf16[1,4,2,2304]{3,2,1,0:T(2,128)(2,1)}, u32[]{:S(2)}) copy-start(bf16[1,4,2,2304]{3,2,1,0:T(2,128)(2,1)} %q_ref.3) | copy-start | bytes 110596
  27.1 13.7 %copy-start.6 = (f32[2304,8]{0,1:T(8,128)S(1)}, f32[2304,8]{0,1:T(8,128)}, u32[]{:S(2)}) copy-start(f32[2304,8]{0,1:T(8,128)} %param.32) | copy-start | bytes 221188
  27.1 13.7 %copy-start.7 = (bf16[1,4,2,2304]{3,2,1,0:T(2,128)(2,1)S(1)}, bf16[1,4,2,2304]{3,2,1,0:T(2,128)(2,1)}, u32[]{:S(2)}) copy-start(bf16[1,4,2,2304]{3,2,1,0:T(2,128)(2,1)} %k_ref.3) | copy-start | bytes 110596
  27.1 13.7 %copy-start.8 = (bf16[1,4,2,2304]{3,2,1,0:T(2,128)(2,1)S(1)}, bf16[1,4,2,2304]{3,2,1,0:T(2,128)(2,1)}, u32[]{:S(2)}) copy-start(bf16[1,4,2,2304]{3,2,1,0:T(2,128)(2,1)} %v_ref.1) | copy-start | bytes 110596
  27.2 13.7 %copy-start.9 = (bf16[1,4,2,2304]{3,2,1,0:T(2,128)(2,1)S(1)}, bf16[1,4,2,2304]{3,2,1,0:T(2,128)(2,1)}, u32[]{:S(2)}) copy-start(bf16[1,4,2,2304]{3,2,1,0:T(2,128)(2,1)} %h_ref.1) | copy-start | bytes 110596
  27.2 13.7 %copy-start.12 = (f32[2304]{0:T(1024)S(1)}, f32[2304]{0:T(1024)}, u32[]{:S(2)}) copy-start(f32[2304]{0:T(1024)} %param.33) | copy-start | bytes 27652
  27.2 13.7 %copy-start.15 = (s32[1,4,2,2]{1,3,2,0:T(2,128)S(1)}, s32[1,4,2,2]{1,3,2,0:T(2,128)}, u32[]{:S(2)}) copy-start(s32[1,4,2,2]{1,3,2,0:T(2,128)} %param.31) | copy-start | bytes 196
  27.2 41.2 %copy-start.1 = (bf16[1,2304,360]{1,2,0:T(8,128)(2,1)S(1)}, bf16[1,2304,360]{1,2,0:T(8,128)(2,1)}, u32[]{:S(2)}) copy-start(bf16[1,2304,360]{1,2,0:T(8,128)(2,1)} %param.35) | copy-start | bytes 4976644
  42.8 4.4 %collective-permute-start = (bf16[32,2304]{1,0:T(8,128)(2,1)S(1)}, bf16[32,2304]{1,0:T(8,128)(2,1)S(1)}, u32[]{:S(2)}, u32[]{:S(2)}) collective-permute-start(bf16[32,2304]{1,0:T(8,128)(2,1)S(1)} %get-tuple-element.13), channel_id=1, source_target_pairs={{0,1},{1,0},{2,3},{3,2},{4,5},{5,4},{6,7},{7,6},{8,9},{9,8},{10,11... | collective-permute-start | bytes 442376 | tf_op jit(solution)/shard_map/ppermute | solution.py:444
  46.1 22.3 %copy-start = (bf16[1,2304,360]{1,2,0:T(8,128)(2,1)S(1)}, bf16[1,2304,360]{1,2,0:T(8,128)(2,1)}, u32[]{:S(2)}) copy-start(bf16[1,2304,360]{1,2,0:T(8,128)(2,1)} %param.34) | copy-start | bytes 4976644
  64.1 10.3 %collective-permute-start.3 = (bf16[128,2304]{1,0:T(8,128)(2,1)S(1)}, bf16[128,2304]{1,0:T(8,128)(2,1)S(1)}, u32[]{:S(2)}, u32[]{:S(2)}) collective-permute-start(bf16[128,2304]{1,0:T(8,128)(2,1)S(1)} %bitcast.45), channel_id=1, source_target_pairs={{1,65},{0,16},{3,67},{2,18},{5,69},{4,20},{7,71},{6,22},{9,73},{8,... | collective-permute-start | bytes 1769480 | tf_op jit(solution)/shard_map/ppermute | solution.py:451
  65.8 14.9 %collective-permute-start.2 = (bf16[128,2304]{1,0:T(8,128)(2,1)S(1)}, bf16[128,2304]{1,0:T(8,128)(2,1)S(1)}, u32[]{:S(2)}, u32[]{:S(2)}) collective-permute-start(bf16[128,2304]{1,0:T(8,128)(2,1)S(1)} %bitcast.46), channel_id=1, source_target_pairs={{1,33},{0,8},{3,35},{2,10},{5,37},{4,12},{7,39},{6,14},{9,41},{8,1... | collective-permute-start | bytes 1769480 | tf_op jit(solution)/shard_map/ppermute | solution.py:451
  66.2 16.8 %collective-permute-start.1 = (bf16[128,2304]{1,0:T(8,128)(2,1)S(1)}, bf16[128,2304]{1,0:T(8,128)(2,1)S(1)}, u32[]{:S(2)}, u32[]{:S(2)}) collective-permute-start(bf16[128,2304]{1,0:T(8,128)(2,1)S(1)} %bitcast.47), channel_id=1, source_target_pairs={{1,97},{0,24},{3,99},{2,26},{5,101},{4,28},{7,103},{6,30},{9,105},... | collective-permute-start | bytes 1769480 | tf_op jit(solution)/shard_map/ppermute | solution.py:451
  76.1 11.3 %collective-permute-start.4 = (bf16[128,2304]{1,0:T(8,128)(2,1)S(1)}, bf16[128,2304]{1,0:T(8,128)(2,1)S(1)}, u32[]{:S(2)}, u32[]{:S(2)}) collective-permute-start(bf16[128,2304]{1,0:T(8,128)(2,1)S(1)} %ffn.5), channel_id=1, source_target_pairs={{1,65},{0,16},{3,67},{2,18},{5,69},{4,20},{7,71},{6,22},{9,73},{8,... | collective-permute-start | bytes 1769480 | tf_op jit(solution)/shard_map/ppermute | solution.py:456
  82.3 10.5 %collective-permute-start.5 = (bf16[128,2304]{1,0:T(8,128)(2,1)S(1)}, bf16[128,2304]{1,0:T(8,128)(2,1)S(1)}, u32[]{:S(2)}, u32[]{:S(2)}) collective-permute-start(bf16[128,2304]{1,0:T(8,128)(2,1)S(1)} %ffn.6), channel_id=1, source_target_pairs={{1,97},{0,24},{3,99},{2,26},{5,101},{4,28},{7,103},{6,30},{9,105},... | collective-permute-start | bytes 1769480 | tf_op jit(solution)/shard_map/ppermute | solution.py:456
  84.6 10.3 %collective-permute-start.6 = (bf16[128,2304]{1,0:T(8,128)(2,1)S(1)}, bf16[128,2304]{1,0:T(8,128)(2,1)S(1)}, u32[]{:S(2)}, u32[]{:S(2)}) collective-permute-start(bf16[128,2304]{1,0:T(8,128)(2,1)S(1)} %ffn.7), channel_id=1, source_target_pairs={{1,33},{0,8},{3,35},{2,10},{5,37},{4,12},{7,39},{6,14},{9,41},{8,1... | collective-permute-start | bytes 1769480 | tf_op jit(solution)/shard_map/ppermute | solution.py:456
  95.2 16.4 %copy-start.11 = (f32[2304]{0:T(1024)S(1)}, f32[2304]{0:T(1024)}, u32[]{:S(2)}) copy-start(f32[2304]{0:T(1024)} %param.37) | copy-start | bytes 27652
  110.2 1.5 %collective-permute-start.7 = (bf16[32,2304]{1,0:T(8,128)(2,1)S(1)}, bf16[32,2304]{1,0:T(8,128)(2,1)S(1)}, u32[]{:S(2)}, u32[]{:S(2)}) collective-permute-start(bf16[32,2304]{1,0:T(8,128)(2,1)S(1)} %bitcast_reduce_fusion.mine_ref), channel_id=1, source_target_pairs={{0,1},{1,0},{2,3},{3,2},{4,5},{5,4},{6,7},{7,6},{8,9},{9,8},{10,11... | collective-permute-start | bytes 442376 | tf_op jit(solution)/shard_map/ppermute | solution.py:463
  (1 other events, 0.9 us)

commit v5 on v4

--- a/solution.py
+++ b/solution.py
@@ -297,28 +297,34 @@
     )(routes, got, query, new_key, new_value, hidden, router, gain)
 
 
-def ffn_kernel(x_ref, gate_ref, up_ref, down_ref, out_ref):
-    x = x_ref[...]
-    gated = dot(x, gate_ref[...], NT)
-    upward = dot(x, up_ref[...], NT)
-    activation = (gated / (1.0 + jnp.exp(-gated)) * upward).astype(BF)
-    out_ref[...] = dot(activation, down_ref[...]).astype(BF)
-
-
-def ffn(x, w_gate, w_up, w_down):
+def ffn(xs, weights):
+    count = len(xs)
+    rows, model = xs[0].shape
+    units = weights[2].shape[0]
+
+    def kernel(*refs):
+        gate_ref, up_ref, down_ref = refs[count : count + 3]
+        x = jnp.concatenate([ref[...] for ref in refs[:count]], axis=0)
+        gated = dot(x, gate_ref[...], NT)
+        upward = dot(x, up_ref[...], NT)
+        activation = (gated / (1.0 + jnp.exp(-gated)) * upward).astype(BF)
+        result = dot(activation, down_ref[...]).astype(BF)
+        for i in range(count):
+            refs[count + 3 + i][...] = result[i * rows : (i + 1) * rows]
+
     return pl.pallas_call(
-        ffn_kernel,
-        out_shape=jax.ShapeDtypeStruct(x.shape, BF),
-        in_specs=[vmem()] * 4,
-        out_specs=vmem(),
+        kernel,
+        out_shape=(jax.ShapeDtypeStruct((rows, model), BF),) * count,
+        in_specs=[vmem()] * (count + 3),
+        out_specs=(vmem(),) * count,
         compiler_params=pltpu.CompilerParams(vmem_limit_bytes=16 << 20),
         cost_estimate=pl.CostEstimate(
-            flops=6 * x.size * w_gate.shape[0],
-            bytes_accessed=2 * (2 * x.size + 3 * w_gate.size),
-            transcendentals=x.shape[0] * w_gate.shape[0],
+            flops=6 * count * rows * model * units,
+            bytes_accessed=4 * count * rows * model + 6 * units * model,
+            transcendentals=count * rows * units,
         ),
         name="ffn",
-    )(x, w_gate, w_up, w_down)
+    )(*xs, *weights)
 
 
 def finish_kernel(routes, mine_ref, back_ref, mixed_ref, gate_ref, weight_ref, out_ref, score_ref):
@@ -447,14 +453,18 @@
     rows = lax.all_to_all(rows, both, 0, 0, tiled=True, axis_index_groups=lines)
     rows = rows.reshape(-1, model)
     weights = (w_gate[0].T, w_up[0].T, w_down[0])
-    order = (2, 1, 3)
-    arrivals = [lax.ppermute(rows, both, shift(s)) for s in order]
-    total = ffn(rows, *weights)
-    parts = [total]
-    for s, arrived in zip(order, arrivals):
-        arrived, parts[0] = lax.optimization_barrier((arrived, parts[0]))
-        parts.append(lax.ppermute(ffn(arrived, *weights), both, shift(-s)))
-    total = sum(part.astype(F32) for part in parts).astype(BF)
+    send = lambda x, step: lax.ppermute(x, both, shift(step))
+    far, before, after = send(rows, 2), send(rows, 1), send(rows, 3)
+    (own,) = ffn((rows,), weights)
+    far, own = lax.optimization_barrier((far, own))
+    (far,) = ffn((far,), weights)
+    home = send(far, -2)
+    before, after, _ = lax.optimization_barrier((before, after, far))
+    before, after = ffn((before, after), weights)
+    after, before = send(after, -3), send(before, -1)
+    partial = own.astype(F32) + home.astype(F32)
+    partial, after, before = lax.optimization_barrier((partial, after, before))
+    total = (partial + after.astype(F32) + before.astype(F32)).astype(BF)
     total = lax.all_to_all(
         total.reshape(-1, 2 * CAP, model), both, 0, 0, tiled=True, axis_index_groups=lines
     )

time: 113 us -> 113 us (level)
    pallas_call x4 -> x3, Pallas kernels: 6.36 us -> 5.29 us  [ffn(): pl.pallas_call(kernel, out_shape=(jax.ShapeDtypeStruct((rows, model), BF)...]
  transfers between devices with their start and end apart: 8 -> 8, of which waited for: 7 -> 7; matrix products, arithmetic and copies ran while one was open for 0% -> 0% of each run, Pallas kernels for 6% -> 5%
where the time goes in v5:
time: 113 us; the launch traced here: 112 us
  blocking collectives  65 us (58%)
  waiting for transfers between devices  18.5 us (16%)
  Pallas kernels  15 us (13%)
  starting transfers between devices  11.4 us (10%)
    all_to_all x2, blocking collectives, exchange(): return lax.all_to_all(x, axis, 0, 0, tiled=True)  32.8 us
    all_to_all x1, blocking collectives, local(): rows = lax.all_to_all(rows, both, 0, 0, tiled=True, axis_index_groups=lines)  16.9 us
    ppermute x6, waiting for transfers between devices, local(): send = lambda x, step: lax.ppermute(x, both, shift(step))  16.1 us
    all_to_all x1, blocking collectives, local(): lax.all_to_all(total.reshape(-1, 2 * CAP, model), both, 0, 0, tiled=True,...  15.3 us
    ppermute x6, starting transfers between devices, local(): send = lambda x, step: lax.ppermute(x, both, shift(step))  7.96 us
    pallas_call x1, Pallas kernels, attend(): pl.pallas_call(attend_kernel, out_shape=jax.ShapeDtypeStruct((rows, model...  6.27 us
    pallas_call x3, Pallas kernels, ffn(): pl.pallas_call(kernel, out_shape=(jax.ShapeDtypeStruct((rows, model), BF)...  5.29 us
    ppermute x1, starting transfers between devices, local(): lax.ppermute(outgoing, 'expert', swap).reshape(wide)  3.35 us
  transfers between devices with their start and end apart: 8, of which 7 were waited for; matrix products, arithmetic and copies ran while one was open for 0% of the time, Pallas kernels for 5%

profile of v5, /device:TPU:1, one launch (start us, length us, event | category | flops | bytes accessed | tf_op | source)
XLA Modules:
  0.0 112.2 jit_solution(9991069051977477246)
XLA Ops:
  0.7 0.9 copy-done.4
  1.6 19.2 %all_to_all.20 = bf16[16,8,2304]{2,1,0:T(8,128)(2,1)S(1)} all-to-all(bf16[16,8,2304]{2,1,0:T(8,128)(2,1)S(1)} %share.1), channel_id=1, replica_groups=mesh['blk'=16,'expert'=8] {'blk'}, dimensions={0} | all-to-all | bytes 1179648 | tf_op jit(solution)/shard_map/all_to_all | solution.py:382
  20.8 6.3 %attend.1 = bf16[128,2432]{1,0:T(8,128)(2,1)S(1)} custom-call(s32[32]{0:T(128)S(1)} %copy-done.16, s32[32,64]{1,0:T(8,128)S(1)} %copy-done.10, s32[16,32]{1,0:T(8,128)S(1)} %copy-done.13, s32[16,32]{1,0:T(8,128)S(1)} %copy-done.14, bf16[128,2304]{1,0:T(8,128)(2,1)S(1)} %bitcast.41, bf16[4,64,2304]{2,1,0:T(8,128)(2,1)S(1)} %copy-done.3, ...), custom_call_target="tpu_custom_call" | custom-call | tf_op jit(solution)/shard_map/attend/pallas_call | solution.py:155
  27.2 13.6 %all_to_all.21.got_ref = bf16[16,8,2432]{2,1,0:T(8,128)(2,1)S(1)} all-to-all(bf16[16,8,2432]{2,1,0:T(8,128)(2,1)S(1)} %bitcast.40), channel_id=1, replica_groups=mesh['blk'=16,'expert'=8] {'blk'}, dimensions={0} | all-to-all | bytes 1245184 | tf_op jit(solution)/shard_map/all_to_all | solution.py:382
  40.9 1.9 %combine.1 = (f32[8,2304]{1,0:T(8,128)S(1)}, bf16[32,2304]{1,0:T(8,128)(2,1)S(1)}, f32[8,128]{1,0:T(8,128)S(1)}) custom-call(s32[2,2,4]{2,1,0:T(2,128)S(1)} %bitcast.49, bf16[16,8,2432]{2,1,0:T(8,128)(2,1)S(1)} %all_to_all.21.got_ref, bf16[1,4,2,2304]{3,2,1,0:T(2,128)(2,1)S(1)} %copy-done.5, bf16[1,4,2,2304]{3,2,1,0:T(2,128)(2,1)S(1)} %copy-done.7, ...), custom_call_target="tpu_custom_call" | custom-call | tf_op jit(solution)/shard_map/combine/pallas_call | solution.py:285
  42.8 3.3 %collective-permute-start = (bf16[32,2304]{1,0:T(8,128)(2,1)S(1)}, bf16[32,2304]{1,0:T(8,128)(2,1)S(1)}, u32[]{:S(2)}, u32[]{:S(2)}) collective-permute-start(bf16[32,2304]{1,0:T(8,128)(2,1)S(1)} %get-tuple-element.16), channel_id=1, source_target_pairs={{0,1},{1,0},{2,3},{3,2},{4,5},{5,4},{6,7},{7,6},{8,9},{9,8},{10,11... | collective-permute-start | bytes 442376 | tf_op jit(solution)/shard_map/ppermute | solution.py:450
  46.1 1.0 collective-permute-done
  47.3 16.9 %all_to_all.22 = bf16[16,8,2304]{2,1,0:T(8,128)(2,1)S(1)} all-to-all(bf16[16,8,2304]{2,1,0:T(8,128)(2,1)S(1)} %bitcast.51), channel_id=1, replica_groups={{1,3,5,7,9,11,13,15,17,19,21,23,25,27,29,31},{33,35,37,39,41,43,45,47,4..., dimensions={0} | all-to-all | bytes 1179648 | tf_op jit(solution)/shard_map/all_to_all | solution.py:453
  64.1 1.6 %collective-permute-start.1 = (bf16[128,2304]{1,0:T(8,128)(2,1)S(1)}, bf16[128,2304]{1,0:T(8,128)(2,1)S(1)}, u32[]{:S(2)}, u32[]{:S(2)}) collective-permute-start(bf16[128,2304]{1,0:T(8,128)(2,1)S(1)} %bitcast.42), channel_id=1, source_target_pairs={{1,65},{0,16},{3,67},{2,18},{5,69},{4,20},{7,71},{6,22},{9,73},{8,... | collective-permute-start | bytes 1769480 | tf_op jit(solution)/shard_map/ppermute | solution.py:456
  65.8 1.7 %collective-permute-start.4 = (bf16[128,2304]{1,0:T(8,128)(2,1)S(1)}, bf16[128,2304]{1,0:T(8,128)(2,1)S(1)}, u32[]{:S(2)}, u32[]{:S(2)}) collective-permute-start(bf16[128,2304]{1,0:T(8,128)(2,1)S(1)} %bitcast.43), channel_id=1, source_target_pairs={{1,97},{0,24},{3,99},{2,26},{5,101},{4,28},{7,103},{6,30},{9,105},... | collective-permute-start | bytes 1769480 | tf_op jit(solution)/shard_map/ppermute | solution.py:456
  67.4 1.6 %ffn.3 = bf16[128,2304]{1,0:T(8,128)(2,1)S(1)} custom-call(bf16[128,2304]{1,0:T(8,128)(2,1)S(1)} %bitcast.45, bf16[360,2304]{1,0:T(8,128)(2,1)S(1)} %bitcast.31, bf16[360,2304]{1,0:T(8,128)(2,1)S(1)} %bitcast.34, bf16[360,2304]{1,0:T(8,128)(2,1)S(1)} %bitcast.37), custom_call_target="tpu_custom_call" | custom-call | flops 637009920 | bytes 6156288 | tf_op jit(solution)/shard_map/ffn/pallas_call | solution.py:315
  69.0 5.4 %collective-permute-done.1.refs_0_ = bf16[128,2304]{1,0:T(8,128)(2,1)S(1)} collective-permute-done((bf16[128,2304]{1,0:T(8,128)(2,1)S(1)}, bf16[128,2304]{1,0:T(8,128)(2,1)S(1)}, u32[]{:S(2)}, u32[]{:S(2)}) %collective-permute-start.1) | collective-permute-done | bytes 589856 | tf_op jit(solution)/shard_map/ppermute | solution.py:456
  74.5 1.6 %ffn.4 = bf16[128,2304]{1,0:T(8,128)(2,1)S(1)} custom-call(bf16[128,2304]{1,0:T(8,128)(2,1)S(1)} %collective-permute-done.1.refs_0_, bf16[360,2304]{1,0:T(8,128)(2,1)S(1)} %bitcast.32, bf16[360,2304]{1,0:T(8,128)(2,1)S(1)} %bitcast.35, bf16[360,2304]{1,0:T(8,128)(2,1)S(1)} %bitcast.38), custom_call_target="tpu_custom_call" | custom-call | flops 637009920 | bytes 6156288 | tf_op jit(solution)/shard_map/ffn/pallas_call | solution.py:315
  76.1 1.9 %collective-permute-start.2 = (bf16[128,2304]{1,0:T(8,128)(2,1)S(1)}, bf16[128,2304]{1,0:T(8,128)(2,1)S(1)}, u32[]{:S(2)}, u32[]{:S(2)}) collective-permute-start(bf16[128,2304]{1,0:T(8,128)(2,1)S(1)} %ffn.4), channel_id=1, source_target_pairs={{1,65},{0,16},{3,67},{2,18},{5,69},{4,20},{7,71},{6,22},{9,73},{8,... | collective-permute-start | bytes 1769480 | tf_op jit(solution)/shard_map/ppermute | solution.py:456
  78.0 2.1 %collective-permute-done.4.refs_1_ = bf16[128,2304]{1,0:T(8,128)(2,1)S(1)} collective-permute-done((bf16[128,2304]{1,0:T(8,128)(2,1)S(1)}, bf16[128,2304]{1,0:T(8,128)(2,1)S(1)}, u32[]{:S(2)}, u32[]{:S(2)}) %collective-permute-start.4) | collective-permute-done | bytes 589856 | tf_op jit(solution)/shard_map/ppermute | solution.py:456
  80.1 0.6 collective-permute-done.3.refs_0_
  80.7 2.1 %ffn.5 = (bf16[128,2304]{1,0:T(8,128)(2,1)S(1)}, bf16[128,2304]{1,0:T(8,128)(2,1)S(1)}) custom-call(bf16[128,2304]{1,0:T(8,128)(2,1)S(1)} %collective-permute-done.3.refs_0_, bf16[128,2304]{1,0:T(8,128)(2,1)S(1)} %collective-permute-done.4.refs_1_, bf16[360,2304]{1,0:T(8,128)(2,1)S(1)} %bitcast.33, bf16[360,2304]{1,0:T(8,128)(2,1)S(1)} %bitcast.36, ...), custom_call_target="tpu_custom_call" | custom-call | flops 1274019840 | bytes 7335936 | tf_op jit(solution)/shard_map/ffn/pallas_call | solution.py:315
  82.8 0.9 collective-permute-start.5
  83.7 1.8 %collective-permute-start.6 = (bf16[128,2304]{1,0:T(8,128)(2,1)S(1)}, bf16[128,2304]{1,0:T(8,128)(2,1)S(1)}, u32[]{:S(2)}, u32[]{:S(2)}) collective-permute-start(bf16[128,2304]{1,0:T(8,128)(2,1)S(1)} %get-tuple-element.22), channel_id=1, source_target_pairs={{1,97},{0,24},{3,99},{2,26},{5,101},{4,28},{7,103},{6,30},{9,105},... | collective-permute-start | bytes 1769480 | tf_op jit(solution)/shard_map/ppermute | solution.py:456
  85.5 1.8 %collective-permute-done.2 = bf16[128,2304]{1,0:T(8,128)(2,1)S(1)} collective-permute-done((bf16[128,2304]{1,0:T(8,128)(2,1)S(1)}, bf16[128,2304]{1,0:T(8,128)(2,1)S(1)}, u32[]{:S(2)}, u32[]{:S(2)}) %collective-permute-start.2) | collective-permute-done | bytes 589856 | tf_op jit(solution)/shard_map/ppermute | solution.py:456
  87.5 6.2 %collective-permute-done.5 = bf16[128,2304]{1,0:T(8,128)(2,1)S(1)} collective-permute-done((bf16[128,2304]{1,0:T(8,128)(2,1)S(1)}, bf16[128,2304]{1,0:T(8,128)(2,1)S(1)}, u32[]{:S(2)}, u32[]{:S(2)}) %collective-permute-start.5) | collective-permute-done | bytes 589856 | tf_op jit(solution)/shard_map/ppermute | solution.py:456
  93.9 15.3 %all_to_all.23 = bf16[16,8,2304]{2,1,0:T(8,128)(2,1)S(1)} all-to-all(bf16[16,8,2304]{2,1,0:T(8,128)(2,1)S(1)} %fusion), channel_id=1, replica_groups={{1,3,5,7,9,11,13,15,17,19,21,23,25,27,29,31},{33,35,37,39,41,43,45,47,4..., dimensions={0} | all-to-all | bytes 1179648 | tf_op jit(solution)/shard_map/all_to_all | solution.py:468
  109.3 1.4 %collective-permute-done.7.back_ref = bf16[32,2304]{1,0:T(8,128)(2,1)S(1)} collective-permute-done((bf16[32,2304]{1,0:T(8,128)(2,1)S(1)}, bf16[32,2304]{1,0:T(8,128)(2,1)S(1)}, u32[]{:S(2)}, u32[]{:S(2)}) %collective-permute-start.7) | collective-permute-done | bytes 147488 | tf_op jit(solution)/shard_map/ppermute | solution.py:473
  110.7 1.5 %finish.1 = (bf16[1,4,2,2304]{3,2,1,0:T(2,128)(2,1)}, f32[2,4]{1,0:T(2,128)}) custom-call(s32[2,2,4]{2,1,0:T(2,128)S(1)} %bitcast.50, bf16[32,2304]{1,0:T(8,128)(2,1)S(1)} %bitcast_reduce_fusion.mine_ref, bf16[32,2304]{1,0:T(8,128)(2,1)S(1)} %collective-permute-done.7.back_ref, f32[8,2304]{1,0:T(8,128)S(1)} %get-tuple-element.26.mixed_ref, ...), custom_call_target="tpu_custom_call" | custom-call | tf_op jit(solution)/shard_map/finish/pallas_call | solution.py:368
  (43 shorter events, 0.7 us)
Async XLA Ops:
  0.6 20.2 %copy-start.3 = (bf16[4,64,2304]{2,1,0:T(8,128)(2,1)S(1)}, bf16[4,64,2304]{2,1,0:T(8,128)(2,1)}, u32[]{:S(2)}) copy-start(bf16[4,64,2304]{2,1,0:T(8,128)(2,1)} %k_ref.2) | copy-start | bytes 3538948
  1.5 19.3 %copy-start.10 = (s32[32,64]{1,0:T(8,128)S(1)}, s32[32,64]{1,0:T(8,128)}, u32[]{:S(2)}) copy-start(s32[32,64]{1,0:T(8,128)} %live.1) | copy-start | bytes 24580
  1.5 19.3 %copy-start.13 = (s32[16,32]{1,0:T(8,128)S(1)}, s32[16,32]{1,0:T(8,128)}, u32[]{:S(2)}) copy-start(s32[16,32]{1,0:T(8,128)} %tail_len.1) | copy-start | bytes 6148
  1.5 19.3 %copy-start.14 = (s32[16,32]{1,0:T(8,128)S(1)}, s32[16,32]{1,0:T(8,128)}, u32[]{:S(2)}) copy-start(s32[16,32]{1,0:T(8,128)} %source.1) | copy-start | bytes 6148
  1.5 19.3 %copy-start.16 = (s32[32]{0:T(128)S(1)}, s32[32]{0:T(128)}, u32[]{:S(2)}) copy-start(s32[32]{0:T(128)} %lengths.1) | copy-start | bytes 388
  20.8 46.6 %copy-start.2 = (bf16[1,360,2304]{2,1,0:T(8,128)(2,1)S(1)}, bf16[1,360,2304]{2,1,0:T(8,128)(2,1)}, u32[]{:S(2)}) copy-start(bf16[1,360,2304]{2,1,0:T(8,128)(2,1)} %param.36) | copy-start | bytes 4976644
  27.1 13.7 %copy-start.5 = (bf16[1,4,2,2304]{3,2,1,0:T(2,128)(2,1)S(1)}, bf16[1,4,2,2304]{3,2,1,0:T(2,128)(2,1)}, u32[]{:S(2)}) copy-start(bf16[1,4,2,2304]{3,2,1,0:T(2,128)(2,1)} %q_ref.3) | copy-start | bytes 110596
  27.1 13.7 %copy-start.6 = (f32[2304,8]{0,1:T(8,128)S(1)}, f32[2304,8]{0,1:T(8,128)}, u32[]{:S(2)}) copy-start(f32[2304,8]{0,1:T(8,128)} %param.32) | copy-start | bytes 221188
  27.1 13.7 %copy-start.7 = (bf16[1,4,2,2304]{3,2,1,0:T(2,128)(2,1)S(1)}, bf16[1,4,2,2304]{3,2,1,0:T(2,128)(2,1)}, u32[]{:S(2)}) copy-start(bf16[1,4,2,2304]{3,2,1,0:T(2,128)(2,1)} %k_ref.3) | copy-start | bytes 110596
  27.1 13.7 %copy-start.8 = (bf16[1,4,2,2304]{3,2,1,0:T(2,128)(2,1)S(1)}, bf16[1,4,2,2304]{3,2,1,0:T(2,128)(2,1)}, u32[]{:S(2)}) copy-start(bf16[1,4,2,2304]{3,2,1,0:T(2,128)(2,1)} %v_ref.1) | copy-start | bytes 110596
  27.2 13.7 %copy-start.9 = (bf16[1,4,2,2304]{3,2,1,0:T(2,128)(2,1)S(1)}, bf16[1,4,2,2304]{3,2,1,0:T(2,128)(2,1)}, u32[]{:S(2)}) copy-start(bf16[1,4,2,2304]{3,2,1,0:T(2,128)(2,1)} %h_ref.1) | copy-start | bytes 110596
  27.2 13.7 %copy-start.12 = (f32[2304]{0:T(1024)S(1)}, f32[2304]{0:T(1024)}, u32[]{:S(2)}) copy-start(f32[2304]{0:T(1024)} %param.33) | copy-start | bytes 27652
  27.2 13.7 %copy-start.15 = (s32[1,4,2,2]{1,3,2,0:T(2,128)S(1)}, s32[1,4,2,2]{1,3,2,0:T(2,128)}, u32[]{:S(2)}) copy-start(s32[1,4,2,2]{1,3,2,0:T(2,128)} %param.31) | copy-start | bytes 196
  27.2 40.2 %copy-start.1 = (bf16[1,2304,360]{1,2,0:T(8,128)(2,1)S(1)}, bf16[1,2304,360]{1,2,0:T(8,128)(2,1)}, u32[]{:S(2)}) copy-start(bf16[1,2304,360]{1,2,0:T(8,128)(2,1)} %param.35) | copy-start | bytes 4976644
  42.8 4.4 %collective-permute-start = (bf16[32,2304]{1,0:T(8,128)(2,1)S(1)}, bf16[32,2304]{1,0:T(8,128)(2,1)S(1)}, u32[]{:S(2)}, u32[]{:S(2)}) collective-permute-start(bf16[32,2304]{1,0:T(8,128)(2,1)S(1)} %get-tuple-element.16), channel_id=1, source_target_pairs={{0,1},{1,0},{2,3},{3,2},{4,5},{5,4},{6,7},{7,6},{8,9},{9,8},{10,11... | collective-permute-start | bytes 442376 | tf_op jit(solution)/shard_map/ppermute | solution.py:450
  46.1 21.3 %copy-start = (bf16[1,2304,360]{1,2,0:T(8,128)(2,1)S(1)}, bf16[1,2304,360]{1,2,0:T(8,128)(2,1)}, u32[]{:S(2)}) copy-start(bf16[1,2304,360]{1,2,0:T(8,128)(2,1)} %param.34) | copy-start | bytes 4976644
  64.1 10.3 %collective-permute-start.1 = (bf16[128,2304]{1,0:T(8,128)(2,1)S(1)}, bf16[128,2304]{1,0:T(8,128)(2,1)S(1)}, u32[]{:S(2)}, u32[]{:S(2)}) collective-permute-start(bf16[128,2304]{1,0:T(8,128)(2,1)S(1)} %bitcast.42), channel_id=1, source_target_pairs={{1,65},{0,16},{3,67},{2,18},{5,69},{4,20},{7,71},{6,22},{9,73},{8,... | collective-permute-start | bytes 1769480 | tf_op jit(solution)/shard_map/ppermute | solution.py:456
  65.8 14.4 %collective-permute-start.4 = (bf16[128,2304]{1,0:T(8,128)(2,1)S(1)}, bf16[128,2304]{1,0:T(8,128)(2,1)S(1)}, u32[]{:S(2)}, u32[]{:S(2)}) collective-permute-start(bf16[128,2304]{1,0:T(8,128)(2,1)S(1)} %bitcast.43), channel_id=1, source_target_pairs={{1,97},{0,24},{3,99},{2,26},{5,101},{4,28},{7,103},{6,30},{9,105},... | collective-permute-start | bytes 1769480 | tf_op jit(solution)/shard_map/ppermute | solution.py:456
  67.4 13.3 %collective-permute-start.3 = (bf16[128,2304]{1,0:T(8,128)(2,1)S(1)}, bf16[128,2304]{1,0:T(8,128)(2,1)S(1)}, u32[]{:S(2)}, u32[]{:S(2)}) collective-permute-start(bf16[128,2304]{1,0:T(8,128)(2,1)S(1)} %bitcast.44), channel_id=1, source_target_pairs={{1,33},{0,8},{3,35},{2,10},{5,37},{4,12},{7,39},{6,14},{9,41},{8,1... | collective-permute-start | bytes 1769480 | tf_op jit(solution)/shard_map/ppermute | solution.py:456
  76.1 11.3 %collective-permute-start.2 = (bf16[128,2304]{1,0:T(8,128)(2,1)S(1)}, bf16[128,2304]{1,0:T(8,128)(2,1)S(1)}, u32[]{:S(2)}, u32[]{:S(2)}) collective-permute-start(bf16[128,2304]{1,0:T(8,128)(2,1)S(1)} %ffn.4), channel_id=1, source_target_pairs={{1,65},{0,16},{3,67},{2,18},{5,69},{4,20},{7,71},{6,22},{9,73},{8,... | collective-permute-start | bytes 1769480 | tf_op jit(solution)/shard_map/ppermute | solution.py:456
  82.8 10.9 %collective-permute-start.5 = (bf16[128,2304]{1,0:T(8,128)(2,1)S(1)}, bf16[128,2304]{1,0:T(8,128)(2,1)S(1)}, u32[]{:S(2)}, u32[]{:S(2)}) collective-permute-start(bf16[128,2304]{1,0:T(8,128)(2,1)S(1)} %get-tuple-element.21), channel_id=1, source_target_pairs={{1,33},{0,8},{3,35},{2,10},{5,37},{4,12},{7,39},{6,14},{9,41},{8,1... | collective-permute-start | bytes 1769480 | tf_op jit(solution)/shard_map/ppermute | solution.py:456
  83.7 9.9 %collective-permute-start.6 = (bf16[128,2304]{1,0:T(8,128)(2,1)S(1)}, bf16[128,2304]{1,0:T(8,128)(2,1)S(1)}, u32[]{:S(2)}, u32[]{:S(2)}) collective-permute-start(bf16[128,2304]{1,0:T(8,128)(2,1)S(1)} %get-tuple-element.22), channel_id=1, source_target_pairs={{1,97},{0,24},{3,99},{2,26},{5,101},{4,28},{7,103},{6,30},{9,105},... | collective-permute-start | bytes 1769480 | tf_op jit(solution)/shard_map/ppermute | solution.py:456
  93.8 16.8 %copy-start.11 = (f32[2304]{0:T(1024)S(1)}, f32[2304]{0:T(1024)}, u32[]{:S(2)}) copy-start(f32[2304]{0:T(1024)} %param.37) | copy-start | bytes 27652
  109.2 1.5 %collective-permute-start.7 = (bf16[32,2304]{1,0:T(8,128)(2,1)S(1)}, bf16[32,2304]{1,0:T(8,128)(2,1)S(1)}, u32[]{:S(2)}, u32[]{:S(2)}) collective-permute-start(bf16[32,2304]{1,0:T(8,128)(2,1)S(1)} %bitcast_reduce_fusion.mine_ref), channel_id=1, source_target_pairs={{0,1},{1,0},{2,3},{3,2},{4,5},{5,4},{6,7},{7,6},{8,9},{9,8},{10,11... | collective-permute-start | bytes 442376 | tf_op jit(solution)/shard_map/ppermute | solution.py:473
  (1 other events, 0.9 us)

commit v6 on v5

--- a/solution.py
+++ b/solution.py
@@ -59,7 +59,7 @@
 
 
 def attend_kernel(
-    lengths, live, tail_len, source, q_ref, k_ref, tk_hbm, v_hbm, tv_hbm, out_ref,
+    lengths, live, tail_len, source, q_ref, k_ref, fresh_ref, tk_hbm, v_hbm, tv_hbm, out_ref, own_ref,
     tk_buf, v_buf, tv_buf, rows_in, rows_out, stats_in, score_buf, weight_buf, sems,
 ):
     prompts, span, model = k_ref.shape
@@ -82,6 +82,27 @@
             copy(p, i).start()
     for i in range(pairs):
         rows_in[i] = q_ref[:, i * LANES : (i + 1) * LANES].astype(F32)
+    own = pl.ds(pl.multiple_of(blk * group, group), group)
+    even = iota((group, LANES), 0) % fresh == 0
+    columns = iota((group, LANES), 1)
+    for u in range(fresh):
+        own_ref[u] = jnp.zeros((group, LANES), F32)
+    for i in range(pairs):
+        cut = slice(i * LANES, (i + 1) * LANES)
+        mine = rows_in[i, own, :]
+        for u in range(fresh):
+            key = jnp.concatenate(
+                [
+                    jnp.broadcast_to(fresh_ref[0, p, u : u + 1, cut].astype(F32), (fresh, LANES))
+                    for p in range(prompts)
+                ],
+                axis=0,
+            )
+            product = mine * key
+            low = jnp.sum(jnp.where(columns < HDIM, product, 0.0), axis=1, keepdims=True)
+            high = jnp.sum(jnp.where(columns < HDIM, 0.0, product), axis=1, keepdims=True)
+            score = jnp.where(columns == 2 * i, low, jnp.where(columns == 2 * i + 1, high, own_ref[u]))
+            own_ref[u] = jnp.where(even, HIDE, score) if u == 1 else score
     lane = iota((each, LANES), 1)
     sample = iota((each, LANES), 0) % samples
 
@@ -146,7 +167,7 @@
     out_ref[:, model:] = stats_in[...].astype(BF)
 
 
-def attend(lengths, live, tail_len, source, everyone, key, tail_key, value, tail_value):
+def attend(lengths, live, tail_len, source, everyone, key, new_key, tail_key, value, tail_value):
     rows, model = everyone.shape
     prompts, span, _ = key.shape
     pairs = model // LANES
@@ -154,9 +175,12 @@
     where = pl.BlockSpec(memory_space=pl.ANY)
     return pl.pallas_call(
         attend_kernel,
-        out_shape=jax.ShapeDtypeStruct((rows, model + LANES), BF),
-        in_specs=[smem()] * 4 + [vmem()] * 2 + [where] * 3,
-        out_specs=vmem(),
+        out_shape=(
+            jax.ShapeDtypeStruct((rows, model + LANES), BF),
+            jax.ShapeDtypeStruct((new_key.shape[2], new_key.shape[1] * new_key.shape[2], LANES), F32),
+        ),
+        in_specs=[smem()] * 4 + [vmem()] * 3 + [where] * 3,
+        out_specs=(vmem(), vmem()),
         scratch_shapes=[
             cache,
             cache,
@@ -170,7 +194,7 @@
         ],
         compiler_params=pltpu.CompilerParams(vmem_limit_bytes=ROOM),
         name="attend",
-    )(lengths, live, tail_len, source, everyone, key, tail_key, value, tail_value)
+    )(lengths, live, tail_len, source, everyone, key, new_key, tail_key, value, tail_value)
 
 
 def row_of(expert, core):
@@ -179,34 +203,25 @@
 
 
 def combine_kernel(
-    routes, got_ref, q_ref, k_ref, v_ref, h_ref, router_ref, gain_ref,
-    mixed_ref, rows_ref, gate_ref, q8, k0, k1, v0, v1, spread,
+    routes, got_ref, own_ref, v_ref, h_ref, router_ref, gain_ref,
+    mixed_ref, rows_ref, gate_ref, v0, v1, spread,
 ):
     parts, tokens, wide = got_ref.shape
     model = wide - LANES
     heads = model // HDIM
-    prompts, fresh = q_ref.shape[1], q_ref.shape[2]
+    prompts, fresh = v_ref.shape[1], v_ref.shape[2]
     experts = router_ref.shape[0]
     for p in range(prompts):
         at = slice(fresh * p, fresh * (p + 1))
-        q8[at, :] = q_ref[0, p].astype(F32)
         mixed_ref[at, :] = h_ref[0, p].astype(F32)
-        key, val = k_ref[0, p].astype(F32), v_ref[0, p].astype(F32)
-        k0[at, :] = jnp.broadcast_to(key[0:1], (fresh, model))
-        k1[at, :] = jnp.broadcast_to(key[1:2], (fresh, model))
+        val = v_ref[0, p].astype(F32)
         v0[at, :] = jnp.broadcast_to(val[0:1], (fresh, model))
         v1[at, :] = jnp.broadcast_to(val[1:2], (fresh, model))
     spread[...] = jnp.where(
         iota((LANES, model), 1) // HDIM == iota((LANES, model), 0), 1.0, 0.0
     ).astype(BF)
-    product = jnp.concatenate([q8[...] * k0[...], q8[...] * k1[...]], axis=0)
-    high = product.astype(BF)
-    low = (product - high.astype(F32)).astype(BF)
-    own = (dot(high, spread[...], NT) + dot(low, spread[...], NT)) * 0.125
     lane = iota((tokens, LANES), 1)
-    sub = iota((tokens, LANES), 0)
-    s0 = own[:tokens]
-    s1 = jnp.where(sub % fresh == 1, own[tokens:], HIDE)
+    s0, s1 = own_ref[0], own_ref[1]
     top = jnp.maximum(s0, s1)
     tops, sums = [], []
     for j in range(parts):
@@ -278,7 +293,7 @@
     rows_ref[...] = dot(pick, normed).astype(BF)
 
 
-def combine(routes, got, query, new_key, new_value, hidden, router, gain):
+def combine(routes, got, own, new_value, hidden, router, gain):
     parts, tokens, wide = got.shape
     model = wide - LANES
     experts = router.shape[0]
@@ -289,12 +304,12 @@
             jax.ShapeDtypeStruct((experts * CAP, model), BF),
             jax.ShapeDtypeStruct((tokens, LANES), F32),
         ),
-        in_specs=[smem()] + [vmem()] * 7,
+        in_specs=[smem()] + [vmem()] * 6,
         out_specs=(vmem(), vmem(), vmem()),
-        scratch_shapes=[pltpu.VMEM((tokens, model), F32)] * 5 + [pltpu.VMEM((LANES, model), BF)],
+        scratch_shapes=[pltpu.VMEM((tokens, model), F32)] * 2 + [pltpu.VMEM((LANES, model), BF)],
         compiler_params=pltpu.CompilerParams(vmem_limit_bytes=16 << 20),
         name="combine",
-    )(routes, got, query, new_key, new_value, hidden, router, gain)
+    )(routes, got, own, new_value, hidden, router, gain)
 
 
 def ffn(xs, weights):
@@ -408,20 +423,21 @@
     tokens = prompts * fresh
     everyone = exchange(share(query, blk_count), "blk")
     chosen = routes[0].transpose(1, 2, 0)
-    sent = attend(
+    sent, own_scores = attend(
         prompt_len,
         live_blocks,
         tail_len,
         tail_source,
         everyone.reshape(blk_count * tokens, model),
         prompt_key,
+        new_key,
         tail_key[0],
         prompt_value,
         tail_value[0],
     )
     got = exchange(sent.reshape(blk_count, tokens, -1), "blk")
     mixed, outgoing, gates = combine(
-        chosen, got, query, new_key, new_value, hidden, router.T, ffn_gain.reshape(-1, LANES)
+        chosen, got, own_scores, new_value, hidden, router.T, ffn_gain.reshape(-1, LANES)
     )
     exp_count = lax.axis_size("expert")
     both = ("blk", "expert")

time: 113 us -> 112 us (level)
  no operation moved by 1% of the time
where the time goes in v6:
time: 112 us
  blocking collectives  64.9 us (58%)
  waiting for transfers between devices  18.5 us (17%)
  Pallas kernels  14.7 us (13%)
  starting transfers between devices  11.4 us (10%)
    all_to_all x2, blocking collectives, exchange(): return lax.all_to_all(x, axis, 0, 0, tiled=True)  32.8 us
    all_to_all x1, blocking collectives, local(): rows = lax.all_to_all(rows, both, 0, 0, tiled=True, axis_index_groups=lines)  16.9 us
    ppermute x6, waiting for transfers between devices, local(): send = lambda x, step: lax.ppermute(x, both, shift(step))  16.1 us
    all_to_all x1, blocking collectives, local(): lax.all_to_all(total.reshape(-1, 2 * CAP, model), both, 0, 0, tiled=True,...  15.3 us
    ppermute x6, starting transfers between devices, local(): send = lambda x, step: lax.ppermute(x, both, shift(step))  7.97 us
    pallas_call x1, Pallas kernels, attend(): pl.pallas_call(attend_kernel, out_shape=(jax.ShapeDtypeStruct((rows, mode...  6.4 us
    pallas_call x3, Pallas kernels, ffn(): pl.pallas_call(kernel, out_shape=(jax.ShapeDtypeStruct((rows, model), BF)...  5.28 us
    ppermute x1, starting transfers between devices, local(): lax.ppermute(outgoing, 'expert', swap).reshape(wide)  3.35 us
  transfers between devices with their start and end apart: 8, of which 7 were waited for; matrix products, arithmetic and copies ran while one was open for 0% of the time, Pallas kernels for 5%

profile of v6, /device:TPU:1, one launch (start us, length us, event | category | flops | bytes accessed | tf_op | source)
XLA Modules:
  0.0 111.9 jit_solution(1789494321872156813)
XLA Ops:
  0.7 0.9 copy-done.6
  1.6 19.2 %all_to_all.20 = bf16[16,8,2304]{2,1,0:T(8,128)(2,1)S(1)} all-to-all(bf16[16,8,2304]{2,1,0:T(8,128)(2,1)S(1)} %share.1), channel_id=1, replica_groups=mesh['blk'=16,'expert'=8] {'blk'}, dimensions={0} | all-to-all | bytes 1179648 | tf_op jit(solution)/shard_map/all_to_all | solution.py:397
  20.8 6.4 %attend.1 = (bf16[128,2432]{1,0:T(8,128)(2,1)S(1)}, f32[2,8,128]{2,1,0:T(8,128)S(1)}) custom-call(s32[32]{0:T(128)S(1)} %copy-done.15, s32[32,64]{1,0:T(8,128)S(1)} %copy-done.9, s32[16,32]{1,0:T(8,128)S(1)} %copy-done.12, s32[16,32]{1,0:T(8,128)S(1)} %copy-done.13, bf16[128,2304]{1,0:T(8,128)(2,1)S(1)} %bitcast.40, bf16[4,64,2304]{2,1,0:T(8,128)(2,1)S(1)} %copy-done.3, ...), custom_call_target="tpu_custom_call" | custom-call | tf_op jit(solution)/shard_map/attend/pallas_call | solution.py:176
  27.3 13.6 %all_to_all.21.got_ref = bf16[16,8,2432]{2,1,0:T(8,128)(2,1)S(1)} all-to-all(bf16[16,8,2432]{2,1,0:T(8,128)(2,1)S(1)} %bitcast.45), channel_id=1, replica_groups=mesh['blk'=16,'expert'=8] {'blk'}, dimensions={0} | all-to-all | bytes 1245184 | tf_op jit(solution)/shard_map/all_to_all | solution.py:397
  41.0 1.5 %combine.1 = (f32[8,2304]{1,0:T(8,128)S(1)}, bf16[32,2304]{1,0:T(8,128)(2,1)S(1)}, f32[8,128]{1,0:T(8,128)S(1)}) custom-call(s32[2,2,4]{2,1,0:T(2,128)S(1)} %bitcast.49, bf16[16,8,2432]{2,1,0:T(8,128)(2,1)S(1)} %all_to_all.21.got_ref, f32[2,8,128]{2,1,0:T(8,128)S(1)} %get-tuple-element.19.own_ref, bf16[1,4,2,2304]{3,2,1,0:T(2,128)(2,1)S(1)} %copy-done.7, ...), custom_call_target="tpu_custom_call" | custom-call | tf_op jit(solution)/shard_map/combine/pallas_call | solution.py:300
  42.5 3.4 %collective-permute-start = (bf16[32,2304]{1,0:T(8,128)(2,1)S(1)}, bf16[32,2304]{1,0:T(8,128)(2,1)S(1)}, u32[]{:S(2)}, u32[]{:S(2)}) collective-permute-start(bf16[32,2304]{1,0:T(8,128)(2,1)S(1)} %get-tuple-element.20), channel_id=1, source_target_pairs={{0,1},{1,0},{2,3},{3,2},{4,5},{5,4},{6,7},{7,6},{8,9},{9,8},{10,11... | collective-permute-start | bytes 442376 | tf_op jit(solution)/shard_map/ppermute | solution.py:466
  45.8 1.0 collective-permute-done
  47.0 16.9 %all_to_all.22 = bf16[16,8,2304]{2,1,0:T(8,128)(2,1)S(1)} all-to-all(bf16[16,8,2304]{2,1,0:T(8,128)(2,1)S(1)} %bitcast.51), channel_id=1, replica_groups={{1,3,5,7,9,11,13,15,17,19,21,23,25,27,29,31},{33,35,37,39,41,43,45,47,4..., dimensions={0} | all-to-all | bytes 1179648 | tf_op jit(solution)/shard_map/all_to_all | solution.py:469
  63.8 1.6 %collective-permute-start.1 = (bf16[128,2304]{1,0:T(8,128)(2,1)S(1)}, bf16[128,2304]{1,0:T(8,128)(2,1)S(1)}, u32[]{:S(2)}, u32[]{:S(2)}) collective-permute-start(bf16[128,2304]{1,0:T(8,128)(2,1)S(1)} %bitcast.41), channel_id=1, source_target_pairs={{1,65},{0,16},{3,67},{2,18},{5,69},{4,20},{7,71},{6,22},{9,73},{8,... | collective-permute-start | bytes 1769480 | tf_op jit(solution)/shard_map/ppermute | solution.py:472
  65.5 1.7 %collective-permute-start.4 = (bf16[128,2304]{1,0:T(8,128)(2,1)S(1)}, bf16[128,2304]{1,0:T(8,128)(2,1)S(1)}, u32[]{:S(2)}, u32[]{:S(2)}) collective-permute-start(bf16[128,2304]{1,0:T(8,128)(2,1)S(1)} %bitcast.42), channel_id=1, source_target_pairs={{1,97},{0,24},{3,99},{2,26},{5,101},{4,28},{7,103},{6,30},{9,105},... | collective-permute-start | bytes 1769480 | tf_op jit(solution)/shard_map/ppermute | solution.py:472
  67.1 1.6 %ffn.3 = bf16[128,2304]{1,0:T(8,128)(2,1)S(1)} custom-call(bf16[128,2304]{1,0:T(8,128)(2,1)S(1)} %bitcast.44, bf16[360,2304]{1,0:T(8,128)(2,1)S(1)} %bitcast.31, bf16[360,2304]{1,0:T(8,128)(2,1)S(1)} %bitcast.34, bf16[360,2304]{1,0:T(8,128)(2,1)S(1)} %bitcast.37), custom_call_target="tpu_custom_call" | custom-call | flops 637009920 | bytes 6156288 | tf_op jit(solution)/shard_map/ffn/pallas_call | solution.py:330
  68.7 5.4 %collective-permute-done.1.refs_0_ = bf16[128,2304]{1,0:T(8,128)(2,1)S(1)} collective-permute-done((bf16[128,2304]{1,0:T(8,128)(2,1)S(1)}, bf16[128,2304]{1,0:T(8,128)(2,1)S(1)}, u32[]{:S(2)}, u32[]{:S(2)}) %collective-permute-start.1) | collective-permute-done | bytes 589856 | tf_op jit(solution)/shard_map/ppermute | solution.py:472
  74.2 1.6 %ffn.4 = bf16[128,2304]{1,0:T(8,128)(2,1)S(1)} custom-call(bf16[128,2304]{1,0:T(8,128)(2,1)S(1)} %collective-permute-done.1.refs_0_, bf16[360,2304]{1,0:T(8,128)(2,1)S(1)} %bitcast.32, bf16[360,2304]{1,0:T(8,128)(2,1)S(1)} %bitcast.35, bf16[360,2304]{1,0:T(8,128)(2,1)S(1)} %bitcast.38), custom_call_target="tpu_custom_call" | custom-call | flops 637009920 | bytes 6156288 | tf_op jit(solution)/shard_map/ffn/pallas_call | solution.py:330
  75.8 1.9 %collective-permute-start.2 = (bf16[128,2304]{1,0:T(8,128)(2,1)S(1)}, bf16[128,2304]{1,0:T(8,128)(2,1)S(1)}, u32[]{:S(2)}, u32[]{:S(2)}) collective-permute-start(bf16[128,2304]{1,0:T(8,128)(2,1)S(1)} %ffn.4), channel_id=1, source_target_pairs={{1,65},{0,16},{3,67},{2,18},{5,69},{4,20},{7,71},{6,22},{9,73},{8,... | collective-permute-start | bytes 1769480 | tf_op jit(solution)/shard_map/ppermute | solution.py:472
  77.7 2.1 %collective-permute-done.4.refs_1_ = bf16[128,2304]{1,0:T(8,128)(2,1)S(1)} collective-permute-done((bf16[128,2304]{1,0:T(8,128)(2,1)S(1)}, bf16[128,2304]{1,0:T(8,128)(2,1)S(1)}, u32[]{:S(2)}, u32[]{:S(2)}) %collective-permute-start.4) | collective-permute-done | bytes 589856 | tf_op jit(solution)/shard_map/ppermute | solution.py:472
  79.8 0.6 collective-permute-done.3.refs_0_
  80.4 2.1 %ffn.5 = (bf16[128,2304]{1,0:T(8,128)(2,1)S(1)}, bf16[128,2304]{1,0:T(8,128)(2,1)S(1)}) custom-call(bf16[128,2304]{1,0:T(8,128)(2,1)S(1)} %collective-permute-done.3.refs_0_, bf16[128,2304]{1,0:T(8,128)(2,1)S(1)} %collective-permute-done.4.refs_1_, bf16[360,2304]{1,0:T(8,128)(2,1)S(1)} %bitcast.33, bf16[360,2304]{1,0:T(8,128)(2,1)S(1)} %bitcast.36, ...), custom_call_target="tpu_custom_call" | custom-call | flops 1274019840 | bytes 7335936 | tf_op jit(solution)/shard_map/ffn/pallas_call | solution.py:330
  82.5 0.9 collective-permute-start.5
  83.4 1.8 %collective-permute-start.6 = (bf16[128,2304]{1,0:T(8,128)(2,1)S(1)}, bf16[128,2304]{1,0:T(8,128)(2,1)S(1)}, u32[]{:S(2)}, u32[]{:S(2)}) collective-permute-start(bf16[128,2304]{1,0:T(8,128)(2,1)S(1)} %get-tuple-element.26), channel_id=1, source_target_pairs={{1,97},{0,24},{3,99},{2,26},{5,101},{4,28},{7,103},{6,30},{9,105},... | collective-permute-start | bytes 1769480 | tf_op jit(solution)/shard_map/ppermute | solution.py:472
  85.2 1.8 %collective-permute-done.2 = bf16[128,2304]{1,0:T(8,128)(2,1)S(1)} collective-permute-done((bf16[128,2304]{1,0:T(8,128)(2,1)S(1)}, bf16[128,2304]{1,0:T(8,128)(2,1)S(1)}, u32[]{:S(2)}, u32[]{:S(2)}) %collective-permute-start.2) | collective-permute-done | bytes 589856 | tf_op jit(solution)/shard_map/ppermute | solution.py:472
  87.2 6.2 %collective-permute-done.5 = bf16[128,2304]{1,0:T(8,128)(2,1)S(1)} collective-permute-done((bf16[128,2304]{1,0:T(8,128)(2,1)S(1)}, bf16[128,2304]{1,0:T(8,128)(2,1)S(1)}, u32[]{:S(2)}, u32[]{:S(2)}) %collective-permute-start.5) | collective-permute-done | bytes 589856 | tf_op jit(solution)/shard_map/ppermute | solution.py:472
  93.6 15.3 %all_to_all.23 = bf16[16,8,2304]{2,1,0:T(8,128)(2,1)S(1)} all-to-all(bf16[16,8,2304]{2,1,0:T(8,128)(2,1)S(1)} %fusion), channel_id=1, replica_groups={{1,3,5,7,9,11,13,15,17,19,21,23,25,27,29,31},{33,35,37,39,41,43,45,47,4..., dimensions={0} | all-to-all | bytes 1179648 | tf_op jit(solution)/shard_map/all_to_all | solution.py:484
  109.0 1.4 %collective-permute-done.7.back_ref = bf16[32,2304]{1,0:T(8,128)(2,1)S(1)} collective-permute-done((bf16[32,2304]{1,0:T(8,128)(2,1)S(1)}, bf16[32,2304]{1,0:T(8,128)(2,1)S(1)}, u32[]{:S(2)}, u32[]{:S(2)}) %collective-permute-start.7) | collective-permute-done | bytes 147488 | tf_op jit(solution)/shard_map/ppermute | solution.py:489
  110.4 1.5 %finish.1 = (bf16[1,4,2,2304]{3,2,1,0:T(2,128)(2,1)}, f32[2,4]{1,0:T(2,128)}) custom-call(s32[2,2,4]{2,1,0:T(2,128)S(1)} %bitcast.50, bf16[32,2304]{1,0:T(8,128)(2,1)S(1)} %bitcast_reduce_fusion.mine_ref, bf16[32,2304]{1,0:T(8,128)(2,1)S(1)} %collective-permute-done.7.back_ref, f32[8,2304]{1,0:T(8,128)S(1)} %get-tuple-element.30.mixed_ref, ...), custom_call_target="tpu_custom_call" | custom-call | tf_op jit(solution)/shard_map/finish/pallas_call | solution.py:383
  (41 shorter events, 0.7 us)
Async XLA Ops:
  0.6 20.2 %copy-start.3 = (bf16[4,64,2304]{2,1,0:T(8,128)(2,1)S(1)}, bf16[4,64,2304]{2,1,0:T(8,128)(2,1)}, u32[]{:S(2)}) copy-start(bf16[4,64,2304]{2,1,0:T(8,128)(2,1)} %k_ref.1) | copy-start | bytes 3538948
  0.6 20.2 %copy-start.5 = (bf16[1,4,2,2304]{3,2,1,0:T(2,128)(2,1)S(1)}, bf16[1,4,2,2304]{3,2,1,0:T(2,128)(2,1)}, u32[]{:S(2)}) copy-start(bf16[1,4,2,2304]{3,2,1,0:T(2,128)(2,1)} %fresh_ref.1) | copy-start | bytes 110596
  0.7 0.9 copy-start.6
  1.5 19.3 %copy-start.9 = (s32[32,64]{1,0:T(8,128)S(1)}, s32[32,64]{1,0:T(8,128)}, u32[]{:S(2)}) copy-start(s32[32,64]{1,0:T(8,128)} %live.1) | copy-start | bytes 24580
  1.5 19.3 %copy-start.12 = (s32[16,32]{1,0:T(8,128)S(1)}, s32[16,32]{1,0:T(8,128)}, u32[]{:S(2)}) copy-start(s32[16,32]{1,0:T(8,128)} %tail_len.1) | copy-start | bytes 6148
  1.5 19.3 %copy-start.13 = (s32[16,32]{1,0:T(8,128)S(1)}, s32[16,32]{1,0:T(8,128)}, u32[]{:S(2)}) copy-start(s32[16,32]{1,0:T(8,128)} %source.1) | copy-start | bytes 6148
  1.5 19.3 %copy-start.15 = (s32[32]{0:T(128)S(1)}, s32[32]{0:T(128)}, u32[]{:S(2)}) copy-start(s32[32]{0:T(128)} %lengths.1) | copy-start | bytes 388
  20.8 46.3 %copy-start.2 = (bf16[1,360,2304]{2,1,0:T(8,128)(2,1)S(1)}, bf16[1,360,2304]{2,1,0:T(8,128)(2,1)}, u32[]{:S(2)}) copy-start(bf16[1,360,2304]{2,1,0:T(8,128)(2,1)} %param.36) | copy-start | bytes 4976644
  27.3 13.7 %copy-start.4 = (f32[2304,8]{0,1:T(8,128)S(1)}, f32[2304,8]{0,1:T(8,128)}, u32[]{:S(2)}) copy-start(f32[2304,8]{0,1:T(8,128)} %param.32) | copy-start | bytes 221188
  27.3 13.7 %copy-start.7 = (bf16[1,4,2,2304]{3,2,1,0:T(2,128)(2,1)S(1)}, bf16[1,4,2,2304]{3,2,1,0:T(2,128)(2,1)}, u32[]{:S(2)}) copy-start(bf16[1,4,2,2304]{3,2,1,0:T(2,128)(2,1)} %v_ref.1) | copy-start | bytes 110596
  27.3 13.7 %copy-start.8 = (bf16[1,4,2,2304]{3,2,1,0:T(2,128)(2,1)S(1)}, bf16[1,4,2,2304]{3,2,1,0:T(2,128)(2,1)}, u32[]{:S(2)}) copy-start(bf16[1,4,2,2304]{3,2,1,0:T(2,128)(2,1)} %h_ref.1) | copy-start | bytes 110596
  27.3 13.7 %copy-start.11 = (f32[2304]{0:T(1024)S(1)}, f32[2304]{0:T(1024)}, u32[]{:S(2)}) copy-start(f32[2304]{0:T(1024)} %param.33) | copy-start | bytes 27652
  27.3 13.7 %copy-start.14 = (s32[1,4,2,2]{1,3,2,0:T(2,128)S(1)}, s32[1,4,2,2]{1,3,2,0:T(2,128)}, u32[]{:S(2)}) copy-start(s32[1,4,2,2]{1,3,2,0:T(2,128)} %param.31) | copy-start | bytes 196
  27.3 39.8 %copy-start.1 = (bf16[1,2304,360]{1,2,0:T(8,128)(2,1)S(1)}, bf16[1,2304,360]{1,2,0:T(8,128)(2,1)}, u32[]{:S(2)}) copy-start(bf16[1,2304,360]{1,2,0:T(8,128)(2,1)} %param.35) | copy-start | bytes 4976644
  42.5 4.4 %collective-permute-start = (bf16[32,2304]{1,0:T(8,128)(2,1)S(1)}, bf16[32,2304]{1,0:T(8,128)(2,1)S(1)}, u32[]{:S(2)}, u32[]{:S(2)}) collective-permute-start(bf16[32,2304]{1,0:T(8,128)(2,1)S(1)} %get-tuple-element.20), channel_id=1, source_target_pairs={{0,1},{1,0},{2,3},{3,2},{4,5},{5,4},{6,7},{7,6},{8,9},{9,8},{10,11... | collective-permute-start | bytes 442376 | tf_op jit(solution)/shard_map/ppermute | solution.py:466
  45.8 21.3 %copy-start = (bf16[1,2304,360]{1,2,0:T(8,128)(2,1)S(1)}, bf16[1,2304,360]{1,2,0:T(8,128)(2,1)}, u32[]{:S(2)}) copy-start(bf16[1,2304,360]{1,2,0:T(8,128)(2,1)} %param.34) | copy-start | bytes 4976644
  63.8 10.3 %collective-permute-start.1 = (bf16[128,2304]{1,0:T(8,128)(2,1)S(1)}, bf16[128,2304]{1,0:T(8,128)(2,1)S(1)}, u32[]{:S(2)}, u32[]{:S(2)}) collective-permute-start(bf16[128,2304]{1,0:T(8,128)(2,1)S(1)} %bitcast.41), channel_id=1, source_target_pairs={{1,65},{0,16},{3,67},{2,18},{5,69},{4,20},{7,71},{6,22},{9,73},{8,... | collective-permute-start | bytes 1769480 | tf_op jit(solution)/shard_map/ppermute | solution.py:472
  65.5 14.4 %collective-permute-start.4 = (bf16[128,2304]{1,0:T(8,128)(2,1)S(1)}, bf16[128,2304]{1,0:T(8,128)(2,1)S(1)}, u32[]{:S(2)}, u32[]{:S(2)}) collective-permute-start(bf16[128,2304]{1,0:T(8,128)(2,1)S(1)} %bitcast.42), channel_id=1, source_target_pairs={{1,97},{0,24},{3,99},{2,26},{5,101},{4,28},{7,103},{6,30},{9,105},... | collective-permute-start | bytes 1769480 | tf_op jit(solution)/shard_map/ppermute | solution.py:472
  67.1 13.3 %collective-permute-start.3 = (bf16[128,2304]{1,0:T(8,128)(2,1)S(1)}, bf16[128,2304]{1,0:T(8,128)(2,1)S(1)}, u32[]{:S(2)}, u32[]{:S(2)}) collective-permute-start(bf16[128,2304]{1,0:T(8,128)(2,1)S(1)} %bitcast.43), channel_id=1, source_target_pairs={{1,33},{0,8},{3,35},{2,10},{5,37},{4,12},{7,39},{6,14},{9,41},{8,1... | collective-permute-start | bytes 1769480 | tf_op jit(solution)/shard_map/ppermute | solution.py:472
  75.8 11.3 %collective-permute-start.2 = (bf16[128,2304]{1,0:T(8,128)(2,1)S(1)}, bf16[128,2304]{1,0:T(8,128)(2,1)S(1)}, u32[]{:S(2)}, u32[]{:S(2)}) collective-permute-start(bf16[128,2304]{1,0:T(8,128)(2,1)S(1)} %ffn.4), channel_id=1, source_target_pairs={{1,65},{0,16},{3,67},{2,18},{5,69},{4,20},{7,71},{6,22},{9,73},{8,... | collective-permute-start | bytes 1769480 | tf_op jit(solution)/shard_map/ppermute | solution.py:472
  82.5 10.9 %collective-permute-start.5 = (bf16[128,2304]{1,0:T(8,128)(2,1)S(1)}, bf16[128,2304]{1,0:T(8,128)(2,1)S(1)}, u32[]{:S(2)}, u32[]{:S(2)}) collective-permute-start(bf16[128,2304]{1,0:T(8,128)(2,1)S(1)} %get-tuple-element.25), channel_id=1, source_target_pairs={{1,33},{0,8},{3,35},{2,10},{5,37},{4,12},{7,39},{6,14},{9,41},{8,1... | collective-permute-start | bytes 1769480 | tf_op jit(solution)/shard_map/ppermute | solution.py:472
  83.4 9.9 %collective-permute-start.6 = (bf16[128,2304]{1,0:T(8,128)(2,1)S(1)}, bf16[128,2304]{1,0:T(8,128)(2,1)S(1)}, u32[]{:S(2)}, u32[]{:S(2)}) collective-permute-start(bf16[128,2304]{1,0:T(8,128)(2,1)S(1)} %get-tuple-element.26), channel_id=1, source_target_pairs={{1,97},{0,24},{3,99},{2,26},{5,101},{4,28},{7,103},{6,30},{9,105},... | collective-permute-start | bytes 1769480 | tf_op jit(solution)/shard_map/ppermute | solution.py:472
  93.5 16.8 %copy-start.10 = (f32[2304]{0:T(1024)S(1)}, f32[2304]{0:T(1024)}, u32[]{:S(2)}) copy-start(f32[2304]{0:T(1024)} %param.37) | copy-start | bytes 27652
  108.9 1.5 %collective-permute-start.7 = (bf16[32,2304]{1,0:T(8,128)(2,1)S(1)}, bf16[32,2304]{1,0:T(8,128)(2,1)S(1)}, u32[]{:S(2)}, u32[]{:S(2)}) collective-permute-start(bf16[32,2304]{1,0:T(8,128)(2,1)S(1)} %bitcast_reduce_fusion.mine_ref), channel_id=1, source_target_pairs={{0,1},{1,0},{2,3},{3,2},{4,5},{5,4},{6,7},{7,6},{8,9},{9,8},{10,11... | collective-permute-start | bytes 442376 | tf_op jit(solution)/shard_map/ppermute | solution.py:489

commit v7 on v6

--- a/solution.py
+++ b/solution.py
@@ -470,17 +470,17 @@
     rows = rows.reshape(-1, model)
     weights = (w_gate[0].T, w_up[0].T, w_down[0])
     send = lambda x, step: lax.ppermute(x, both, shift(step))
-    far, before, after = send(rows, 2), send(rows, 1), send(rows, 3)
+    far, after, before = send(rows, 2), send(rows, 3), send(rows, 1)
     (own,) = ffn((rows,), weights)
     far, own = lax.optimization_barrier((far, own))
     (far,) = ffn((far,), weights)
     home = send(far, -2)
-    before, after, _ = lax.optimization_barrier((before, after, far))
-    before, after = ffn((before, after), weights)
-    after, before = send(after, -3), send(before, -1)
+    after, before, _ = lax.optimization_barrier((after, before, far))
+    after, before = ffn((after, before), weights)
+    before, after = send(before, -1), send(after, -3)
     partial = own.astype(F32) + home.astype(F32)
-    partial, after, before = lax.optimization_barrier((partial, after, before))
-    total = (partial + after.astype(F32) + before.astype(F32)).astype(BF)
+    partial, before, after = lax.optimization_barrier((partial, before, after))
+    total = (partial + before.astype(F32) + after.astype(F32)).astype(BF)
     total = lax.all_to_all(
         total.reshape(-1, 2 * CAP, model), both, 0, 0, tiled=True, axis_index_groups=lines
     )

time: 112 us -> 112 us (level)
  no operation moved by 1% of the time
where the time goes in v7:
time: 112 us
  blocking collectives  63.9 us (57%)
  waiting for transfers between devices  19.5 us (17%)
  Pallas kernels  14.7 us (13%)
  starting transfers between devices  11.6 us (10%)
    all_to_all x2, blocking collectives, exchange(): return lax.all_to_all(x, axis, 0, 0, tiled=True)  32.8 us
    ppermute x6, waiting for transfers between devices, local(): send = lambda x, step: lax.ppermute(x, both, shift(step))  17.2 us
    all_to_all x1, blocking collectives, local(): rows = lax.all_to_all(rows, both, 0, 0, tiled=True, axis_index_groups=lines)  16.9 us
    all_to_all x1, blocking collectives, local(): lax.all_to_all(total.reshape(-1, 2 * CAP, model), both, 0, 0, tiled=True,...  14.3 us
    ppermute x6, starting transfers between devices, local(): send = lambda x, step: lax.ppermute(x, both, shift(step))  8.1 us
    pallas_call x1, Pallas kernels, attend(): pl.pallas_call(attend_kernel, out_shape=(jax.ShapeDtypeStruct((rows, mode...  6.4 us
    pallas_call x3, Pallas kernels, ffn(): pl.pallas_call(kernel, out_shape=(jax.ShapeDtypeStruct((rows, model), BF)...  5.28 us
    ppermute x1, starting transfers between devices, local(): lax.ppermute(outgoing, 'expert', swap).reshape(wide)  3.35 us
  transfers between devices with their start and end apart: 8, of which 7 were waited for; matrix products, arithmetic and copies ran while one was open for 0% of the time, Pallas kernels for 5%

profile of v7, /device:TPU:1, one launch (start us, length us, event | category | flops | bytes accessed | tf_op | source)
XLA Modules:
  0.0 112.1 jit_solution(6674416442891442322)
XLA Ops:
  0.7 0.9 copy-done.6
  1.6 19.2 %all_to_all.20 = bf16[16,8,2304]{2,1,0:T(8,128)(2,1)S(1)} all-to-all(bf16[16,8,2304]{2,1,0:T(8,128)(2,1)S(1)} %share.1), channel_id=1, replica_groups=mesh['blk'=16,'expert'=8] {'blk'}, dimensions={0} | all-to-all | bytes 1179648 | tf_op jit(solution)/shard_map/all_to_all | solution.py:397
  20.8 6.4 %attend.1 = (bf16[128,2432]{1,0:T(8,128)(2,1)S(1)}, f32[2,8,128]{2,1,0:T(8,128)S(1)}) custom-call(s32[32]{0:T(128)S(1)} %copy-done.15, s32[32,64]{1,0:T(8,128)S(1)} %copy-done.9, s32[16,32]{1,0:T(8,128)S(1)} %copy-done.12, s32[16,32]{1,0:T(8,128)S(1)} %copy-done.13, bf16[128,2304]{1,0:T(8,128)(2,1)S(1)} %bitcast.40, bf16[4,64,2304]{2,1,0:T(8,128)(2,1)S(1)} %copy-done.3, ...), custom_call_target="tpu_custom_call" | custom-call | tf_op jit(solution)/shard_map/attend/pallas_call | solution.py:176
  27.3 13.6 %all_to_all.21.got_ref = bf16[16,8,2432]{2,1,0:T(8,128)(2,1)S(1)} all-to-all(bf16[16,8,2432]{2,1,0:T(8,128)(2,1)S(1)} %bitcast.45), channel_id=1, replica_groups=mesh['blk'=16,'expert'=8] {'blk'}, dimensions={0} | all-to-all | bytes 1245184 | tf_op jit(solution)/shard_map/all_to_all | solution.py:397
  41.0 1.5 %combine.1 = (f32[8,2304]{1,0:T(8,128)S(1)}, bf16[32,2304]{1,0:T(8,128)(2,1)S(1)}, f32[8,128]{1,0:T(8,128)S(1)}) custom-call(s32[2,2,4]{2,1,0:T(2,128)S(1)} %bitcast.49, bf16[16,8,2432]{2,1,0:T(8,128)(2,1)S(1)} %all_to_all.21.got_ref, f32[2,8,128]{2,1,0:T(8,128)S(1)} %get-tuple-element.19.own_ref, bf16[1,4,2,2304]{3,2,1,0:T(2,128)(2,1)S(1)} %copy-done.7, ...), custom_call_target="tpu_custom_call" | custom-call | tf_op jit(solution)/shard_map/combine/pallas_call | solution.py:300
  42.5 3.4 %collective-permute-start = (bf16[32,2304]{1,0:T(8,128)(2,1)S(1)}, bf16[32,2304]{1,0:T(8,128)(2,1)S(1)}, u32[]{:S(2)}, u32[]{:S(2)}) collective-permute-start(bf16[32,2304]{1,0:T(8,128)(2,1)S(1)} %get-tuple-element.20), channel_id=1, source_target_pairs={{0,1},{1,0},{2,3},{3,2},{4,5},{5,4},{6,7},{7,6},{8,9},{9,8},{10,11... | collective-permute-start | bytes 442376 | tf_op jit(solution)/shard_map/ppermute | solution.py:466
  45.8 1.0 collective-permute-done
  47.0 16.9 %all_to_all.22 = bf16[16,8,2304]{2,1,0:T(8,128)(2,1)S(1)} all-to-all(bf16[16,8,2304]{2,1,0:T(8,128)(2,1)S(1)} %bitcast.51), channel_id=1, replica_groups={{1,3,5,7,9,11,13,15,17,19,21,23,25,27,29,31},{33,35,37,39,41,43,45,47,4..., dimensions={0} | all-to-all | bytes 1179648 | tf_op jit(solution)/shard_map/all_to_all | solution.py:469
  63.8 1.6 %collective-permute-start.1 = (bf16[128,2304]{1,0:T(8,128)(2,1)S(1)}, bf16[128,2304]{1,0:T(8,128)(2,1)S(1)}, u32[]{:S(2)}, u32[]{:S(2)}) collective-permute-start(bf16[128,2304]{1,0:T(8,128)(2,1)S(1)} %bitcast.41), channel_id=1, source_target_pairs={{1,65},{0,16},{3,67},{2,18},{5,69},{4,20},{7,71},{6,22},{9,73},{8,... | collective-permute-start | bytes 1769480 | tf_op jit(solution)/shard_map/ppermute | solution.py:472
  65.5 0.4 collective-permute-start.4
  65.9 2.2 %collective-permute-start.3 = (bf16[128,2304]{1,0:T(8,128)(2,1)S(1)}, bf16[128,2304]{1,0:T(8,128)(2,1)S(1)}, u32[]{:S(2)}, u32[]{:S(2)}) collective-permute-start(bf16[128,2304]{1,0:T(8,128)(2,1)S(1)} %bitcast.43), channel_id=1, source_target_pairs={{1,97},{0,24},{3,99},{2,26},{5,101},{4,28},{7,103},{6,30},{9,105},... | collective-permute-start | bytes 1769480 | tf_op jit(solution)/shard_map/ppermute | solution.py:472
  68.1 1.6 %ffn.3 = bf16[128,2304]{1,0:T(8,128)(2,1)S(1)} custom-call(bf16[128,2304]{1,0:T(8,128)(2,1)S(1)} %bitcast.44, bf16[360,2304]{1,0:T(8,128)(2,1)S(1)} %bitcast.31, bf16[360,2304]{1,0:T(8,128)(2,1)S(1)} %bitcast.34, bf16[360,2304]{1,0:T(8,128)(2,1)S(1)} %bitcast.37), custom_call_target="tpu_custom_call" | custom-call | flops 637009920 | bytes 6156288 | tf_op jit(solution)/shard_map/ffn/pallas_call | solution.py:330
  69.7 4.4 %collective-permute-done.1.refs_0_ = bf16[128,2304]{1,0:T(8,128)(2,1)S(1)} collective-permute-done((bf16[128,2304]{1,0:T(8,128)(2,1)S(1)}, bf16[128,2304]{1,0:T(8,128)(2,1)S(1)}, u32[]{:S(2)}, u32[]{:S(2)}) %collective-permute-start.1) | collective-permute-done | bytes 589856 | tf_op jit(solution)/shard_map/ppermute | solution.py:472
  74.2 1.6 %ffn.4 = bf16[128,2304]{1,0:T(8,128)(2,1)S(1)} custom-call(bf16[128,2304]{1,0:T(8,128)(2,1)S(1)} %collective-permute-done.1.refs_0_, bf16[360,2304]{1,0:T(8,128)(2,1)S(1)} %bitcast.32, bf16[360,2304]{1,0:T(8,128)(2,1)S(1)} %bitcast.35, bf16[360,2304]{1,0:T(8,128)(2,1)S(1)} %bitcast.38), custom_call_target="tpu_custom_call" | custom-call | flops 637009920 | bytes 6156288 | tf_op jit(solution)/shard_map/ffn/pallas_call | solution.py:330
  75.8 1.9 %collective-permute-start.2 = (bf16[128,2304]{1,0:T(8,128)(2,1)S(1)}, bf16[128,2304]{1,0:T(8,128)(2,1)S(1)}, u32[]{:S(2)}, u32[]{:S(2)}) collective-permute-start(bf16[128,2304]{1,0:T(8,128)(2,1)S(1)} %ffn.4), channel_id=1, source_target_pairs={{1,65},{0,16},{3,67},{2,18},{5,69},{4,20},{7,71},{6,22},{9,73},{8,... | collective-permute-start | bytes 1769480 | tf_op jit(solution)/shard_map/ppermute | solution.py:472
  77.7 2.7 %collective-permute-done.4.refs_1_ = bf16[128,2304]{1,0:T(8,128)(2,1)S(1)} collective-permute-done((bf16[128,2304]{1,0:T(8,128)(2,1)S(1)}, bf16[128,2304]{1,0:T(8,128)(2,1)S(1)}, u32[]{:S(2)}, u32[]{:S(2)}) %collective-permute-start.4) | collective-permute-done | bytes 589856 | tf_op jit(solution)/shard_map/ppermute | solution.py:472
  80.4 2.1 %ffn.5 = (bf16[128,2304]{1,0:T(8,128)(2,1)S(1)}, bf16[128,2304]{1,0:T(8,128)(2,1)S(1)}) custom-call(bf16[128,2304]{1,0:T(8,128)(2,1)S(1)} %collective-permute-done.3.refs_0_, bf16[128,2304]{1,0:T(8,128)(2,1)S(1)} %collective-permute-done.4.refs_1_, bf16[360,2304]{1,0:T(8,128)(2,1)S(1)} %bitcast.33, bf16[360,2304]{1,0:T(8,128)(2,1)S(1)} %bitcast.36, ...), custom_call_target="tpu_custom_call" | custom-call | flops 1274019840 | bytes 7335936 | tf_op jit(solution)/shard_map/ffn/pallas_call | solution.py:330
  82.5 1.9 %collective-permute-start.5 = (bf16[128,2304]{1,0:T(8,128)(2,1)S(1)}, bf16[128,2304]{1,0:T(8,128)(2,1)S(1)}, u32[]{:S(2)}, u32[]{:S(2)}) collective-permute-start(bf16[128,2304]{1,0:T(8,128)(2,1)S(1)} %get-tuple-element.25), channel_id=1, source_target_pairs={{1,97},{0,24},{3,99},{2,26},{5,101},{4,28},{7,103},{6,30},{9,105},... | collective-permute-start | bytes 1769480 | tf_op jit(solution)/shard_map/ppermute | solution.py:472
  84.4 2.7 %collective-permute-done.2 = bf16[128,2304]{1,0:T(8,128)(2,1)S(1)} collective-permute-done((bf16[128,2304]{1,0:T(8,128)(2,1)S(1)}, bf16[128,2304]{1,0:T(8,128)(2,1)S(1)}, u32[]{:S(2)}, u32[]{:S(2)}) %collective-permute-start.2) | collective-permute-done | bytes 589856 | tf_op jit(solution)/shard_map/ppermute | solution.py:472
  87.2 5.3 %collective-permute-done.5 = bf16[128,2304]{1,0:T(8,128)(2,1)S(1)} collective-permute-done((bf16[128,2304]{1,0:T(8,128)(2,1)S(1)}, bf16[128,2304]{1,0:T(8,128)(2,1)S(1)}, u32[]{:S(2)}, u32[]{:S(2)}) %collective-permute-start.5) | collective-permute-done | bytes 589856 | tf_op jit(solution)/shard_map/ppermute | solution.py:472
  92.5 2.1 %collective-permute-done.6 = bf16[128,2304]{1,0:T(8,128)(2,1)S(1)} collective-permute-done((bf16[128,2304]{1,0:T(8,128)(2,1)S(1)}, bf16[128,2304]{1,0:T(8,128)(2,1)S(1)}, u32[]{:S(2)}, u32[]{:S(2)}) %collective-permute-start.6) | collective-permute-done | bytes 589856 | tf_op jit(solution)/shard_map/ppermute | solution.py:472
  94.8 14.3 %all_to_all.23 = bf16[16,8,2304]{2,1,0:T(8,128)(2,1)S(1)} all-to-all(bf16[16,8,2304]{2,1,0:T(8,128)(2,1)S(1)} %fusion), channel_id=1, replica_groups={{1,3,5,7,9,11,13,15,17,19,21,23,25,27,29,31},{33,35,37,39,41,43,45,47,4..., dimensions={0} | all-to-all | bytes 1179648 | tf_op jit(solution)/shard_map/all_to_all | solution.py:484
  109.3 1.3 %collective-permute-done.7.back_ref = bf16[32,2304]{1,0:T(8,128)(2,1)S(1)} collective-permute-done((bf16[32,2304]{1,0:T(8,128)(2,1)S(1)}, bf16[32,2304]{1,0:T(8,128)(2,1)S(1)}, u32[]{:S(2)}, u32[]{:S(2)}) %collective-permute-start.7) | collective-permute-done | bytes 147488 | tf_op jit(solution)/shard_map/ppermute | solution.py:489
  110.6 1.5 %finish.1 = (bf16[1,4,2,2304]{3,2,1,0:T(2,128)(2,1)}, f32[2,4]{1,0:T(2,128)}) custom-call(s32[2,2,4]{2,1,0:T(2,128)S(1)} %bitcast.50, bf16[32,2304]{1,0:T(8,128)(2,1)S(1)} %bitcast_reduce_fusion.mine_ref, bf16[32,2304]{1,0:T(8,128)(2,1)S(1)} %collective-permute-done.7.back_ref, f32[8,2304]{1,0:T(8,128)S(1)} %get-tuple-element.30.mixed_ref, ...), custom_call_target="tpu_custom_call" | custom-call | tf_op jit(solution)/shard_map/finish/pallas_call | solution.py:383
  (41 shorter events, 0.8 us)
Async XLA Ops:
  0.6 20.2 %copy-start.3 = (bf16[4,64,2304]{2,1,0:T(8,128)(2,1)S(1)}, bf16[4,64,2304]{2,1,0:T(8,128)(2,1)}, u32[]{:S(2)}) copy-start(bf16[4,64,2304]{2,1,0:T(8,128)(2,1)} %k_ref.1) | copy-start | bytes 3538948
  0.6 20.2 %copy-start.5 = (bf16[1,4,2,2304]{3,2,1,0:T(2,128)(2,1)S(1)}, bf16[1,4,2,2304]{3,2,1,0:T(2,128)(2,1)}, u32[]{:S(2)}) copy-start(bf16[1,4,2,2304]{3,2,1,0:T(2,128)(2,1)} %fresh_ref.1) | copy-start | bytes 110596
  0.7 0.9 copy-start.6
  1.5 19.3 %copy-start.9 = (s32[32,64]{1,0:T(8,128)S(1)}, s32[32,64]{1,0:T(8,128)}, u32[]{:S(2)}) copy-start(s32[32,64]{1,0:T(8,128)} %live.1) | copy-start | bytes 24580
  1.5 19.3 %copy-start.12 = (s32[16,32]{1,0:T(8,128)S(1)}, s32[16,32]{1,0:T(8,128)}, u32[]{:S(2)}) copy-start(s32[16,32]{1,0:T(8,128)} %tail_len.1) | copy-start | bytes 6148
  1.5 19.3 %copy-start.13 = (s32[16,32]{1,0:T(8,128)S(1)}, s32[16,32]{1,0:T(8,128)}, u32[]{:S(2)}) copy-start(s32[16,32]{1,0:T(8,128)} %source.1) | copy-start | bytes 6148
  1.5 19.3 %copy-start.15 = (s32[32]{0:T(128)S(1)}, s32[32]{0:T(128)}, u32[]{:S(2)}) copy-start(s32[32]{0:T(128)} %lengths.1) | copy-start | bytes 388
  20.8 47.3 %copy-start.2 = (bf16[1,360,2304]{2,1,0:T(8,128)(2,1)S(1)}, bf16[1,360,2304]{2,1,0:T(8,128)(2,1)}, u32[]{:S(2)}) copy-start(bf16[1,360,2304]{2,1,0:T(8,128)(2,1)} %param.36) | copy-start | bytes 4976644
  27.3 13.7 %copy-start.4 = (f32[2304,8]{0,1:T(8,128)S(1)}, f32[2304,8]{0,1:T(8,128)}, u32[]{:S(2)}) copy-start(f32[2304,8]{0,1:T(8,128)} %param.32) | copy-start | bytes 221188
  27.3 13.7 %copy-start.7 = (bf16[1,4,2,2304]{3,2,1,0:T(2,128)(2,1)S(1)}, bf16[1,4,2,2304]{3,2,1,0:T(2,128)(2,1)}, u32[]{:S(2)}) copy-start(bf16[1,4,2,2304]{3,2,1,0:T(2,128)(2,1)} %v_ref.1) | copy-start | bytes 110596
  27.3 13.7 %copy-start.8 = (bf16[1,4,2,2304]{3,2,1,0:T(2,128)(2,1)S(1)}, bf16[1,4,2,2304]{3,2,1,0:T(2,128)(2,1)}, u32[]{:S(2)}) copy-start(bf16[1,4,2,2304]{3,2,1,0:T(2,128)(2,1)} %h_ref.1) | copy-start | bytes 110596
  27.3 13.7 %copy-start.11 = (f32[2304]{0:T(1024)S(1)}, f32[2304]{0:T(1024)}, u32[]{:S(2)}) copy-start(f32[2304]{0:T(1024)} %param.33) | copy-start | bytes 27652
  27.3 13.7 %copy-start.14 = (s32[1,4,2,2]{1,3,2,0:T(2,128)S(1)}, s32[1,4,2,2]{1,3,2,0:T(2,128)}, u32[]{:S(2)}) copy-start(s32[1,4,2,2]{1,3,2,0:T(2,128)} %param.31) | copy-start | bytes 196
  27.3 40.8 %copy-start.1 = (bf16[1,2304,360]{1,2,0:T(8,128)(2,1)S(1)}, bf16[1,2304,360]{1,2,0:T(8,128)(2,1)}, u32[]{:S(2)}) copy-start(bf16[1,2304,360]{1,2,0:T(8,128)(2,1)} %param.35) | copy-start | bytes 4976644
  42.5 4.4 %collective-permute-start = (bf16[32,2304]{1,0:T(8,128)(2,1)S(1)}, bf16[32,2304]{1,0:T(8,128)(2,1)S(1)}, u32[]{:S(2)}, u32[]{:S(2)}) collective-permute-start(bf16[32,2304]{1,0:T(8,128)(2,1)S(1)} %get-tuple-element.20), channel_id=1, source_target_pairs={{0,1},{1,0},{2,3},{3,2},{4,5},{5,4},{6,7},{7,6},{8,9},{9,8},{10,11... | collective-permute-start | bytes 442376 | tf_op jit(solution)/shard_map/ppermute | solution.py:466
  45.8 22.3 %copy-start = (bf16[1,2304,360]{1,2,0:T(8,128)(2,1)S(1)}, bf16[1,2304,360]{1,2,0:T(8,128)(2,1)}, u32[]{:S(2)}) copy-start(bf16[1,2304,360]{1,2,0:T(8,128)(2,1)} %param.34) | copy-start | bytes 4976644
  63.8 10.3 %collective-permute-start.1 = (bf16[128,2304]{1,0:T(8,128)(2,1)S(1)}, bf16[128,2304]{1,0:T(8,128)(2,1)S(1)}, u32[]{:S(2)}, u32[]{:S(2)}) collective-permute-start(bf16[128,2304]{1,0:T(8,128)(2,1)S(1)} %bitcast.41), channel_id=1, source_target_pairs={{1,65},{0,16},{3,67},{2,18},{5,69},{4,20},{7,71},{6,22},{9,73},{8,... | collective-permute-start | bytes 1769480 | tf_op jit(solution)/shard_map/ppermute | solution.py:472
  65.5 14.9 %collective-permute-start.4 = (bf16[128,2304]{1,0:T(8,128)(2,1)S(1)}, bf16[128,2304]{1,0:T(8,128)(2,1)S(1)}, u32[]{:S(2)}, u32[]{:S(2)}) collective-permute-start(bf16[128,2304]{1,0:T(8,128)(2,1)S(1)} %bitcast.42), channel_id=1, source_target_pairs={{1,33},{0,8},{3,35},{2,10},{5,37},{4,12},{7,39},{6,14},{9,41},{8,1... | collective-permute-start | bytes 1769480 | tf_op jit(solution)/shard_map/ppermute | solution.py:472
  65.9 14.5 %collective-permute-start.3 = (bf16[128,2304]{1,0:T(8,128)(2,1)S(1)}, bf16[128,2304]{1,0:T(8,128)(2,1)S(1)}, u32[]{:S(2)}, u32[]{:S(2)}) collective-permute-start(bf16[128,2304]{1,0:T(8,128)(2,1)S(1)} %bitcast.43), channel_id=1, source_target_pairs={{1,97},{0,24},{3,99},{2,26},{5,101},{4,28},{7,103},{6,30},{9,105},... | collective-permute-start | bytes 1769480 | tf_op jit(solution)/shard_map/ppermute | solution.py:472
  75.8 11.3 %collective-permute-start.2 = (bf16[128,2304]{1,0:T(8,128)(2,1)S(1)}, bf16[128,2304]{1,0:T(8,128)(2,1)S(1)}, u32[]{:S(2)}, u32[]{:S(2)}) collective-permute-start(bf16[128,2304]{1,0:T(8,128)(2,1)S(1)} %ffn.4), channel_id=1, source_target_pairs={{1,65},{0,16},{3,67},{2,18},{5,69},{4,20},{7,71},{6,22},{9,73},{8,... | collective-permute-start | bytes 1769480 | tf_op jit(solution)/shard_map/ppermute | solution.py:472
  82.5 10.0 %collective-permute-start.5 = (bf16[128,2304]{1,0:T(8,128)(2,1)S(1)}, bf16[128,2304]{1,0:T(8,128)(2,1)S(1)}, u32[]{:S(2)}, u32[]{:S(2)}) collective-permute-start(bf16[128,2304]{1,0:T(8,128)(2,1)S(1)} %get-tuple-element.25), channel_id=1, source_target_pairs={{1,97},{0,24},{3,99},{2,26},{5,101},{4,28},{7,103},{6,30},{9,105},... | collective-permute-start | bytes 1769480 | tf_op jit(solution)/shard_map/ppermute | solution.py:472
  84.4 10.2 %collective-permute-start.6 = (bf16[128,2304]{1,0:T(8,128)(2,1)S(1)}, bf16[128,2304]{1,0:T(8,128)(2,1)S(1)}, u32[]{:S(2)}, u32[]{:S(2)}) collective-permute-start(bf16[128,2304]{1,0:T(8,128)(2,1)S(1)} %get-tuple-element.26), channel_id=1, source_target_pairs={{1,33},{0,8},{3,35},{2,10},{5,37},{4,12},{7,39},{6,14},{9,41},{8,1... | collective-permute-start | bytes 1769480 | tf_op jit(solution)/shard_map/ppermute | solution.py:472
  94.8 15.8 %copy-start.10 = (f32[2304]{0:T(1024)S(1)}, f32[2304]{0:T(1024)}, u32[]{:S(2)}) copy-start(f32[2304]{0:T(1024)} %param.37) | copy-start | bytes 27652
  109.1 1.5 %collective-permute-start.7 = (bf16[32,2304]{1,0:T(8,128)(2,1)S(1)}, bf16[32,2304]{1,0:T(8,128)(2,1)S(1)}, u32[]{:S(2)}, u32[]{:S(2)}) collective-permute-start(bf16[32,2304]{1,0:T(8,128)(2,1)S(1)} %bitcast_reduce_fusion.mine_ref), channel_id=1, source_target_pairs={{0,1},{1,0},{2,3},{3,2},{4,5},{5,4},{6,7},{7,6},{8,9},{9,8},{10,11... | collective-permute-start | bytes 442376 | tf_op jit(solution)/shard_map/ppermute | solution.py:489
